TPU v7x, 256 devices: a whole 4x4x8 slice. The times are simulated.
256 devices in a mesh: sample: 64 (over z, y, core), rep: 4 (over x).
Axes of the slice: x: 4, y: 4, z: 8, core: 2. Of those that a mesh axis runs over, the one named last changes fastest.
Arguments:
- tokens: bfloat16 [32768, 128], P(('sample', 'rep')), may hold values from -6 to 6
- cache: bfloat16 [32768, 48, 256], P(('sample', 'rep')), may hold values from -144 to 144
- gain: float32 [128], replicated, may hold values from 0.25 to 1.75
- w_query: bfloat16 [128, 128], replicated, may hold values from -0.5 to 0.5
- w_key: bfloat16 [128, 128], replicated, may hold values from -0.5 to 0.5
- w_value: bfloat16 [128, 128], replicated, may hold values from -0.5 to 0.5
- w_out: bfloat16 [128, 128], replicated, may hold values from -0.5 to 0.5
- w_head: bfloat16 [128, 4], replicated, may hold values from -0.5 to 0.5
- coef: float32 [32768], P(('sample', 'rep')), may hold values from -0.625 to 0.625
- chosen: int32 [32768], P(('sample', 'rep')), may hold values from 0 to 3
- dest: int32 [32768, 1], P(('sample', 'rep')), may hold values from 0 to 63; in each aligned block of 128 rows (0 to 127, 128 to 255, ...) at most 4 rows name the same one
Outputs:
- new_cache: bfloat16 [65536, 49, 256], P(('sample', 'rep'))
- log_probs: float32 [65536, 4], P(('sample', 'rep'))
- grad_out: float32 [128, 128], replicated
- grad_head: float32 [128, 4], replicated
Inputs may be any that keep to these rules, and one draw needn't show every extreme that they name: `dest`: within the rows of one device, no value is named by more than 4 rows, a bound that some block reaches.
All inputs are finite; a program needn't handle non-finite values.
Results may differ from a plain program's by a relative error of at most 0.022.
Values may be sent and summed in bfloat16 or wider, within the bound.
No kernel may reach another device: no remote copies, remote signals or barrier semaphores. Data moves between devices by JAX's collectives and lax.ppermute only.
A program may use at most 64 MiB of HBM per device.

v0:
```python
import math

import jax
import jax.numpy as jnp
from jax import lax
from jax.sharding import PartitionSpec as P

HEADS = 4
OUTCOMES = 4


def decode_rows(tokens, cache, coef, chosen, gain, w_query, w_key, w_value, w_out, w_head):
    count = tokens.shape[0]
    width = tokens.shape[1]
    levels = cache.shape[1]
    size = width // HEADS
    xf = tokens.astype(jnp.float32)
    normed = (xf * lax.rsqrt(jnp.mean(xf * xf, -1, keepdims=True) + 1e-05) * gain).astype(
        jnp.bfloat16
    )
    query = (
        jnp.dot(normed, w_query, preferred_element_type=jnp.float32) * (1.0 / math.sqrt(size))
    ).astype(jnp.bfloat16)
    key_new = jnp.dot(normed, w_key, preferred_element_type=jnp.float32).astype(jnp.bfloat16)
    value_new = jnp.dot(normed, w_value, preferred_element_type=jnp.float32).astype(jnp.bfloat16)
    query_heads = query.reshape(count, HEADS, size)
    key_rows = cache[:, :, :width].reshape(count, levels, HEADS, size)
    value_rows = cache[:, :, width:].reshape(count, levels, HEADS, size)
    cached_scores = jnp.einsum(
        "yfn,yjfn->yfj", query_heads, key_rows, preferred_element_type=jnp.float32
    )
    score_self = jnp.sum(
        query_heads.astype(jnp.float32) * key_new.astype(jnp.float32).reshape(count, HEADS, size),
        -1,
    )
    top = jnp.maximum(jnp.max(cached_scores, -1), score_self)
    exp_cache = jnp.exp(cached_scores - top[..., None])
    exp_self = jnp.exp(score_self - top)
    total = jnp.sum(exp_cache, -1) + exp_self
    cached_weights = (exp_cache / total[..., None]).astype(jnp.bfloat16)
    weight_self = (exp_self / total).astype(jnp.bfloat16)
    attention_output = jnp.einsum(
        "jat,jtaf->jaf", cached_weights, value_rows, preferred_element_type=jnp.float32
    )
    attention_output = attention_output + weight_self.astype(jnp.float32)[
        ..., None
    ] * value_new.astype(jnp.float32).reshape(count, HEADS, size)
    attention_output = attention_output.reshape(count, width).astype(jnp.bfloat16)
    hidden = (xf + jnp.dot(attention_output, w_out, preferred_element_type=jnp.float32)).astype(
        jnp.bfloat16
    )
    logits = jnp.dot(hidden, w_head, preferred_element_type=jnp.float32)
    logp = jax.nn.log_softmax(logits, -1)
    picked = (chosen[:, None] == jnp.arange(OUTCOMES, dtype=jnp.int32)[None, :]).astype(jnp.float32)
    dlog = coef[:, None] * (picked - jnp.exp(logp))
    grad_head = jnp.dot(hidden.astype(jnp.float32).T, dlog, precision=lax.Precision.HIGHEST)
    hidden_gradient = jnp.dot(dlog, w_head.astype(jnp.float32).T, precision=lax.Precision.HIGHEST)
    grad_out = jnp.dot(
        attention_output.astype(jnp.float32).T, hidden_gradient, precision=lax.Precision.HIGHEST
    )
    both = jnp.concatenate([key_new, value_new], -1)
    return (both, logp, grad_out, grad_head)


def placed(value_rows, place, slots):
    return jnp.zeros((slots,) + value_rows.shape[1:], value_rows.dtype).at[place].set(value_rows)


def on_device(tokens, cache, gain, w_query, w_key, w_value, w_out, w_head, coef, chosen, dest):
    count = tokens.shape[0]
    peers = lax.axis_size("sample")
    capacity = 2 * count // peers
    slots = peers * capacity
    target = dest[:, 0]
    onehot = (target[:, None] == jnp.arange(peers, dtype=jnp.int32)[None, :]).astype(jnp.int32)
    rank = jnp.sum(jnp.cumsum(onehot, 0) * onehot, 1) - 1
    place = target * capacity + rank
    filled = jnp.ones((count,), jnp.int32)
    got_tokens, got_cache, got_coef, got_chosen, got_filled = (
        lax.all_to_all(
            placed(tokens, place, slots), "sample", split_axis=0, concat_axis=0, tiled=True
        ),
        lax.all_to_all(
            placed(cache, place, slots), "sample", split_axis=0, concat_axis=0, tiled=True
        ),
        lax.all_to_all(
            placed(coef, place, slots).astype(jnp.bfloat16),
            "sample",
            split_axis=0,
            concat_axis=0,
            tiled=True,
        ).astype(jnp.float32),
        lax.all_to_all(
            placed(chosen, place, slots), "sample", split_axis=0, concat_axis=0, tiled=True
        ),
        lax.all_to_all(
            placed(filled, place, slots), "sample", split_axis=0, concat_axis=0, tiled=True
        ),
    )
    both, logp, grad_out, grad_head = decode_rows(
        got_tokens, got_cache, got_coef, got_chosen, gain, w_query, w_key, w_value, w_out, w_head
    )
    logp = logp * got_filled[:, None].astype(jnp.float32)
    new_cache = jnp.concatenate([got_cache, both[:, None, :]], 1)
    grad_out, grad_head = lax.psum((grad_out, grad_head), ("sample", "rep"))
    return (new_cache, logp, grad_out, grad_head)


def solution(mesh):
    placed = (
        P(("sample", "rep"), None),
        P(("sample", "rep"), None, None),
        P(),
        P(),
        P(),
        P(),
        P(),
        P(),
        P(("sample", "rep")),
        P(("sample", "rep")),
        P(("sample", "rep"), None),
    )
    return jax.shard_map(
        on_device,
        mesh=mesh,
        in_specs=placed,
        out_specs=(P(("sample", "rep"), None, None), P(("sample", "rep"), None), P(), P()),
        check_vma=False,
    )
```

profile of v0, /device:TPU:1, one launch (start us, length us, event | category | flops | bytes accessed | tf_op | source)
XLA Modules:
  0.0 504.9 jit_solution(15651331253304061399)
XLA Ops:
  7.2 0.0 copy-start
  7.2 0.0 copy-start.1
  7.2 0.9 fusion.8
  8.1 0.2 reduce_window_sum.11
  8.3 0.8 select_reduce_fusion
  9.1 0.7 fusion.13
  9.8 1.1 scatter_custom_fusion.3
  10.9 0.7 all_to_all.36
  11.6 13.2 %all-to-all-start.3 = ((bf16[64,4,1]{1,2,0:T(2,128)(2,1)}), bf16[64,4,1]{1,2,0:T(2,128)(2,1)S(1)}, u32[]{:S(2)}, u32[]{:S(2)}) async-start(bf16[64,4,1]{1,2,0:T(2,128)(2,1)} %all_to_all.36), calls=%async_computation.3 | async-start | bytes 65536 | tf_op jit(solution)/shard_map/all_to_all | solution.py:86
  24.8 1.1 scatter_custom_fusion.4
  25.9 0.7 all_to_all.34
  26.6 7.5 %all-to-all-done.3 = bf16[64,4,1]{1,2,0:T(2,128)(2,1)S(1)} async-done(((bf16[64,4,1]{1,2,0:T(2,128)(2,1)}), bf16[64,4,1]{1,2,0:T(2,128)(2,1)S(1)}, u32[]{:S(2)}, u32[]{:S(2)}) %all-to-all-start.3) | async-done | bytes 544 | tf_op jit(solution)/shard_map/all_to_all | solution.py:86
  34.1 4.7 all-to-all-start.4
  38.8 1.0 scatter_custom_fusion.2
  39.8 0.7 all_to_all.30
  40.5 7.7 %all-to-all-done.4 = s32[64,4,1]{1,2,0:T(1,128)S(1)} async-done(((s32[64,4,1]{1,2,0:T(1,128)}), s32[64,4,1]{1,2,0:T(1,128)S(1)}, u32[]{:S(2)}, u32[]{:S(2)}) %all-to-all-start.4) | async-done | bytes 1056 | tf_op jit(solution)/shard_map/all_to_all | solution.py:93
  48.2 4.7 all-to-all-start.2
  52.9 1.7 scatter_custom_fusion.1
  54.6 7.7 %all-to-all-done.2 = s32[64,4,1]{1,2,0:T(1,128)S(1)} async-done(((s32[64,4,1]{1,2,0:T(1,128)}), s32[64,4,1]{1,2,0:T(1,128)S(1)}, u32[]{:S(2)}, u32[]{:S(2)}) %all-to-all-start.2) | async-done | bytes 1056 | tf_op jit(solution)/shard_map/all_to_all | solution.py:96
  62.3 4.7 all-to-all-start.1
  67.1 3.1 broadcast_in_dim.10
  70.2 16.2 %scatter_fusion = bf16[256,48,256]{2,1,0:T(8,128)(2,1)} fusion(bf16[256,48,256]{2,1,0:T(8,128)(2,1)} %broadcast_in_dim.10, s32[128]{0:T(128)S(1)} %fusion.13, bf16[128,48,256]{2,1,0:T(8,128)(2,1)S(1)} %copy-done.1), kind=kCustom, calls=%fused_computation | custom fusion | bytes 9437696 | tf_op jit(solution)/shard_map/scatter | solution.py:66
  86.4 0.0 all-to-all-done.1
  86.4 10.7 %all-to-all-start = ((bf16[256,48,256]{2,1,0:T(8,128)(2,1)}), bf16[256,48,256]{2,1,0:T(8,128)(2,1)}, u32[]{:S(2)}, u32[]{:S(2)}) async-start(bf16[256,48,256]{2,1,0:T(8,128)(2,1)} %scatter_fusion), calls=%async_computation | async-start | bytes 12582912 | tf_op jit(solution)/shard_map/all_to_all | solution.py:83
  97.1 0.2 all-reduce.2.cloned.1.call-start
  97.3 0.1 convert_reduce_fusion
  97.4 0.1 reshape.124
  97.5 0.5 broadcast.74
  98.0 0.7 reduce.16
  98.8 0.1 eq.34
  98.9 0.1 convert_reduce_fusion.1
  99.0 0.7 convert_element_type.101
  99.6 0.1 multiply_reduce_fusion.2
  99.8 0.1 rsqrt.12
  99.9 0.7 multiply_convert_fusion
  100.6 0.2 convolution_convert_fusion.1
  100.8 0.0 copy-done.4
  100.8 0.2 convolution_convert_fusion
  101.1 0.9 copy.34
  101.9 0.9 bitcast_convert_fusion
  102.8 132.8 %all-to-all-done = bf16[256,48,256]{2,1,0:T(8,128)(2,1)} async-done(((bf16[256,48,256]{2,1,0:T(8,128)(2,1)}), bf16[256,48,256]{2,1,0:T(8,128)(2,1)}, u32[]{:S(2)}, u32[]{:S(2)}) %all-to-all-start) | async-done | bytes 6291488 | tf_op jit(solution)/shard_map/all_to_all | solution.py:83
  235.6 6.7 %fusion.22 = (bf16[256,48,128]{2,1,0:T(8,128)(2,1)}, bf16[256,48,128]{2,1,0:T(8,128)(2,1)}) fusion(bf16[256,48,256]{2,1,0:T(8,128)(2,1)} %all-to-all-done), kind=kLoop, calls=%fused_computation.55 | loop fusion | bytes 12582912 | tf_op jit(solution)/shard_map/slice | solution.py:27
  242.3 3.9 copy.54
  246.2 2.3 multiply_reduce_fusion.1
  248.4 0.0 copy-start.5
  248.5 0.1 reduce_max.19
  248.5 0.1 fusion.3
  248.6 0.1 fusion.7
  248.7 0.8 copy.58
  249.5 3.9 copy.55
  253.4 1.7 multiply_reduce_fusion
  255.1 1.1 fusion.1
  256.2 0.8 fusion.23
  257.1 0.1 fusion.20
  257.3 1.0 fusion.21
  258.3 0.8 fusion.24
  259.1 0.0 all-reduce.2.cloned.1.call-update
  259.1 0.0 copy-start.6
  259.1 3.5 pad_maximum_fusion
  262.7 0.6 subtract_multiply_fusion.1
  263.3 4.3 copy.40
  267.6 78.6 %psum.15 = f32[128,4]{0,1:T(4,128)} all-reduce(f32[128,4]{0,1:T(4,128)S(1)} %fusion.20), channel_id=1, replica_groups=mesh['sample'=64,'rep'=4] {'sample','rep'}, use_global_device_ids=true, to_apply=%region_14.15 | all-reduce | flops 512 | bytes 4096 | tf_op jit(solution)/shard_map/psum | solution.py:105
  346.1 150.4 %all-reduce.2.cloned.1.call-done = f32[128,128]{1,0:T(8,128)} async-done(((f32[128,128]{1,0:T(8,128)}), f32[128,128]{1,0:T(8,128)}) %all-reduce.2.cloned.1.call-update) | async-done | bytes 65552 | tf_op jit(solution)/shard_map/psum | solution.py:105
  496.6 1.5 copy.71
  (21 shorter events, 0.2 us)
Async XLA Ops:
  7.2 94.8 %copy-start = (bf16[128,128]{1,0:T(8,128)(2,1)S(1)}, bf16[128,128]{1,0:T(8,128)(2,1)}, u32[]{:S(2)}) copy-start(bf16[128,128]{1,0:T(8,128)(2,1)} %param.14) | copy-start | bytes 98308
  7.2 63.0 %copy-start.1 = (bf16[128,48,256]{2,1,0:T(8,128)(2,1)S(1)}, bf16[128,48,256]{2,1,0:T(8,128)(2,1)}, u32[]{:S(2)}) copy-start(bf16[128,48,256]{2,1,0:T(8,128)(2,1)} %param.12) | copy-start | bytes 9437188
  11.6 22.5 %all-to-all-start.3 = ((bf16[64,4,1]{1,2,0:T(2,128)(2,1)}), bf16[64,4,1]{1,2,0:T(2,128)(2,1)S(1)}, u32[]{:S(2)}, u32[]{:S(2)}) async-start(bf16[64,4,1]{1,2,0:T(2,128)(2,1)} %all_to_all.36), calls=%async_computation.3 | async-start | bytes 65536 | tf_op jit(solution)/shard_map/all_to_all | solution.py:86
  34.1 14.1 %all-to-all-start.4 = ((s32[64,4,1]{1,2,0:T(1,128)}), s32[64,4,1]{1,2,0:T(1,128)S(1)}, u32[]{:S(2)}, u32[]{:S(2)}) async-start(s32[64,4,1]{1,2,0:T(1,128)} %bitcast.19), calls=%async_computation.4 | async-start | bytes 65536 | tf_op jit(solution)/shard_map/all_to_all | solution.py:93
  48.2 14.1 %all-to-all-start.2 = ((s32[64,4,1]{1,2,0:T(1,128)}), s32[64,4,1]{1,2,0:T(1,128)S(1)}, u32[]{:S(2)}, u32[]{:S(2)}) async-start(s32[64,4,1]{1,2,0:T(1,128)} %bitcast.18), calls=%async_computation.2 | async-start | bytes 65536 | tf_op jit(solution)/shard_map/all_to_all | solution.py:96
  62.3 24.0 %all-to-all-start.1 = ((bf16[64,4,128]{2,1,0:T(4,128)(2,1)}), bf16[64,4,128]{2,1,0:T(4,128)(2,1)S(1)}, u32[]{:S(2)}, u32[]{:S(2)}) async-start(bf16[64,4,128]{2,1,0:T(4,128)(2,1)} %bitcast.5), calls=%async_computation.1 | async-start | bytes 131072 | tf_op jit(solution)/shard_map/all_to_all | solution.py:80
  86.4 13.6 %copy-start.7 = (f32[128]{0:T(128)S(1)}, f32[128]{0:T(128)}, u32[]{:S(2)}) copy-start(f32[128]{0:T(128)} %param.13) | copy-start | bytes 1540
  86.4 14.2 %copy-start.3 = (bf16[128,128]{1,0:T(8,128)(2,1)S(1)}, bf16[128,128]{1,0:T(8,128)(2,1)}, u32[]{:S(2)}) copy-start(bf16[128,128]{1,0:T(8,128)(2,1)} %param.15) | copy-start | bytes 98308
  86.4 14.5 %copy-start.4 = (bf16[128,128]{1,0:T(8,128)(2,1)S(1)}, bf16[128,128]{1,0:T(8,128)(2,1)}, u32[]{:S(2)}) copy-start(bf16[128,128]{1,0:T(8,128)(2,1)} %param.16) | copy-start | bytes 98308
  86.4 149.3 %all-to-all-start = ((bf16[256,48,256]{2,1,0:T(8,128)(2,1)}), bf16[256,48,256]{2,1,0:T(8,128)(2,1)}, u32[]{:S(2)}, u32[]{:S(2)}) async-start(bf16[256,48,256]{2,1,0:T(8,128)(2,1)} %scatter_fusion), calls=%async_computation | async-start | bytes 12582912 | tf_op jit(solution)/shard_map/all_to_all | solution.py:83
  97.1 399.5 %all-reduce.2.cloned.1.call-start = ((), (), s32[]{:S(2)}) async-start(), calls=%async_computation.5 | async-start | bytes 131072 | tf_op jit(solution)/shard_map/psum | solution.py:105
  248.4 6.7 %copy-start.5 = (bf16[128,128]{1,0:T(8,128)(2,1)S(1)}, bf16[128,128]{1,0:T(8,128)(2,1)}, u32[]{:S(2)}) copy-start(bf16[128,128]{1,0:T(8,128)(2,1)} %param.17) | copy-start | bytes 98308
  248.4 10.7 %copy-start.2 = (bf16[256,1,256]{2,1,0:T(2,128)(2,1)S(1)}, bf16[256,1,256]{2,1,0:T(2,128)(2,1)}, u32[]{:S(2)}) copy-start(bf16[256,1,256]{2,1,0:T(2,128)(2,1)} %copy.34) | copy-start | bytes 393220
  259.1 3.5 copy-start.6
Sparse Core Ops, SparseCore 0:
  259.2 237.2 all-reduce.1
where the time goes:
time: 506 us; the launch traced here: 505 us
  waiting for transfers between devices  306 us (60%)
  blocking collectives  78.6 us (16%)
  local copies, waits for them, and re-layouts  49.7 us (10%)
  starting transfers between devices  38.2 us (8%)
  between operations  14.4 us (3%)
  other arithmetic  12.7 us (3%)
  matrix products  5.2 us (1%)
    psum x1, waiting for transfers between devices, on_device(): grad_out, grad_head = lax.psum((grad_out, grad_head), ('sample', 'rep'))  150 us
    all_to_all x1, waiting for transfers between devices, on_device(): lax.all_to_all(placed(cache, place, slots), 'sample', split_axis=0, conca...  133 us
    psum x1, blocking collectives, on_device(): grad_out, grad_head = lax.psum((grad_out, grad_head), ('sample', 'rep'))  78.6 us
    scatter x5, local copies, waits for them, and re-layouts, placed(): jnp.zeros((slots,) + value_rows.shape[1:], value_rows.dtype).at[place]  21.1 us
    unnamed x21, local copies, waits for them, and re-layouts  14.4 us
    all_to_all x1, starting transfers between devices, on_device(): lax.all_to_all(placed(coef, place, slots).astype(jnp.bfloat16), 'sample',...  13.2 us
    all_to_all x1, starting transfers between devices, on_device(): lax.all_to_all(placed(cache, place, slots), 'sample', split_axis=0, conca...  10.7 us
  transfers between devices with their start and end apart: 6, of which 5 were waited for; matrix products, arithmetic and copies ran while one was open for 7% of the time, Pallas kernels for 0%

commit v1 on v0

v1 whole, which is shorter than its diff:
```python
import functools
import math

import jax
import jax.numpy as jnp
from jax import lax
from jax.experimental import pallas as pl
from jax.experimental.pallas import tpu as pltpu
from jax.sharding import PartitionSpec as P

HEADS = 4
OUTCOMES = 4
ROWS = 128
LEVELS = 48
WIDTH = 256
PEERS = 64
PLANES = 8
SIDE = 8
RELAY = 8
DIRECT = 2 * LEVELS + 8
PIECE = RELAY * LEVELS + 8
LAST = 2 * PLANES * LEVELS + 8
ANY = pl.BlockSpec(memory_space=pl.ANY)
SMEM = pl.BlockSpec(memory_space=pltpu.SMEM)


def decode_rows(tokens, cache, coef, chosen, gain, w_query, w_key, w_value, w_out, w_head):
    count = tokens.shape[0]
    width = tokens.shape[1]
    levels = cache.shape[1]
    size = width // HEADS
    xf = tokens.astype(jnp.float32)
    normed = (xf * lax.rsqrt(jnp.mean(xf * xf, -1, keepdims=True) + 1e-05) * gain).astype(
        jnp.bfloat16
    )
    query = (
        jnp.dot(normed, w_query, preferred_element_type=jnp.float32) * (1.0 / math.sqrt(size))
    ).astype(jnp.bfloat16)
    key_new = jnp.dot(normed, w_key, preferred_element_type=jnp.float32).astype(jnp.bfloat16)
    value_new = jnp.dot(normed, w_value, preferred_element_type=jnp.float32).astype(jnp.bfloat16)
    query_heads = query.reshape(count, HEADS, size)
    key_rows = cache[:, :, :width].reshape(count, levels, HEADS, size)
    value_rows = cache[:, :, width:].reshape(count, levels, HEADS, size)
    cached_scores = jnp.einsum(
        "yfn,yjfn->yfj", query_heads, key_rows, preferred_element_type=jnp.float32
    )
    score_self = jnp.sum(
        query_heads.astype(jnp.float32) * key_new.astype(jnp.float32).reshape(count, HEADS, size),
        -1,
    )
    top = jnp.maximum(jnp.max(cached_scores, -1), score_self)
    exp_cache = jnp.exp(cached_scores - top[..., None])
    exp_self = jnp.exp(score_self - top)
    total = jnp.sum(exp_cache, -1) + exp_self
    cached_weights = (exp_cache / total[..., None]).astype(jnp.bfloat16)
    weight_self = (exp_self / total).astype(jnp.bfloat16)
    attention_output = jnp.einsum(
        "jat,jtaf->jaf", cached_weights, value_rows, preferred_element_type=jnp.float32
    )
    attention_output = attention_output + weight_self.astype(jnp.float32)[
        ..., None
    ] * value_new.astype(jnp.float32).reshape(count, HEADS, size)
    attention_output = attention_output.reshape(count, width).astype(jnp.bfloat16)
    hidden = (xf + jnp.dot(attention_output, w_out, preferred_element_type=jnp.float32)).astype(
        jnp.bfloat16
    )
    logits = jnp.dot(hidden, w_head, preferred_element_type=jnp.float32)
    logp = jax.nn.log_softmax(logits, -1)
    picked = (chosen[:, None] == jnp.arange(OUTCOMES, dtype=jnp.int32)[None, :]).astype(jnp.float32)
    dlog = coef[:, None] * (picked - jnp.exp(logp))
    grad_head = jnp.dot(dlog.T, hidden.astype(jnp.float32), precision=lax.Precision.HIGHEST)
    hidden_gradient = jnp.dot(dlog, w_head.astype(jnp.float32).T, precision=lax.Precision.HIGHEST)
    grad_out = jnp.dot(
        attention_output.astype(jnp.float32).T, hidden_gradient, precision=lax.Precision.HIGHEST
    )
    both = jnp.concatenate([key_new, value_new], -1)
    return (both, logp, grad_out, grad_head)


def cleared(ref, count):
    @pl.loop(0, count)
    def _(i):
        ref[i] = 0


def relay_kernel(dest, cache, out, count, filled, meta, tile, rows_sem, tile_sem):
    cleared(count, PEERS)
    cleared(filled, PLANES + 1)
    meta[...] = jnp.full(meta.shape, -1.0, jnp.float32)
    lane = lax.broadcasted_iota(jnp.int32, (8, WIDTH), 1)

    @pl.loop(0, ROWS)
    def _(i):
        d = dest[i]
        rank = count[d]
        count[d] = rank + 1

        @pl.when(rank >= 2)
        def _():
            plane = lax.div(d, SIDE)
            at = filled[plane]
            filled[plane] = at + 1

            @pl.when(at < RELAY)
            def _():
                start = pl.multiple_of(at * LEVELS, LEVELS)
                pltpu.make_async_copy(
                    cache.at[i], out.at[plane, pl.ds(start, LEVELS)], rows_sem
                ).start()
                code = lax.rem(d, SIDE) * 2 + rank - 2
                meta[plane] = jnp.where(lane == at, code.astype(jnp.float32), meta[plane])
                filled[PLANES] += 1

    most = filled[0]
    for plane in range(1, PLANES):
        most = jnp.maximum(most, filled[plane])
    over = jnp.where(most > RELAY, 1.0, 0.0)
    for plane in range(PLANES):
        tile[plane] = jnp.where(lane == RELAY, over, meta[plane]).astype(jnp.bfloat16)
    last = pltpu.make_async_copy(tile, out.at[:, pl.ds(RELAY * LEVELS, 8)], tile_sem)
    last.start()

    @pl.loop(0, filled[PLANES])
    def _(i):
        pltpu.make_async_copy(cache.at[0], out.at[0, pl.ds(0, LEVELS)], rows_sem).wait()

    last.wait()


def direct_kernel(low, dest, cache, tiles, out, count, zero, rows_sem, tile_sem):
    cleared(count, PEERS)
    zero[...] = jnp.zeros(zero.shape, zero.dtype)
    last = pltpu.make_async_copy(tiles, out.at[:, pl.ds(2 * LEVELS, 8)], tile_sem)
    last.start()

    @pl.loop(0, ROWS)
    def _(i):
        d = dest[i]
        rank = count[d]
        count[d] = rank + 1

        @pl.when((rank >= low) & (rank < low + 2))
        def _():
            start = pl.multiple_of((rank - low) * LEVELS, LEVELS)
            pltpu.make_async_copy(cache.at[i], out.at[d, pl.ds(start, LEVELS)], rows_sem).start()

    @pl.loop(0, PEERS)
    def _(d):
        for r in range(2):

            @pl.when(count[d] <= low + r)
            def _():
                pltpu.make_async_copy(zero, out.at[d, pl.ds(r * LEVELS, LEVELS)], rows_sem).start()

    whole = out.at[:, pl.ds(0, 2 * LEVELS)]
    pltpu.make_async_copy(whole, whole, rows_sem).wait()
    last.wait()


def forward_kernel(codes, side, got, *refs):
    outs, (source, zero, tile, rows_sem, tile_sem) = refs[:SIDE], refs[SIDE:]
    zero[...] = jnp.zeros(zero.shape, zero.dtype)

    @pl.loop(0, SIDE * 2 * PLANES)
    def _(i):
        source[i] = -1

    over = jnp.int32(0)
    for plane in range(PLANES):
        over = jnp.maximum(over, codes[plane, RELAY])
        for at in range(RELAY):
            code = codes[plane, at]

            @pl.when(code >= 0)
            def _():
                source[code * PLANES + plane] = at

    tile[...] = jnp.full(tile.shape, over.astype(jnp.float32)).astype(jnp.bfloat16)
    for k, out in enumerate(outs):
        pltpu.make_async_copy(tile, out.at[pl.ds(2 * PLANES * LEVELS, 8)], tile_sem.at[k]).start()
        peer = side[k]

        @pl.loop(0, 2 * PLANES)
        def _(i):
            plane = lax.div(i, 2)
            r = lax.rem(i, 2)
            at = source[(peer * 2 + r) * PLANES + plane]
            to = out.at[pl.ds(pl.multiple_of(i * LEVELS, LEVELS), LEVELS)]

            @pl.when(at >= 0)
            def _():
                start = pl.multiple_of(at * LEVELS, LEVELS)
                pltpu.make_async_copy(
                    got.at[plane, pl.ds(start, LEVELS)], to, rows_sem.at[k]
                ).start()

            @pl.when(at < 0)
            def _():
                pltpu.make_async_copy(zero, to, rows_sem.at[k]).start()

    for k, out in enumerate(outs):
        whole = out.at[pl.ds(0, 2 * PLANES * LEVELS)]
        pltpu.make_async_copy(whole, whole, rows_sem.at[k]).wait()
        pltpu.make_async_copy(tile, out.at[pl.ds(2 * PLANES * LEVELS, 8)], tile_sem.at[k]).wait()


def settle_kernel(side, direct, *refs):
    lasts, out, (held, sems) = refs[:SIDE], refs[SIDE], refs[SIDE + 1 :]
    t = pl.program_id(0)
    rows = 2 * PLANES * LEVELS

    @pl.when(t == 0)
    def _():
        copies = [
            pltpu.make_async_copy(last.at[pl.ds(0, rows)], held.at[side[k]], sems.at[k])
            for k, last in enumerate(lasts)
        ]
        for copy in copies:
            copy.start()
        for copy in copies:
            copy.wait()

    plane = lax.div(t, SIDE // 2)
    pair = lax.rem(t, SIDE // 2) * 2
    parts = []
    for j in range(2):
        for r in range(2):
            parts.append(direct[j, r * LEVELS : (r + 1) * LEVELS, :])
        for r in range(2):
            start = pl.multiple_of((plane * 2 + r) * LEVELS, LEVELS)
            parts.append(held[pair + j, pl.ds(start, LEVELS), :])
    stacked = jnp.stack([p.astype(jnp.float32) for p in parts], 0)
    out[:LEVELS] = jnp.swapaxes(stacked, 0, 1).astype(out.dtype)
    new = [direct[j, 2 * LEVELS : 2 * LEVELS + 4, :] for j in range(2)]
    out[LEVELS] = jnp.concatenate(new, 0)


def settle(side, direct, lasts):
    return pl.pallas_call(
        settle_kernel,
        grid=(PEERS // 2,),
        out_shape=jax.ShapeDtypeStruct((LEVELS + 1, 4 * PEERS, WIDTH), jnp.bfloat16),
        in_specs=[SMEM, pl.BlockSpec((2, DIRECT, WIDTH), lambda t: (t, 0, 0))] + [ANY] * SIDE,
        out_specs=pl.BlockSpec((LEVELS + 1, 8, WIDTH), lambda t: (0, t, 0)),
        scratch_shapes=[
            pltpu.VMEM((SIDE, 2 * PLANES * LEVELS, WIDTH), jnp.bfloat16),
            pltpu.SemaphoreType.DMA((SIDE,)),
        ],
        compiler_params=pltpu.CompilerParams(vmem_limit_bytes=32 << 20),
        name="settle",
    )(side, direct, *lasts)


def pack_direct(low, dest, cache, tiles):
    return pl.pallas_call(
        functools.partial(direct_kernel, low),
        out_shape=jax.ShapeDtypeStruct((PEERS, DIRECT, WIDTH), jnp.bfloat16),
        in_specs=[SMEM, ANY, ANY],
        out_specs=ANY,
        scratch_shapes=[
            pltpu.SMEM((PEERS,), jnp.int32),
            pltpu.VMEM((LEVELS, WIDTH), jnp.bfloat16),
            pltpu.SemaphoreType.DMA,
            pltpu.SemaphoreType.DMA,
        ],
        name="pack_direct",
    )(dest, cache, tiles)


def exchanged(x, groups=None):
    return lax.all_to_all(
        x, "sample", split_axis=0, concat_axis=0, tiled=True, axis_index_groups=groups
    )


def xor_pairs(size, bit):
    return [(i, i ^ bit) for i in range(size)]


def summed_in_plane(grads):
    for axis, size, bit in (
        ("sample", PEERS, 1),
        ("rep", 4, 1),
        ("rep", 4, 2),
        ("sample", PEERS, 2),
        ("sample", PEERS, 4),
    ):
        grads = grads + lax.ppermute(grads, axis, xor_pairs(size, bit))
    return grads


def summed_over_planes(grads):
    terms = [grads] + [
        lax.ppermute(grads, "sample", xor_pairs(PEERS, SIDE * k)) for k in range(1, PLANES)
    ]
    while len(terms) > 1:
        terms = [terms[i] + terms[i + 1] for i in range(0, len(terms), 2)]
    return terms[0]


def bf16_terms(x):
    terms = []
    for _ in range(3):
        term = lax.reduce_precision(x, 8, 7)
        terms.append(term.astype(jnp.bfloat16))
        x = x - term
    return terms


def on_device(tokens, cache, gain, w_query, w_key, w_value, w_out, w_head, coef, chosen, dest):
    target = dest[:, 0]
    me = lax.axis_index("sample")
    y, core = lax.rem(lax.div(me, 2), 4), lax.rem(me, 2)

    relay = pl.pallas_call(
        relay_kernel,
        out_shape=jax.ShapeDtypeStruct((PLANES, PIECE, WIDTH), jnp.bfloat16),
        in_specs=[SMEM, ANY],
        out_specs=ANY,
        scratch_shapes=[
            pltpu.SMEM((PEERS,), jnp.int32),
            pltpu.SMEM((PLANES + 1,), jnp.int32),
            pltpu.VMEM((PLANES, 8, WIDTH), jnp.float32),
            pltpu.VMEM((PLANES, 8, WIDTH), jnp.bfloat16),
            pltpu.SemaphoreType.DMA,
            pltpu.SemaphoreType.DMA,
        ],
        name="pack_relay",
    )(target, cache)
    relayed = exchanged(relay, [[z * SIDE + i for z in range(PLANES)] for i in range(SIDE)])

    both, logp, grad_out, grad_head = decode_rows(
        tokens, cache, coef, chosen, gain, w_query, w_key, w_value, w_out, w_head
    )
    grads = summed_in_plane(jnp.concatenate([grad_out, grad_head], 0))

    rows = jnp.arange(ROWS, dtype=jnp.int32)
    same = (target[:, None] == target[None, :]) & (rows[:, None] < rows[None, :])
    place = target * 4 + jnp.sum(same.astype(jnp.int32), 0)
    slot = (jnp.arange(4 * PEERS, dtype=jnp.int32)[:, None] == place[None, :]).astype(jnp.bfloat16)
    small = jnp.concatenate([both] + bf16_terms(logp), -1)
    slotted = jnp.dot(slot, small, preferred_element_type=jnp.float32).astype(jnp.bfloat16)
    new_rows = slotted[:, :WIDTH].reshape(PEERS, 4, WIDTH)
    logp_row = jnp.pad(
        slotted[:, WIDTH:].reshape(PEERS, 1, 4 * 3 * OUTCOMES),
        ((0, 0), (0, 3), (0, WIDTH - 12 * OUTCOMES)),
    )
    tiles = jnp.concatenate([new_rows, logp_row], 1)
    direct = exchanged(pack_direct(0, target, cache, tiles))

    codes = relayed[:, RELAY * LEVELS, : 2 * RELAY].astype(jnp.int32)
    shifts = [(dy, dc) for dy in range(4) for dc in range(2)]
    onto = jnp.stack([lax.rem(y + dy, 4) * 2 + (core ^ dc) for dy, dc in shifts])
    came = jnp.stack([lax.rem(y - dy + 4, 4) * 2 + (core ^ dc) for dy, dc in shifts])
    onward = pl.pallas_call(
        forward_kernel,
        out_shape=[jax.ShapeDtypeStruct((LAST, WIDTH), jnp.bfloat16)] * SIDE,
        in_specs=[SMEM, SMEM, ANY],
        out_specs=[ANY] * SIDE,
        scratch_shapes=[
            pltpu.SMEM((SIDE * 2 * PLANES,), jnp.int32),
            pltpu.VMEM((LEVELS, WIDTH), jnp.bfloat16),
            pltpu.VMEM((8, WIDTH), jnp.bfloat16),
            pltpu.SemaphoreType.DMA((SIDE,)),
            pltpu.SemaphoreType.DMA((SIDE,)),
        ],
        name="pack_plane",
    )(codes, onto.astype(jnp.int32), relayed)
    lasts = [onward[0]]
    for k in range(1, SIDE):
        dy, dc = shifts[k]
        pairs = [
            ((z * 4 + y0) * 2 + c0, (z * 4 + (y0 + dy) % 4) * 2 + (c0 ^ dc))
            for z in range(PLANES)
            for y0 in range(4)
            for c0 in range(2)
        ]
        lasts.append(lax.ppermute(onward[k], "sample", pairs))
    grads, lasts = lax.optimization_barrier((grads, lasts))
    grads = summed_over_planes(grads)
    over = jnp.max(jnp.stack([last[2 * PLANES * LEVELS, 0] for last in lasts]))
    came = came.astype(jnp.int32)

    def by_relay(direct, lasts):
        return settle(came, direct, lasts)

    def by_pairs(direct, lasts):
        high = exchanged(pack_direct(2, target, cache, jnp.zeros_like(tiles)))
        high = high[:, : 2 * LEVELS].reshape(PLANES, SIDE, 2 * LEVELS, WIDTH)
        high = jnp.swapaxes(high, 0, 1).reshape(SIDE, 2 * PLANES * LEVELS, WIDTH)
        high = [
            lax.dynamic_index_in_dim(high, came[k], 0, keepdims=False) for k in range(SIDE)
        ]
        return settle(came, direct, [jnp.pad(h, ((0, 8), (0, 0))) for h in high])

    new_cache = lax.cond(over > 0, by_pairs, by_relay, direct, lasts)
    terms = direct[:, 2 * LEVELS + 4, : 12 * OUTCOMES].astype(jnp.float32)
    terms = terms.reshape(4 * PEERS, 3, OUTCOMES)
    log_probs = (terms[:, 2] + terms[:, 1]) + terms[:, 0]
    return (jnp.swapaxes(new_cache, 0, 1), log_probs, grads[:ROWS], grads[ROWS:].T)


def solution(mesh):
    split = P(("sample", "rep"))
    whole = P()
    return jax.shard_map(
        on_device,
        mesh=mesh,
        in_specs=(split, split) + (whole,) * 6 + (split,) * 3,
        out_specs=(split, split, whole, whole),
        check_vma=False,
    )
```

time: 506 us -> 234 us (0.46)
  waiting for transfers between devices: 306 us -> 82.2 us
  blocking collectives: 78.6 us -> 0 us
  Pallas kernels: 0 us -> 62.5 us
  local copies, waits for them, and re-layouts: 49.7 us -> 22 us
  starting transfers between devices: 38.2 us -> 49.5 us
  between operations: 14.4 us -> 6.36 us
    psum x1 -> x0, waiting for transfers between devices: 150 us -> none  [on_device(): grad_out, grad_head = lax.psum((grad_out, grad_head), ('sample', 'rep'))]
    all_to_all x5 -> x2, waiting for transfers between devices: 156 us -> 14 us  [exchanged(): lax.all_to_all(x, 'sample', split_axis=0, concat_axis=0, tiled=True, axis...]
    psum x1 -> x0, blocking collectives: 78.6 us -> none  [on_device(): grad_out, grad_head = lax.psum((grad_out, grad_head), ('sample', 'rep'))]
    ppermute x0 -> x19, waiting for transfers between devices: none -> 68.2 us  [the longest x7 34.8 us: on_device(): lasts.append(lax.ppermute(onward[k], 'sample', pairs))]
    pallas_call x0 -> x4, Pallas kernels: none -> 62.5 us  [the longest x1 21.2 us: settle(): pl.pallas_call(settle_kernel, grid=(PEERS // 2,), out_shape=jax.ShapeDtyp...]
    ppermute x0 -> x19, starting transfers between devices: none -> 31.6 us  [the longest x7 15.1 us: summed_over_planes(): lax.ppermute(grads, 'sample', xor_pairs(PEERS, SIDE * k))]
    scatter x5 -> x0, local copies, waits for them, and re-layouts: 21.1 us -> none  [placed(): jnp.zeros((slots,) + value_rows.shape[1:], value_rows.dtype).at[place]]
    all_to_all x5 -> x2, starting transfers between devices: 38 us -> 17.9 us  [exchanged(): lax.all_to_all(x, 'sample', split_axis=0, concat_axis=0, tiled=True, axis...]
  transfers between devices with their start and end apart: 6 -> 21, of which waited for: 5 -> 9; matrix products, arithmetic and copies ran while one was open for 7% -> 12% of each run, Pallas kernels for 0% -> 12%
where the time goes in v1:
time: 234 us; the launch traced here: 235 us
  waiting for transfers between devices  82.2 us (35%)
  Pallas kernels  62.5 us (27%)
  starting transfers between devices  49.5 us (21%)
  local copies, waits for them, and re-layouts  22 us (9%)
  other arithmetic  10.1 us (4%)
  between operations  6.36 us (3%)
    ppermute x7, waiting for transfers between devices, on_device(): lasts.append(lax.ppermute(onward[k], 'sample', pairs))  34.8 us
    ppermute x5, waiting for transfers between devices, summed_in_plane(): grads = grads + lax.ppermute(grads, axis, xor_pairs(size, bit))  33.4 us
    pallas_call x1, Pallas kernels, settle(): pl.pallas_call(settle_kernel, grid=(PEERS // 2,), out_shape=jax.ShapeDtyp...  21.2 us
    pallas_call x1, Pallas kernels, on_device(): pl.pallas_call(forward_kernel, out_shape=[jax.ShapeDtypeStruct((LAST, WID...  19.3 us
    all_to_all x2, starting transfers between devices, exchanged(): lax.all_to_all(x, 'sample', split_axis=0, concat_axis=0, tiled=True, axis...  17.9 us
    ppermute x7, starting transfers between devices, summed_over_planes(): lax.ppermute(grads, 'sample', xor_pairs(PEERS, SIDE * k))  15.1 us
    all_to_all x2, waiting for transfers between devices, exchanged(): lax.all_to_all(x, 'sample', split_axis=0, concat_axis=0, tiled=True, axis...  14 us
    pallas_call x1, Pallas kernels, on_device(): pl.pallas_call(relay_kernel, out_shape=jax.ShapeDtypeStruct((PLANES, PIEC...  12 us
  transfers between devices with their start and end apart: 21, of which 9 were waited for; matrix products, arithmetic and copies ran while one was open for 12% of the time, Pallas kernels for 12%

profile of v1, /device:TPU:1, one launch (start us, length us, event | category | flops | bytes accessed | tf_op | source)
XLA Modules:
  0.0 234.5 jit_solution(16047052395102306068)
XLA Ops:
  0.7 12.0 %pack_relay.1 = bf16[8,392,256]{2,1,0:T(8,128)(2,1)} custom-call(s32[128]{0:T(128)} %bitcast.75, bf16[128,48,256]{2,1,0:T(8,128)(2,1)} %cache.3), custom_call_target="tpu_custom_call" | custom-call | tf_op jit(solution)/shard_map/pack_relay/pallas_call | solution.py:315
  12.6 10.0 %all-to-all-start.1 = ((bf16[8,392,256]{2,1,0:T(8,128)(2,1)}), bf16[8,392,256]{2,1,0:T(8,128)(2,1)}, u32[]{:S(2)}, u32[]{:S(2)}) async-start(bf16[8,392,256]{2,1,0:T(8,128)(2,1)} %pack_relay.1), calls=%async_computation.1 | async-start | bytes 3211264 | tf_op jit(solution)/shard_map/all_to_all | solution.py:271
  22.6 2.2 fusion.30
  24.8 0.1 fusion.6
  25.0 0.2 bitcast_convert_fusion
  25.2 0.2 convolution_convert_fusion.2
  25.5 2.9 %copy.53 = bf16[128,48,128]{0,2,1:T(8,128)(2,1)} copy(bf16[128,48,128]{2,1,0:T(8,128)(2,1)} %get-tuple-element.123) | data formatting | bytes 3145728
  28.4 2.0 multiply_reduce_fusion.1
  30.6 2.8 %copy.54 = bf16[128,48,128]{0,2,1:T(8,128)(2,1)} copy(bf16[128,48,128]{2,1,0:T(8,128)(2,1)} %get-tuple-element.124) | data formatting | bytes 3145728
  33.5 1.7 multiply_reduce_fusion
  35.2 0.2 convolution_convert_fusion.1
  35.5 0.2 fusion.1
  35.7 0.1 fusion.31
  36.0 0.1 convert_reduce_fusion
  36.1 0.2 convolution_convert_fusion
  36.5 0.1 copy.36
  36.7 0.8 fusion.3.tiles
  37.5 10.0 %pack_direct.3 = bf16[64,104,256]{2,1,0:T(8,128)(2,1)} custom-call(s32[128]{0:T(128)S(1)} %bitcast.77, bf16[128,48,256]{2,1,0:T(8,128)(2,1)S(1)} %copy-done.1, bf16[64,8,256]{2,1,0:T(8,128)(2,1)} %fusion.3.tiles), custom_call_target="tpu_custom_call" | custom-call | tf_op jit(solution)/shard_map/pack_direct/pallas_call | solution.py:255
  47.6 14.0 %all-to-all-done.1.got = bf16[8,392,256]{2,1,0:T(8,128)(2,1)} async-done(((bf16[8,392,256]{2,1,0:T(8,128)(2,1)}), bf16[8,392,256]{2,1,0:T(8,128)(2,1)}, u32[]{:S(2)}, u32[]{:S(2)}) %all-to-all-start.1) | async-done | bytes 1605664 | tf_op jit(solution)/shard_map/all_to_all | solution.py:271
  61.6 7.9 %all-to-all-start.2 = ((bf16[64,104,256]{2,1,0:T(8,128)(2,1)}), bf16[64,104,256]{2,1,0:T(8,128)(2,1)}, u32[]{:S(2)}, u32[]{:S(2)}) async-start(bf16[64,104,256]{2,1,0:T(8,128)(2,1)} %pack_direct.3), calls=%async_computation.2 | async-start | bytes 6815744 | tf_op jit(solution)/shard_map/all_to_all | solution.py:271
  69.5 0.1 fusion.18
  69.6 0.3 fusion.19
  69.9 0.2 fusion.32
  70.2 0.6 collective-permute-start
  70.8 0.6 stack.51.side
  71.4 1.3 slice_convert_fusion.1
  72.7 19.3 %pack_plane.1 = (bf16[776,256]{1,0:T(8,128)(2,1)}, bf16[776,256]{1,0:T(8,128)(2,1)}, bf16[776,256]{1,0:T(8,128)(2,1)}, bf16[776,256]{1,0:T(8,128)(2,1)}, bf16[77...) custom-call(s32[8,16]{1,0:T(8,128)} %bitcast.74, ...), custom_call_target="tpu_custom_call" | custom-call | tf_op jit(solution)/shard_map/pack_plane/pallas_call | solution.py:355
  92.0 2.9 %collective-permute-start.10 = (bf16[776,256]{1,0:T(8,128)(2,1)}, bf16[776,256]{1,0:T(8,128)(2,1)}, u32[]{:S(2)}, u32[]{:S(2)}) collective-permute-start(bf16[776,256]{1,0:T(8,128)(2,1)} %get-tuple-element.96), channel_id=1, source_target_pairs={{0,24},{4,28},{8,0},{12,4},{16,8},{20,12},{24,16},{28,20},{32,56},... | collective-permute-start | bytes 1191944 | tf_op jit(solution)/shard_map/ppermute | solution.py:378
  94.9 2.1 collective-permute-start.11
  97.1 3.9 %collective-permute-done.1 = f32[132,128]{1,0:T(8,128)S(1)} collective-permute-done((f32[132,128]{1,0:T(8,128)S(1)}, f32[132,128]{1,0:T(8,128)S(1)}, u32[]{:S(2)}, u32[]{:S(2)}) %collective-permute-start.1) | collective-permute-done | bytes 67616 | tf_op jit(solution)/shard_map/ppermute | solution.py:288
  101.1 4.9 %collective-permute-start.2 = (f32[132,128]{1,0:T(8,128)S(1)}, f32[132,128]{1,0:T(8,128)S(1)}, u32[]{:S(2)}, u32[]{:S(2)}) collective-permute-start(f32[132,128]{1,0:T(8,128)S(1)} %add.196), channel_id=1, source_target_pairs={{0,2},{1,3},{2,0},{3,1},{4,6},{5,7},{6,4},{7,5},{8,10},{9,11},{10,... | collective-permute-start | bytes 202760 | tf_op jit(solution)/shard_map/ppermute | solution.py:288
  106.0 2.1 collective-permute-done.2
  108.2 23.1 %collective-permute-done.3 = f32[132,128]{1,0:T(8,128)S(1)} collective-permute-done((f32[132,128]{1,0:T(8,128)S(1)}, f32[132,128]{1,0:T(8,128)S(1)}, u32[]{:S(2)}, u32[]{:S(2)}) %collective-permute-start.3) | collective-permute-done | bytes 67616 | tf_op jit(solution)/shard_map/ppermute | solution.py:288
  131.4 1.4 collective-permute-start.4
  132.7 1.1 collective-permute-start.5
  133.9 4.3 %collective-permute-done.4 = f32[132,128]{1,0:T(8,128)S(1)} collective-permute-done((f32[132,128]{1,0:T(8,128)S(1)}, f32[132,128]{1,0:T(8,128)S(1)}, u32[]{:S(2)}, u32[]{:S(2)}) %collective-permute-start.4) | collective-permute-done | bytes 67616 | tf_op jit(solution)/shard_map/ppermute | solution.py:288
  138.2 0.3 collective-permute-start.7
  138.4 1.8 collective-permute-start.8
  140.2 1.2 collective-permute-start.9
  141.5 8.1 %collective-permute-done.6 = bf16[776,256]{1,0:T(8,128)(2,1)} collective-permute-done((bf16[776,256]{1,0:T(8,128)(2,1)}, bf16[776,256]{1,0:T(8,128)(2,1)}, u32[]{:S(2)}, u32[]{:S(2)}) %collective-permute-start.6) | collective-permute-done | bytes 397344 | tf_op jit(solution)/shard_map/ppermute | solution.py:378
  149.5 8.5 %collective-permute-done.7 = bf16[776,256]{1,0:T(8,128)(2,1)} collective-permute-done((bf16[776,256]{1,0:T(8,128)(2,1)}, bf16[776,256]{1,0:T(8,128)(2,1)}, u32[]{:S(2)}, u32[]{:S(2)}) %collective-permute-start.7) | collective-permute-done | bytes 397344 | tf_op jit(solution)/shard_map/ppermute | solution.py:378
  158.0 9.6 %collective-permute-done.8 = bf16[776,256]{1,0:T(8,128)(2,1)} collective-permute-done((bf16[776,256]{1,0:T(8,128)(2,1)}, bf16[776,256]{1,0:T(8,128)(2,1)}, u32[]{:S(2)}, u32[]{:S(2)}) %collective-permute-start.8) | collective-permute-done | bytes 397344 | tf_op jit(solution)/shard_map/ppermute | solution.py:378
  167.7 8.5 %collective-permute-done.9 = bf16[776,256]{1,0:T(8,128)(2,1)} collective-permute-done((bf16[776,256]{1,0:T(8,128)(2,1)}, bf16[776,256]{1,0:T(8,128)(2,1)}, u32[]{:S(2)}, u32[]{:S(2)}) %collective-permute-start.9) | collective-permute-done | bytes 397344 | tf_op jit(solution)/shard_map/ppermute | solution.py:378
  176.2 3.5 %collective-permute-start.14 = (f32[132,128]{1,0:T(8,128)S(1)}, f32[132,128]{1,0:T(8,128)S(1)}, u32[]{:S(2)}, u32[]{:S(2)}) collective-permute-start(f32[132,128]{1,0:T(8,128)S(1)} %add.199), channel_id=1, source_target_pairs={{0,96},{4,100},{8,104},{12,108},{16,112},{20,116},{24,120},{28,124... | collective-permute-start | bytes 202760 | tf_op jit(solution)/shard_map/ppermute | solution.py:294
  179.7 4.1 %collective-permute-start.15 = (f32[132,128]{1,0:T(8,128)S(1)}, f32[132,128]{1,0:T(8,128)S(1)}, u32[]{:S(2)}, u32[]{:S(2)}) collective-permute-start(f32[132,128]{1,0:T(8,128)S(1)} %add.199), channel_id=1, source_target_pairs={{0,128},{4,132},{8,136},{12,140},{16,144},{20,148},{24,152},{28,15... | collective-permute-start | bytes 202760 | tf_op jit(solution)/shard_map/ppermute | solution.py:294
  183.9 4.5 %collective-permute-start.17 = (f32[132,128]{1,0:T(8,128)S(1)}, f32[132,128]{1,0:T(8,128)}, u32[]{:S(2)}, u32[]{:S(2)}) collective-permute-start(f32[132,128]{1,0:T(8,128)S(1)} %add.199), channel_id=1, source_target_pairs={{0,192},{4,196},{8,200},{12,204},{16,208},{20,212},{24,216},{28,22... | collective-permute-start | bytes 202760 | tf_op jit(solution)/shard_map/ppermute | solution.py:294
  188.4 3.0 %collective-permute-start.18 = (f32[132,128]{1,0:T(8,128)S(1)}, f32[132,128]{1,0:T(8,128)}, u32[]{:S(2)}, u32[]{:S(2)}) collective-permute-start(f32[132,128]{1,0:T(8,128)S(1)} %add.199), channel_id=1, source_target_pairs={{0,224},{4,228},{8,232},{12,236},{16,240},{20,244},{24,248},{28,25... | collective-permute-start | bytes 202760 | tf_op jit(solution)/shard_map/ppermute | solution.py:294
  191.4 1.2 slice.63
  192.6 1.2 slice.64
  193.8 1.2 slice.65
  194.9 1.2 slice.66
  196.2 1.2 slice.67
  197.4 1.2 slice.68
  198.6 1.2 slice.69
  199.8 1.2 slice.70
  206.2 1.0 add_add_fusion
  207.2 0.6 slice.87
  207.9 0.6 slice_bitcast_fusion
  208.4 1.0 fusion.15
  209.5 1.3 reshape.126
  210.8 1.7 slice_add_fusion
  212.5 0.7 copy.38
  213.2 21.2 %conditional.1 = (bf16[49,256,256]{2,1,0:T(8,128)(2,1)}) conditional(s32[]{:T(128)} %bitcast.31, (s32[8]{0:T(128)S(1)}, bf16[64,104,256]{2,1,0:T(8,128)(2,1)}, bf16[776,256]{1,0:T(8,128)(2,1)}, bf16[776,256]{1,0:T(8,128)(2,1)}, bf16[776,256]{1,0:T(8,128)(2,1)}, /*index=5*/bf16[776,256]{1,0:T(8,128)(2,1)}, bf16[776,256]{1,0:T(8,128)(2,1)}, ...), branch_computations={%region_7.8_spmd, %region_8.9_spmd} | conditional | flops 24 | bytes 35684696 | solution.py:396
  213.2 21.2 %settle.2 = bf16[49,256,256]{2,1,0:T(8,128)(2,1)} custom-call(s32[8]{0:T(128)S(1)} %get-tuple-element.31.side, bf16[64,104,256]{2,1,0:T(8,128)(2,1)} %get-tuple-element.48.direct, bf16[776,256]{1,0:T(8,128)(2,1)} %get-tuple-element.49.refs_0_, bf16[776,256]{1,0:T(8,128)(2,1)} %get-tuple-element.50.refs_1_, bf16[776,256]{1,0:T(8,128)(2,1)} %get-tuple-element.51.refs_2_, ...), custom_call_target="tpu_custom_call" | custom-call | tf_op jit(solution)/shard_map/cond/branch_0_fun/settle/pallas_call | solution.py:239
  (66 shorter events, 1.1 us)
Async XLA Ops:
  0.6 24.3 %copy-start = (bf16[128,128]{1,0:T(8,128)(2,1)S(1)}, bf16[128,128]{1,0:T(8,128)(2,1)}, u32[]{:S(2)}) copy-start(bf16[128,128]{1,0:T(8,128)(2,1)} %param.16) | copy-start | bytes 98308
  0.6 22.0 %copy-start.1 = (bf16[128,48,256]{2,1,0:T(8,128)(2,1)S(1)}, bf16[128,48,256]{2,1,0:T(8,128)(2,1)}, u32[]{:S(2)}) copy-start(bf16[128,48,256]{2,1,0:T(8,128)(2,1)} %cache.3) | copy-start | bytes 9437188
  12.6 48.9 %all-to-all-start.1 = ((bf16[8,392,256]{2,1,0:T(8,128)(2,1)}), bf16[8,392,256]{2,1,0:T(8,128)(2,1)}, u32[]{:S(2)}, u32[]{:S(2)}) async-start(bf16[8,392,256]{2,1,0:T(8,128)(2,1)} %pack_relay.1), calls=%async_computation.1 | async-start | bytes 3211264 | tf_op jit(solution)/shard_map/all_to_all | solution.py:271
  22.6 2.2 copy-start.2
  22.6 2.4 %copy-start.6 = (f32[128]{0:T(128)S(1)}, f32[128]{0:T(128)}, u32[]{:S(2)}) copy-start(f32[128]{0:T(128)} %param.15) | copy-start | bytes 1540
  22.6 2.6 %copy-start.3 = (bf16[128,128]{1,0:T(8,128)(2,1)S(1)}, bf16[128,128]{1,0:T(8,128)(2,1)}, u32[]{:S(2)}) copy-start(bf16[128,128]{1,0:T(8,128)(2,1)} %param.17) | copy-start | bytes 98308
  30.4 4.9 %copy-start.4 = (bf16[128,128]{1,0:T(8,128)(2,1)S(1)}, bf16[128,128]{1,0:T(8,128)(2,1)}, u32[]{:S(2)}) copy-start(bf16[128,128]{1,0:T(8,128)(2,1)} %param.18) | copy-start | bytes 98308
  30.4 5.1 %copy-start.5 = (bf16[128,128]{1,0:T(8,128)(2,1)S(1)}, bf16[128,128]{1,0:T(8,128)(2,1)}, u32[]{:S(2)}) copy-start(bf16[128,128]{1,0:T(8,128)(2,1)} %param.19) | copy-start | bytes 98308
  30.4 5.3 %copy-start.8 = (bf16[128,4]{0,1:T(4,128)(2,1)S(1)}, bf16[128,4]{0,1:T(4,128)(2,1)}, u32[]{:S(2)}) copy-start(bf16[128,4]{0,1:T(4,128)(2,1)} %param.20) | copy-start | bytes 3076
  30.4 5.6 %copy-start.7 = (s32[128,1]{0,1:T(1,128)S(1)}, s32[128,1]{0,1:T(1,128)}, u32[]{:S(2)}) copy-start(s32[128,1]{0,1:T(1,128)} %param.23) | copy-start | bytes 1540
  47.6 21.9 %copy-start.9 = (s32[128]{0:T(128)S(1)}, s32[128]{0:T(128)}, u32[]{:S(2)}) copy-start(s32[128]{0:T(128)} %param.22) | copy-start | bytes 1540
  47.6 21.9 %copy-start.10 = (f32[128]{0:T(128)S(1)}, f32[128]{0:T(128)}, u32[]{:S(2)}) copy-start(f32[128]{0:T(128)} %param.21) | copy-start | bytes 1540
  61.6 146.9 %all-to-all-start.2 = ((bf16[64,104,256]{2,1,0:T(8,128)(2,1)}), bf16[64,104,256]{2,1,0:T(8,128)(2,1)}, u32[]{:S(2)}, u32[]{:S(2)}) async-start(bf16[64,104,256]{2,1,0:T(8,128)(2,1)} %pack_direct.3), calls=%async_computation.2 | async-start | bytes 6815744 | tf_op jit(solution)/shard_map/all_to_all | solution.py:271
  70.2 26.9 %collective-permute-start = (f32[132,128]{1,0:T(8,128)S(1)}, f32[132,128]{1,0:T(8,128)S(1)}, u32[]{:S(2)}, u32[]{:S(2)}) collective-permute-start(f32[132,128]{1,0:T(8,128)S(1)} %pad_maximum_fusion), channel_id=1, source_target_pairs={{0,4},{4,0},{8,12},{12,8},{16,20},{20,16},{24,28},{28,24},{32,36},... | collective-permute-start | bytes 202760 | tf_op jit(solution)/shard_map/ppermute | solution.py:288
  92.0 46.4 %collective-permute-start.10 = (bf16[776,256]{1,0:T(8,128)(2,1)}, bf16[776,256]{1,0:T(8,128)(2,1)}, u32[]{:S(2)}, u32[]{:S(2)}) collective-permute-start(bf16[776,256]{1,0:T(8,128)(2,1)} %get-tuple-element.96), channel_id=1, source_target_pairs={{0,24},{4,28},{8,0},{12,4},{16,8},{20,12},{24,16},{28,20},{32,56},... | collective-permute-start | bytes 1191944 | tf_op jit(solution)/shard_map/ppermute | solution.py:378
  94.9 45.3 %collective-permute-start.11 = (bf16[776,256]{1,0:T(8,128)(2,1)}, bf16[776,256]{1,0:T(8,128)(2,1)}, u32[]{:S(2)}, u32[]{:S(2)}) collective-permute-start(bf16[776,256]{1,0:T(8,128)(2,1)} %get-tuple-element.97), channel_id=1, source_target_pairs={{0,28},{4,24},{8,4},{12,0},{16,12},{20,8},{24,20},{28,16},{32,60},... | collective-permute-start | bytes 1191944 | tf_op jit(solution)/shard_map/ppermute | solution.py:378
  97.0 4.0 %collective-permute-start.1 = (f32[132,128]{1,0:T(8,128)S(1)}, f32[132,128]{1,0:T(8,128)S(1)}, u32[]{:S(2)}, u32[]{:S(2)}) collective-permute-start(f32[132,128]{1,0:T(8,128)S(1)} %fusion.26), channel_id=1, source_target_pairs={{0,1},{1,0},{2,3},{3,2},{4,5},{5,4},{6,7},{7,6},{8,9},{9,8},{10,11... | collective-permute-start | bytes 202760 | tf_op jit(solution)/shard_map/ppermute | solution.py:288
  101.1 7.0 %collective-permute-start.2 = (f32[132,128]{1,0:T(8,128)S(1)}, f32[132,128]{1,0:T(8,128)S(1)}, u32[]{:S(2)}, u32[]{:S(2)}) collective-permute-start(f32[132,128]{1,0:T(8,128)S(1)} %add.196), channel_id=1, source_target_pairs={{0,2},{1,3},{2,0},{3,1},{4,6},{5,7},{6,4},{7,5},{8,10},{9,11},{10,... | collective-permute-start | bytes 202760 | tf_op jit(solution)/shard_map/ppermute | solution.py:288
  108.1 23.2 %collective-permute-start.3 = (f32[132,128]{1,0:T(8,128)S(1)}, f32[132,128]{1,0:T(8,128)S(1)}, u32[]{:S(2)}, u32[]{:S(2)}) collective-permute-start(f32[132,128]{1,0:T(8,128)S(1)} %add.197), channel_id=1, source_target_pairs={{0,8},{4,12},{8,0},{12,4},{16,24},{20,28},{24,16},{28,20},{32,40},... | collective-permute-start | bytes 202760 | tf_op jit(solution)/shard_map/ppermute | solution.py:288
  131.4 6.8 %collective-permute-start.4 = (f32[132,128]{1,0:T(8,128)S(1)}, f32[132,128]{1,0:T(8,128)S(1)}, u32[]{:S(2)}, u32[]{:S(2)}) collective-permute-start(f32[132,128]{1,0:T(8,128)S(1)} %add.198), channel_id=1, source_target_pairs={{0,16},{4,20},{8,24},{12,28},{16,0},{20,4},{24,8},{28,12},{32,48},... | collective-permute-start | bytes 202760 | tf_op jit(solution)/shard_map/ppermute | solution.py:288
  132.7 8.7 %collective-permute-start.5 = (bf16[776,256]{1,0:T(8,128)(2,1)}, bf16[776,256]{1,0:T(8,128)(2,1)}, u32[]{:S(2)}, u32[]{:S(2)}) collective-permute-start(bf16[776,256]{1,0:T(8,128)(2,1)} %get-tuple-element.91), channel_id=1, source_target_pairs={{0,4},{4,0},{8,12},{12,8},{16,20},{20,16},{24,28},{28,24},{32,36},... | collective-permute-start | bytes 1191944 | tf_op jit(solution)/shard_map/ppermute | solution.py:378
  133.9 15.6 %collective-permute-start.6 = (bf16[776,256]{1,0:T(8,128)(2,1)}, bf16[776,256]{1,0:T(8,128)(2,1)}, u32[]{:S(2)}, u32[]{:S(2)}) collective-permute-start(bf16[776,256]{1,0:T(8,128)(2,1)} %get-tuple-element.92), channel_id=1, source_target_pairs={{0,8},{4,12},{8,16},{12,20},{16,24},{20,28},{24,0},{28,4},{32,40},... | collective-permute-start | bytes 1191944 | tf_op jit(solution)/shard_map/ppermute | solution.py:378
  138.2 19.9 %collective-permute-start.7 = (bf16[776,256]{1,0:T(8,128)(2,1)}, bf16[776,256]{1,0:T(8,128)(2,1)}, u32[]{:S(2)}, u32[]{:S(2)}) collective-permute-start(bf16[776,256]{1,0:T(8,128)(2,1)} %get-tuple-element.93), channel_id=1, source_target_pairs={{0,12},{4,8},{8,20},{12,16},{16,28},{20,24},{24,4},{28,0},{32,44},... | collective-permute-start | bytes 1191944 | tf_op jit(solution)/shard_map/ppermute | solution.py:378
  138.4 29.3 %collective-permute-start.8 = (bf16[776,256]{1,0:T(8,128)(2,1)}, bf16[776,256]{1,0:T(8,128)(2,1)}, u32[]{:S(2)}, u32[]{:S(2)}) collective-permute-start(bf16[776,256]{1,0:T(8,128)(2,1)} %get-tuple-element.94), channel_id=1, source_target_pairs={{0,16},{4,20},{8,24},{12,28},{16,0},{20,4},{24,8},{28,12},{32,48},... | collective-permute-start | bytes 1191944 | tf_op jit(solution)/shard_map/ppermute | solution.py:378
  140.2 36.0 %collective-permute-start.9 = (bf16[776,256]{1,0:T(8,128)(2,1)}, bf16[776,256]{1,0:T(8,128)(2,1)}, u32[]{:S(2)}, u32[]{:S(2)}) collective-permute-start(bf16[776,256]{1,0:T(8,128)(2,1)} %get-tuple-element.95), channel_id=1, source_target_pairs={{0,20},{4,16},{8,28},{12,24},{16,4},{20,0},{24,12},{28,8},{32,52},... | collective-permute-start | bytes 1191944 | tf_op jit(solution)/shard_map/ppermute | solution.py:378
  176.2 7.7 %collective-permute-start.12 = (f32[132,128]{1,0:T(8,128)S(1)}, f32[132,128]{1,0:T(8,128)S(1)}, u32[]{:S(2)}, u32[]{:S(2)}) collective-permute-start(f32[132,128]{1,0:T(8,128)S(1)} %add.199), channel_id=1, source_target_pairs={{0,32},{4,36},{8,40},{12,44},{16,48},{20,52},{24,56},{28,60},{32,0... | collective-permute-start | bytes 202760 | tf_op jit(solution)/shard_map/ppermute | solution.py:294
  176.2 12.2 %collective-permute-start.13 = (f32[132,128]{1,0:T(8,128)S(1)}, f32[132,128]{1,0:T(8,128)S(1)}, u32[]{:S(2)}, u32[]{:S(2)}) collective-permute-start(f32[132,128]{1,0:T(8,128)S(1)} %add.199), channel_id=1, source_target_pairs={{0,64},{4,68},{8,72},{12,76},{16,80},{20,84},{24,88},{28,92},{32,9... | collective-permute-start | bytes 202760 | tf_op jit(solution)/shard_map/ppermute | solution.py:294
  176.2 30.0 %collective-permute-start.14 = (f32[132,128]{1,0:T(8,128)S(1)}, f32[132,128]{1,0:T(8,128)S(1)}, u32[]{:S(2)}, u32[]{:S(2)}) collective-permute-start(f32[132,128]{1,0:T(8,128)S(1)} %add.199), channel_id=1, source_target_pairs={{0,96},{4,100},{8,104},{12,108},{16,112},{20,116},{24,120},{28,124... | collective-permute-start | bytes 202760 | tf_op jit(solution)/shard_map/ppermute | solution.py:294
  179.7 26.4 %collective-permute-start.15 = (f32[132,128]{1,0:T(8,128)S(1)}, f32[132,128]{1,0:T(8,128)S(1)}, u32[]{:S(2)}, u32[]{:S(2)}) collective-permute-start(f32[132,128]{1,0:T(8,128)S(1)} %add.199), channel_id=1, source_target_pairs={{0,128},{4,132},{8,136},{12,140},{16,144},{20,148},{24,152},{28,15... | collective-permute-start | bytes 202760 | tf_op jit(solution)/shard_map/ppermute | solution.py:294
  183.9 22.3 %collective-permute-start.16 = (f32[132,128]{1,0:T(8,128)S(1)}, f32[132,128]{1,0:T(8,128)}, u32[]{:S(2)}, u32[]{:S(2)}) collective-permute-start(f32[132,128]{1,0:T(8,128)S(1)} %add.199), channel_id=1, source_target_pairs={{0,160},{4,164},{8,168},{12,172},{16,176},{20,180},{24,184},{28,18... | collective-permute-start | bytes 202760 | tf_op jit(solution)/shard_map/ppermute | solution.py:294
  183.9 22.3 %collective-permute-start.17 = (f32[132,128]{1,0:T(8,128)S(1)}, f32[132,128]{1,0:T(8,128)}, u32[]{:S(2)}, u32[]{:S(2)}) collective-permute-start(f32[132,128]{1,0:T(8,128)S(1)} %add.199), channel_id=1, source_target_pairs={{0,192},{4,196},{8,200},{12,204},{16,208},{20,212},{24,216},{28,22... | collective-permute-start | bytes 202760 | tf_op jit(solution)/shard_map/ppermute | solution.py:294
  188.4 17.9 %collective-permute-start.18 = (f32[132,128]{1,0:T(8,128)S(1)}, f32[132,128]{1,0:T(8,128)}, u32[]{:S(2)}, u32[]{:S(2)}) collective-permute-start(f32[132,128]{1,0:T(8,128)S(1)} %add.199), channel_id=1, source_target_pairs={{0,224},{4,228},{8,232},{12,236},{16,240},{20,244},{24,248},{28,25... | collective-permute-start | bytes 202760 | tf_op jit(solution)/shard_map/ppermute | solution.py:294

commit v2 on v1

--- a/solution.py
+++ b/solution.py
@@ -19,7 +19,7 @@
 RELAY = 8
 DIRECT = 2 * LEVELS + 8
 PIECE = RELAY * LEVELS + 8
-LAST = 2 * PLANES * LEVELS + 8
+LAST = 2 * PLANES * LEVELS
 ANY = pl.BlockSpec(memory_space=pl.ANY)
 SMEM = pl.BlockSpec(memory_space=pltpu.SMEM)
 
@@ -83,7 +83,7 @@
         ref[i] = 0
 
 
-def relay_kernel(dest, cache, out, count, filled, meta, tile, rows_sem, tile_sem):
+def relay_kernel(dest, cache, out, over, count, filled, meta, held, rows_sem, out_sem):
     cleared(count, PEERS)
     cleared(filled, PLANES + 1)
     meta[...] = jnp.full(meta.shape, -1.0, jnp.float32)
@@ -105,7 +105,7 @@
             def _():
                 start = pl.multiple_of(at * LEVELS, LEVELS)
                 pltpu.make_async_copy(
-                    cache.at[i], out.at[plane, pl.ds(start, LEVELS)], rows_sem
+                    cache.at[i], held.at[plane, pl.ds(start, LEVELS)], rows_sem
                 ).start()
                 code = lax.rem(d, SIDE) * 2 + rank - 2
                 meta[plane] = jnp.where(lane == at, code.astype(jnp.float32), meta[plane])
@@ -114,17 +114,17 @@
     most = filled[0]
     for plane in range(1, PLANES):
         most = jnp.maximum(most, filled[plane])
-    over = jnp.where(most > RELAY, 1.0, 0.0)
+    over[...] = jnp.full(over.shape, jnp.where(most > RELAY, 1.0, 0.0), jnp.float32)
     for plane in range(PLANES):
-        tile[plane] = jnp.where(lane == RELAY, over, meta[plane]).astype(jnp.bfloat16)
-    last = pltpu.make_async_copy(tile, out.at[:, pl.ds(RELAY * LEVELS, 8)], tile_sem)
-    last.start()
+        held[plane, RELAY * LEVELS :, :] = meta[plane].astype(jnp.bfloat16)
 
     @pl.loop(0, filled[PLANES])
     def _(i):
-        pltpu.make_async_copy(cache.at[0], out.at[0, pl.ds(0, LEVELS)], rows_sem).wait()
-
-    last.wait()
+        pltpu.make_async_copy(cache.at[0], held.at[0, pl.ds(0, LEVELS)], rows_sem).wait()
+
+    whole = pltpu.make_async_copy(held, out, out_sem)
+    whole.start()
+    whole.wait()
 
 
 def direct_kernel(low, dest, cache, tiles, out, count, zero, rows_sem, tile_sem):
@@ -158,16 +158,14 @@
 
 
 def forward_kernel(codes, side, got, *refs):
-    outs, (source, zero, tile, rows_sem, tile_sem) = refs[:SIDE], refs[SIDE:]
+    outs, (source, zero, rows_sem) = refs[:SIDE], refs[SIDE:]
     zero[...] = jnp.zeros(zero.shape, zero.dtype)
 
     @pl.loop(0, SIDE * 2 * PLANES)
     def _(i):
         source[i] = -1
 
-    over = jnp.int32(0)
     for plane in range(PLANES):
-        over = jnp.maximum(over, codes[plane, RELAY])
         for at in range(RELAY):
             code = codes[plane, at]
 
@@ -175,9 +173,7 @@
             def _():
                 source[code * PLANES + plane] = at
 
-    tile[...] = jnp.full(tile.shape, over.astype(jnp.float32)).astype(jnp.bfloat16)
     for k, out in enumerate(outs):
-        pltpu.make_async_copy(tile, out.at[pl.ds(2 * PLANES * LEVELS, 8)], tile_sem.at[k]).start()
         peer = side[k]
 
         @pl.loop(0, 2 * PLANES)
@@ -199,54 +195,62 @@
                 pltpu.make_async_copy(zero, to, rows_sem.at[k]).start()
 
     for k, out in enumerate(outs):
-        whole = out.at[pl.ds(0, 2 * PLANES * LEVELS)]
-        pltpu.make_async_copy(whole, whole, rows_sem.at[k]).wait()
-        pltpu.make_async_copy(tile, out.at[pl.ds(2 * PLANES * LEVELS, 8)], tile_sem.at[k]).wait()
+        pltpu.make_async_copy(out, out, rows_sem.at[k]).wait()
+
+
+def chosen_rows(count, size, pick):
+    i = lax.broadcasted_iota(jnp.int32, (count, size), 0)
+    j = lax.broadcasted_iota(jnp.int32, (count, size), 1)
+    return (j == pick(i)).astype(jnp.float32).astype(jnp.bfloat16)
 
 
 def settle_kernel(side, direct, *refs):
-    lasts, out, (held, sems) = refs[:SIDE], refs[SIDE], refs[SIDE + 1 :]
-    t = pl.program_id(0)
-    rows = 2 * PLANES * LEVELS
-
-    @pl.when(t == 0)
-    def _():
-        copies = [
-            pltpu.make_async_copy(last.at[pl.ds(0, rows)], held.at[side[k]], sems.at[k])
-            for k, last in enumerate(lasts)
-        ]
-        for copy in copies:
-            copy.start()
-        for copy in copies:
-            copy.wait()
-
-    plane = lax.div(t, SIDE // 2)
-    pair = lax.rem(t, SIDE // 2) * 2
-    parts = []
-    for j in range(2):
-        for r in range(2):
-            parts.append(direct[j, r * LEVELS : (r + 1) * LEVELS, :])
-        for r in range(2):
-            start = pl.multiple_of((plane * 2 + r) * LEVELS, LEVELS)
-            parts.append(held[pair + j, pl.ds(start, LEVELS), :])
-    stacked = jnp.stack([p.astype(jnp.float32) for p in parts], 0)
-    out[:LEVELS] = jnp.swapaxes(stacked, 0, 1).astype(out.dtype)
-    new = [direct[j, 2 * LEVELS : 2 * LEVELS + 4, :] for j in range(2)]
-    out[LEVELS] = jnp.concatenate(new, 0)
+    lasts, (out, logp, held) = refs[:SIDE], refs[SIDE:]
+    for k, last in enumerate(lasts):
+        held[side[k]] = last[...]
+    turn = chosen_rows(WIDTH, WIDTH, lambda i: lax.rem(i, 16) * 16 + lax.div(i, 16))
+    for group in range(2):
+        for low in range(0, LEVELS, 16):
+            parts = []
+            for j in range(4 * group, 4 * group + 4):
+                for ref in (direct, held):
+                    for r in range(2):
+                        start = r * LEVELS + low
+                        parts.append(ref[j, start : start + 16, :])
+            turned = jnp.dot(turn, jnp.concatenate(parts, 0), preferred_element_type=jnp.float32)
+            turned = turned.astype(jnp.bfloat16).reshape(16, 16, WIDTH)
+            out[low : low + 16, 16 * group : 16 * group + 16, :] = turned
+    tiles = jnp.concatenate([direct[j, 2 * LEVELS :, :] for j in range(SIDE)], 0)
+    new = chosen_rows(4 * SIDE, 8 * SIDE, lambda i: lax.div(i, 4) * 8 + lax.rem(i, 4))
+    out[LEVELS] = jnp.dot(new, tiles, preferred_element_type=jnp.float32).astype(jnp.bfloat16)
+    spread = chosen_rows(4 * SIDE, 8 * SIDE, lambda i: lax.div(i, 4) * 8 + 4)
+    terms = jnp.dot(spread, tiles, preferred_element_type=jnp.float32)
+    slot = lax.broadcasted_iota(jnp.int32, terms.shape, 0)
+    lane = lax.broadcasted_iota(jnp.int32, terms.shape, 1)
+    mine = lax.div(lane, 3 * OUTCOMES) == lax.rem(slot, 4)
+    terms = jnp.where(mine, terms, 0.0).astype(jnp.bfloat16)
+    lane = lax.broadcasted_iota(jnp.int32, (WIDTH, 128), 0)
+    outcome = lax.broadcasted_iota(jnp.int32, (WIDTH, 128), 1)
+    gather = (lax.rem(lane, OUTCOMES) == outcome).astype(jnp.float32).astype(jnp.bfloat16)
+    logp[...] = jnp.dot(terms, gather, preferred_element_type=jnp.float32)
 
 
 def settle(side, direct, lasts):
     return pl.pallas_call(
         settle_kernel,
-        grid=(PEERS // 2,),
-        out_shape=jax.ShapeDtypeStruct((LEVELS + 1, 4 * PEERS, WIDTH), jnp.bfloat16),
-        in_specs=[SMEM, pl.BlockSpec((2, DIRECT, WIDTH), lambda t: (t, 0, 0))] + [ANY] * SIDE,
-        out_specs=pl.BlockSpec((LEVELS + 1, 8, WIDTH), lambda t: (0, t, 0)),
-        scratch_shapes=[
-            pltpu.VMEM((SIDE, 2 * PLANES * LEVELS, WIDTH), jnp.bfloat16),
-            pltpu.SemaphoreType.DMA((SIDE,)),
-        ],
-        compiler_params=pltpu.CompilerParams(vmem_limit_bytes=32 << 20),
+        grid=(PLANES,),
+        out_shape=(
+            jax.ShapeDtypeStruct((LEVELS + 1, 4 * PEERS, WIDTH), jnp.bfloat16),
+            jax.ShapeDtypeStruct((4 * PEERS, 128), jnp.float32),
+        ),
+        in_specs=[SMEM, pl.BlockSpec((SIDE, DIRECT, WIDTH), lambda t: (t, 0, 0))]
+        + [pl.BlockSpec((2 * LEVELS, WIDTH), lambda t: (t, 0))] * SIDE,
+        out_specs=(
+            pl.BlockSpec((LEVELS + 1, 4 * SIDE, WIDTH), lambda t: (0, t, 0)),
+            pl.BlockSpec((4 * SIDE, 128), lambda t: (t, 0)),
+        ),
+        scratch_shapes=[pltpu.VMEM((SIDE, 2 * LEVELS, WIDTH), jnp.bfloat16)],
+        compiler_params=pltpu.CompilerParams(vmem_limit_bytes=24 << 20),
         name="settle",
     )(side, direct, *lasts)
 
@@ -277,22 +281,8 @@
     return [(i, i ^ bit) for i in range(size)]
 
 
-def summed_in_plane(grads):
-    for axis, size, bit in (
-        ("sample", PEERS, 1),
-        ("rep", 4, 1),
-        ("rep", 4, 2),
-        ("sample", PEERS, 2),
-        ("sample", PEERS, 4),
-    ):
-        grads = grads + lax.ppermute(grads, axis, xor_pairs(size, bit))
-    return grads
-
-
-def summed_over_planes(grads):
-    terms = [grads] + [
-        lax.ppermute(grads, "sample", xor_pairs(PEERS, SIDE * k)) for k in range(1, PLANES)
-    ]
+def tree_sum(x, axis, size, bits):
+    terms = [x] + [lax.ppermute(x, axis, xor_pairs(size, bit)) for bit in bits]
     while len(terms) > 1:
         terms = [terms[i] + terms[i + 1] for i in range(0, len(terms), 2)]
     return terms[0]
@@ -312,16 +302,19 @@
     me = lax.axis_index("sample")
     y, core = lax.rem(lax.div(me, 2), 4), lax.rem(me, 2)
 
-    relay = pl.pallas_call(
+    relay, over = pl.pallas_call(
         relay_kernel,
-        out_shape=jax.ShapeDtypeStruct((PLANES, PIECE, WIDTH), jnp.bfloat16),
+        out_shape=(
+            jax.ShapeDtypeStruct((PLANES, PIECE, WIDTH), jnp.bfloat16),
+            jax.ShapeDtypeStruct((4, 128), jnp.float32),
+        ),
         in_specs=[SMEM, ANY],
-        out_specs=ANY,
+        out_specs=(ANY, pl.BlockSpec(memory_space=pltpu.VMEM)),
         scratch_shapes=[
             pltpu.SMEM((PEERS,), jnp.int32),
             pltpu.SMEM((PLANES + 1,), jnp.int32),
             pltpu.VMEM((PLANES, 8, WIDTH), jnp.float32),
-            pltpu.VMEM((PLANES, 8, WIDTH), jnp.bfloat16),
+            pltpu.VMEM((PLANES, PIECE, WIDTH), jnp.bfloat16),
             pltpu.SemaphoreType.DMA,
             pltpu.SemaphoreType.DMA,
         ],
@@ -332,7 +325,14 @@
     both, logp, grad_out, grad_head = decode_rows(
         tokens, cache, coef, chosen, gain, w_query, w_key, w_value, w_out, w_head
     )
-    grads = summed_in_plane(jnp.concatenate([grad_out, grad_head], 0))
+    sums = jnp.concatenate([grad_out, grad_head, over], 0)
+    sums = tree_sum(sums, "rep", 4, (1, 2, 3))
+    sums = tree_sum(sums, "sample", PEERS, (2, 4, 6))
+    sums = tree_sum(sums, "sample", PEERS, (1,))
+    share = sums.shape[0] // SIDE
+    piece = lax.dynamic_slice_in_dim(sums, (y * 2 + core) * share, share, 0)
+    piece = jnp.concatenate([piece, sums[-1:]], 0)
+    piece = tree_sum(piece, "sample", PEERS, [SIDE * k for k in range(1, PLANES)])
 
     rows = jnp.arange(ROWS, dtype=jnp.int32)
     same = (target[:, None] == target[None, :]) & (rows[:, None] < rows[None, :])
@@ -346,9 +346,10 @@
         ((0, 0), (0, 3), (0, WIDTH - 12 * OUTCOMES)),
     )
     tiles = jnp.concatenate([new_rows, logp_row], 1)
-    direct = exchanged(pack_direct(0, target, cache, tiles))
-
-    codes = relayed[:, RELAY * LEVELS, : 2 * RELAY].astype(jnp.int32)
+    packed, piece = lax.optimization_barrier((pack_direct(0, target, cache, tiles), piece))
+    direct = exchanged(packed)
+
+    codes = relayed[:, RELAY * LEVELS, :RELAY].astype(jnp.int32)
     shifts = [(dy, dc) for dy in range(4) for dc in range(2)]
     onto = jnp.stack([lax.rem(y + dy, 4) * 2 + (core ^ dc) for dy, dc in shifts])
     came = jnp.stack([lax.rem(y - dy + 4, 4) * 2 + (core ^ dc) for dy, dc in shifts])
@@ -360,14 +361,11 @@
         scratch_shapes=[
             pltpu.SMEM((SIDE * 2 * PLANES,), jnp.int32),
             pltpu.VMEM((LEVELS, WIDTH), jnp.bfloat16),
-            pltpu.VMEM((8, WIDTH), jnp.bfloat16),
-            pltpu.SemaphoreType.DMA((SIDE,)),
             pltpu.SemaphoreType.DMA((SIDE,)),
         ],
         name="pack_plane",
     )(codes, onto.astype(jnp.int32), relayed)
-    lasts = [onward[0]]
-    for k in range(1, SIDE):
+    def in_plane(x, k):
         dy, dc = shifts[k]
         pairs = [
             ((z * 4 + y0) * 2 + c0, (z * 4 + (y0 + dy) % 4) * 2 + (c0 ^ dc))
@@ -375,11 +373,16 @@
             for y0 in range(4)
             for c0 in range(2)
         ]
-        lasts.append(lax.ppermute(onward[k], "sample", pairs))
-    grads, lasts = lax.optimization_barrier((grads, lasts))
-    grads = summed_over_planes(grads)
-    over = jnp.max(jnp.stack([last[2 * PLANES * LEVELS, 0] for last in lasts]))
+        return lax.ppermute(x, "sample", pairs)
+
+    lasts = [onward[0]] + [in_plane(onward[k], k) for k in range(1, SIDE)]
+    piece, lasts = lax.optimization_barrier((piece, lasts))
     came = came.astype(jnp.int32)
+    shares = jnp.stack([piece[:share]] + [in_plane(piece[:share], k) for k in range(1, SIDE)])
+    peers = jnp.arange(SIDE, dtype=jnp.int32)
+    order = lax.rem(y - lax.div(peers, 2) + 4, 4) * 2 + (core ^ lax.rem(peers, 2))
+    ours = (order[:, None] == peers[None, :])[..., None, None]
+    grads = jnp.sum(jnp.where(ours, shares[None], 0.0), 1).reshape(sums.shape)
 
     def by_relay(direct, lasts):
         return settle(came, direct, lasts)
@@ -391,13 +394,15 @@
         high = [
             lax.dynamic_index_in_dim(high, came[k], 0, keepdims=False) for k in range(SIDE)
         ]
-        return settle(came, direct, [jnp.pad(h, ((0, 8), (0, 0))) for h in high])
-
-    new_cache = lax.cond(over > 0, by_pairs, by_relay, direct, lasts)
-    terms = direct[:, 2 * LEVELS + 4, : 12 * OUTCOMES].astype(jnp.float32)
-    terms = terms.reshape(4 * PEERS, 3, OUTCOMES)
-    log_probs = (terms[:, 2] + terms[:, 1]) + terms[:, 0]
-    return (jnp.swapaxes(new_cache, 0, 1), log_probs, grads[:ROWS], grads[ROWS:].T)
+        return settle(came, direct, high)
+
+    new_cache, log_probs = lax.cond(piece[share, 0] > 0, by_pairs, by_relay, direct, lasts)
+    return (
+        jnp.swapaxes(new_cache, 0, 1),
+        log_probs[:, :OUTCOMES],
+        grads[:ROWS],
+        grads[ROWS : ROWS + OUTCOMES].T,
+    )
 
 
 def solution(mesh):

time: 234 us -> 199 us (0.85)
  the two profiles are of different devices: /device:TPU:1 before, /device:TPU:96 now
where the time goes in v2:
time: 199 us; the launch traced here: 197 us
  waiting for transfers between devices  70.2 us (35%)
  starting transfers between devices  54.8 us (28%)
  Pallas kernels  50.3 us (25%)
  local copies, waits for them, and re-layouts  11.6 us (6%)
  other arithmetic  6.74 us (3%)
    ppermute x14, waiting for transfers between devices, in_plane(): return lax.ppermute(x, 'sample', pairs)  60.1 us
    pallas_call x1, Pallas kernels, on_device(): pl.pallas_call(forward_kernel, out_shape=[jax.ShapeDtypeStruct((LAST, WID...  25.2 us
    ppermute x14, starting transfers between devices, tree_sum(): terms = [x] + [lax.ppermute(x, axis, xor_pairs(size, bit)) for bit in bits]  23.2 us
    all_to_all x2, starting transfers between devices, exchanged(): lax.all_to_all(x, 'sample', split_axis=0, concat_axis=0, tiled=True, axis...  17.2 us
    ppermute x14, starting transfers between devices, in_plane(): return lax.ppermute(x, 'sample', pairs)  14.3 us
    ppermute x14, waiting for transfers between devices, tree_sum(): terms = [x] + [lax.ppermute(x, axis, xor_pairs(size, bit)) for bit in bits]  10.1 us
    pallas_call x1, Pallas kernels, pack_direct(): pl.pallas_call(functools.partial(direct_kernel, low), out_shape=jax.Shape...  10 us
    pallas_call x1, Pallas kernels, settle(): pl.pallas_call(settle_kernel, grid=(PLANES,), out_shape=(jax.ShapeDtypeSt...  9.01 us
  transfers between devices with their start and end apart: 30, of which 10 were waited for; matrix products, arithmetic and copies ran while one was open for 10% of the time, Pallas kernels for 18%

profile of v2, /device:TPU:96, one launch (start us, length us, event | category | flops | bytes accessed | tf_op | source)
XLA Modules:
  0.0 197.5 jit_solution(4307701211809521788)
XLA Ops:
  0.7 6.2 %pack_relay.1 = (bf16[8,392,256]{2,1,0:T(8,128)(2,1)}, f32[4,128]{1,0:T(4,128)}) custom-call(s32[128]{0:T(128)} %bitcast.100, bf16[128,48,256]{2,1,0:T(8,128)(2,1)} %cache.3), custom_call_target="tpu_custom_call" | custom-call | tf_op jit(solution)/shard_map/pack_relay/pallas_call | solution.py:305
  6.8 7.6 %all-to-all-start.1 = ((bf16[8,392,256]{2,1,0:T(8,128)(2,1)}), bf16[8,392,256]{2,1,0:T(8,128)(2,1)}, u32[]{:S(2)}, u32[]{:S(2)}) async-start(bf16[8,392,256]{2,1,0:T(8,128)(2,1)} %get-tuple-element.104), calls=%async_computation.1 | async-start | bytes 3211264 | tf_op jit(solution)/shard_map/all_to_all | solution.py:275
  14.5 2.2 %fusion.31 = (bf16[128,48,128]{2,1,0:T(8,128)(2,1)}, bf16[128,48,128]{2,1,0:T(8,128)(2,1)}) fusion(bf16[128,48,256]{2,1,0:T(8,128)(2,1)S(1)} %copy-done.1), kind=kLoop, calls=%fused_computation.86 | loop fusion | bytes 6291456 | tf_op jit(solution)/shard_map/slice | solution.py:42
  16.7 0.1 fusion.6
  16.8 0.2 convolution_convert_fusion.1
  17.1 0.2 convolution_convert_fusion.2
  17.3 0.2 bitcast_convert_fusion
  17.6 2.8 %copy.54 = bf16[128,48,128]{0,2,1:T(8,128)(2,1)} copy(bf16[128,48,128]{2,1,0:T(8,128)(2,1)} %get-tuple-element.146) | data formatting | bytes 3145728
  20.4 2.0 %multiply_reduce_fusion.1 = f32[128,4,48]{0,1,2:T(4,128)S(1)} fusion(f32[128,4,32]{0,2,1:T(8,128)S(1)} %get-tuple-element.153, bf16[128,48,128]{0,2,1:T(8,128)(2,1)} %copy.54), kind=kLoop, calls=%fused_computation.9 | loop fusion | flops 2334720 | bytes 1736704
  22.7 2.8 %copy.55 = bf16[128,48,128]{0,2,1:T(8,128)(2,1)} copy(bf16[128,48,128]{2,1,0:T(8,128)(2,1)} %get-tuple-element.147) | data formatting | bytes 3145728
  25.5 1.7 multiply_reduce_fusion
  27.3 0.2 fusion.1
  27.5 0.1 fusion.32
  27.7 0.1 fusion.17
  27.9 0.3 fusion.18
  28.2 0.2 fusion.33
  28.4 3.1 %collective-permute-start.1 = (f32[136,128]{1,0:T(8,128)S(1)}, f32[136,128]{1,0:T(8,128)S(1)}, u32[]{:S(2)}, u32[]{:S(2)}) collective-permute-start(f32[136,128]{1,0:T(8,128)S(1)} %pad_maximum_fusion), channel_id=1, source_target_pairs={{0,2},{1,3},{2,0},{3,1},{4,6},{5,7},{6,4},{7,5},{8,10},{9,11},{10,... | collective-permute-start | bytes 208904 | tf_op jit(solution)/shard_map/ppermute | solution.py:285
  31.4 1.2 collective-permute-start.2
  32.7 1.6 collective-permute-done.1
  34.3 2.7 %collective-permute-done.2 = f32[136,128]{1,0:T(8,128)S(1)} collective-permute-done((f32[136,128]{1,0:T(8,128)S(1)}, f32[136,128]{1,0:T(8,128)S(1)}, u32[]{:S(2)}, u32[]{:S(2)}) %collective-permute-start.2) | collective-permute-done | bytes 69664 | tf_op jit(solution)/shard_map/ppermute | solution.py:285
  37.0 3.1 %collective-permute-start.5 = (f32[136,128]{1,0:T(8,128)S(1)}, f32[136,128]{1,0:T(8,128)S(1)}, u32[]{:S(2)}, u32[]{:S(2)}) collective-permute-start(f32[136,128]{1,0:T(8,128)S(1)} %add_add_fusion.1), channel_id=1, source_target_pairs={{0,24},{4,28},{8,16},{12,20},{16,8},{20,12},{24,0},{28,4},{32,56},... | collective-permute-start | bytes 208904 | tf_op jit(solution)/shard_map/ppermute | solution.py:285
  40.2 0.7 collective-permute-start.4
  40.8 0.3 collective-permute-start.3
  41.3 2.1 %collective-permute-done.5 = f32[136,128]{1,0:T(8,128)S(1)} collective-permute-done((f32[136,128]{1,0:T(8,128)S(1)}, f32[136,128]{1,0:T(8,128)S(1)}, u32[]{:S(2)}, u32[]{:S(2)}) %collective-permute-start.5) | collective-permute-done | bytes 69664 | tf_op jit(solution)/shard_map/ppermute | solution.py:285
  43.4 2.6 %collective-permute-done.4 = f32[136,128]{1,0:T(8,128)S(1)} collective-permute-done((f32[136,128]{1,0:T(8,128)S(1)}, f32[136,128]{1,0:T(8,128)S(1)}, u32[]{:S(2)}, u32[]{:S(2)}) %collective-permute-start.4) | collective-permute-done | bytes 69664 | tf_op jit(solution)/shard_map/ppermute | solution.py:285
  46.2 1.1 collective-permute-done.6
  47.4 2.8 %collective-permute-start.12 = (f32[18,128]{1,0:T(8,128)S(1)}, f32[18,128]{1,0:T(8,128)S(1)}, u32[]{:S(2)}, u32[]{:S(2)}) collective-permute-start(f32[18,128]{1,0:T(8,128)S(1)} %pad_maximum_fusion.1), channel_id=1, source_target_pairs={{0,192},{4,196},{8,200},{12,204},{16,208},{20,212},{24,216},{28,22... | collective-permute-start | bytes 27656 | tf_op jit(solution)/shard_map/ppermute | solution.py:285
  50.3 0.2 convolution_convert_fusion
  50.6 0.1 copy.34
  50.9 5.9 %collective-permute-start.10 = (f32[18,128]{1,0:T(8,128)S(1)}, f32[18,128]{1,0:T(8,128)S(1)}, u32[]{:S(2)}, u32[]{:S(2)}) collective-permute-start(f32[18,128]{1,0:T(8,128)S(1)} %pad_maximum_fusion.1), channel_id=1, source_target_pairs={{0,128},{4,132},{8,136},{12,140},{16,144},{20,148},{24,152},{28,15... | collective-permute-start | bytes 27656 | tf_op jit(solution)/shard_map/ppermute | solution.py:285
  56.8 0.6 collective-permute-start.9
  57.4 1.5 collective-permute-start.8
  58.8 0.6 collective-permute-start.13
  59.4 3.3 %collective-permute-start.7 = (f32[18,128]{1,0:T(8,128)S(1)}, f32[18,128]{1,0:T(8,128)S(1)}, u32[]{:S(2)}, u32[]{:S(2)}) collective-permute-start(f32[18,128]{1,0:T(8,128)S(1)} %pad_maximum_fusion.1), channel_id=1, source_target_pairs={{0,32},{4,36},{8,40},{12,44},{16,48},{20,52},{24,56},{28,60},{32,0... | collective-permute-start | bytes 27656 | tf_op jit(solution)/shard_map/ppermute | solution.py:285
  62.7 0.9 fusion.3.tiles
  63.5 10.0 %pack_direct.3 = bf16[64,104,256]{2,1,0:T(8,128)(2,1)} custom-call(s32[128]{0:T(128)S(1)} %bitcast.102, bf16[128,48,256]{2,1,0:T(8,128)(2,1)S(1)} %copy-done.1, bf16[64,8,256]{2,1,0:T(8,128)(2,1)} %fusion.3.tiles), custom_call_target="tpu_custom_call" | custom-call | tf_op jit(solution)/shard_map/pack_direct/pallas_call | solution.py:259
  73.6 9.6 %all-to-all-start.2 = ((bf16[64,104,256]{2,1,0:T(8,128)(2,1)}), bf16[64,104,256]{2,1,0:T(8,128)(2,1)}, u32[]{:S(2)}, u32[]{:S(2)}) async-start(bf16[64,104,256]{2,1,0:T(8,128)(2,1)} %pack_direct.3), calls=%async_computation.2 | async-start | bytes 6815744 | tf_op jit(solution)/shard_map/all_to_all | solution.py:275
  83.3 0.6 stack.77.side
  83.9 1.3 slice_convert_fusion
  85.2 25.2 %pack_plane.1 = (bf16[768,256]{1,0:T(8,128)(2,1)}, bf16[768,256]{1,0:T(8,128)(2,1)}, bf16[768,256]{1,0:T(8,128)(2,1)}, bf16[768,256]{1,0:T(8,128)(2,1)}, bf16[76...) custom-call(s32[8,8]{1,0:T(8,128)} %bitcast.99, ...), custom_call_target="tpu_custom_call" | custom-call | tf_op jit(solution)/shard_map/pack_plane/pallas_call | solution.py:356
  110.5 0.2 collective-permute-start.15
  110.7 1.6 collective-permute-start.16
  112.2 2.8 %collective-permute-start.17 = (bf16[768,256]{1,0:T(8,128)(2,1)}, bf16[768,256]{1,0:T(8,128)(2,1)}, u32[]{:S(2)}, u32[]{:S(2)}) collective-permute-start(bf16[768,256]{1,0:T(8,128)(2,1)} %get-tuple-element.109), channel_id=1, source_target_pairs={{0,16},{4,20},{8,24},{12,28},{16,0},{20,4},{24,8},{28,12},{32,48},... | collective-permute-start | bytes 1179656 | tf_op jit(solution)/shard_map/ppermute | solution.py:376
  115.0 0.8 collective-permute-start.18
  115.8 1.1 collective-permute-start.19
  116.9 17.6 %collective-permute-done.15 = bf16[768,256]{1,0:T(8,128)(2,1)} collective-permute-done((bf16[768,256]{1,0:T(8,128)(2,1)}, bf16[768,256]{1,0:T(8,128)(2,1)}, u32[]{:S(2)}, u32[]{:S(2)}) %collective-permute-start.15) | collective-permute-done | bytes 393248 | tf_op jit(solution)/shard_map/ppermute | solution.py:376
  134.6 36.1 %collective-permute-done.16 = bf16[768,256]{1,0:T(8,128)(2,1)} collective-permute-done((bf16[768,256]{1,0:T(8,128)(2,1)}, bf16[768,256]{1,0:T(8,128)(2,1)}, u32[]{:S(2)}, u32[]{:S(2)}) %collective-permute-start.16) | collective-permute-done | bytes 393248 | tf_op jit(solution)/shard_map/ppermute | solution.py:376
  170.7 0.7 collective-permute-done.20
  171.4 2.2 %collective-permute-start.26 = (f32[17,128]{1,0:T(8,128)S(1)}, f32[17,128]{1,0:T(8,128)S(1)}, u32[]{:S(2)}, u32[]{:S(2)}) collective-permute-start(f32[17,128]{1,0:T(8,128)S(1)} %bitcast.92), channel_id=1, source_target_pairs={{0,24},{4,28},{8,0},{12,4},{16,8},{20,12},{24,16},{28,20},{32,56},... | collective-permute-start | bytes 26120 | tf_op jit(solution)/shard_map/ppermute | solution.py:376
  173.6 1.4 collective-permute-start.25
  175.0 1.3 collective-permute-start.24
  176.3 0.1 collective-permute-start.23
  176.5 0.5 collective-permute-start.21
  177.0 0.5 slice.53
  178.2 1.7 collective-permute-start.22
  179.9 3.3 %collective-permute-done.22 = f32[17,128]{1,0:T(8,128)S(1)} collective-permute-done((f32[17,128]{1,0:T(8,128)S(1)}, f32[17,128]{1,0:T(8,128)S(1)}, u32[]{:S(2)}, u32[]{:S(2)}) %collective-permute-start.22) | collective-permute-done | bytes 8736 | tf_op jit(solution)/shard_map/ppermute | solution.py:376
  183.2 0.6 collective-permute-start.27
  183.8 2.5 %collective-permute-done.27 = f32[17,128]{1,0:T(8,128)S(1)} collective-permute-done((f32[17,128]{1,0:T(8,128)S(1)}, f32[17,128]{1,0:T(8,128)S(1)}, u32[]{:S(2)}, u32[]{:S(2)}) %collective-permute-start.27) | collective-permute-done | bytes 8736 | tf_op jit(solution)/shard_map/ppermute | solution.py:376
  186.3 0.2 select_reduce_fusion
  186.5 0.6 slice.62
  187.2 0.6 slice_bitcast_fusion
  187.8 9.1 %conditional.1 = (bf16[49,256,256]{2,1,0:T(8,128)(2,1)}, f32[256,4]{0,1:T(4,128)S(1)}) conditional(s32[]{:T(128)} %bitcast.31, (s32[8]{0:T(128)S(1)}, bf16[64,104,256]{2,1,0:T(8,128)(2,1)}, bf16[768,256]{1,0:T(8,128)(2,1)}, bf16[768,256]{1,0:T(8,128)(2,1)}, bf16[768,256]{1,0:T(8,128)(2,1)}, /*index=5*/bf16[768,256]{1,0:T(8,128)(2,1)}, ...), branch_computations={%region_7.8_spmd, %region_8.9_spmd} | conditional | flops 24 | bytes 29368660 | solution.py:399
  187.8 9.0 %settle.2 = (bf16[49,256,256]{2,1,0:T(8,128)(2,1)}, f32[256,128]{1,0:T(8,128)S(1)}) custom-call(s32[8]{0:T(128)S(1)} %get-tuple-element.49.side, bf16[64,104,256]{2,1,0:T(8,128)(2,1)} %get-tuple-element.50.direct, bf16[768,256]{1,0:T(8,128)(2,1)} %get-tuple-element.51.refs_0_, bf16[768,256]{1,0:T(8,128)(2,1)} %get-tuple-element.52.refs_1_, ...), custom_call_target="tpu_custom_call" | custom-call | tf_op jit(solution)/shard_map/cond/branch_0_fun/settle/pallas_call | solution.py:239
  196.9 0.6 copy-done.10
  (92 shorter events, 1.5 us)
Async XLA Ops:
  0.6 16.7 %copy-start = (bf16[128,128]{1,0:T(8,128)(2,1)S(1)}, bf16[128,128]{1,0:T(8,128)(2,1)}, u32[]{:S(2)}) copy-start(bf16[128,128]{1,0:T(8,128)(2,1)} %param.16) | copy-start | bytes 98308
  0.6 13.8 %copy-start.1 = (bf16[128,48,256]{2,1,0:T(8,128)(2,1)S(1)}, bf16[128,48,256]{2,1,0:T(8,128)(2,1)}, u32[]{:S(2)}) copy-start(bf16[128,48,256]{2,1,0:T(8,128)(2,1)} %cache.3) | copy-start | bytes 9437188
  6.8 66.8 %all-to-all-start.1 = ((bf16[8,392,256]{2,1,0:T(8,128)(2,1)}), bf16[8,392,256]{2,1,0:T(8,128)(2,1)}, u32[]{:S(2)}, u32[]{:S(2)}) async-start(bf16[8,392,256]{2,1,0:T(8,128)(2,1)} %get-tuple-element.104), calls=%async_computation.1 | async-start | bytes 3211264 | tf_op jit(solution)/shard_map/all_to_all | solution.py:275
  14.4 2.2 %copy-start.2 = (bf16[128,128]{1,0:T(8,128)(2,1)S(1)}, bf16[128,128]{1,0:T(8,128)(2,1)}, u32[]{:S(2)}) copy-start(bf16[128,128]{1,0:T(8,128)(2,1)} %param.13) | copy-start | bytes 98308
  14.4 2.4 %copy-start.3 = (bf16[128,128]{1,0:T(8,128)(2,1)S(1)}, bf16[128,128]{1,0:T(8,128)(2,1)}, u32[]{:S(2)}) copy-start(bf16[128,128]{1,0:T(8,128)(2,1)} %param.18) | copy-start | bytes 98308
  14.4 2.4 %copy-start.7 = (f32[128]{0:T(128)S(1)}, f32[128]{0:T(128)}, u32[]{:S(2)}) copy-start(f32[128]{0:T(128)} %param.15) | copy-start | bytes 1540
  14.4 2.6 %copy-start.4 = (bf16[128,128]{1,0:T(8,128)(2,1)S(1)}, bf16[128,128]{1,0:T(8,128)(2,1)}, u32[]{:S(2)}) copy-start(bf16[128,128]{1,0:T(8,128)(2,1)} %param.17) | copy-start | bytes 98308
  22.4 4.9 %copy-start.5 = (bf16[128,128]{1,0:T(8,128)(2,1)S(1)}, bf16[128,128]{1,0:T(8,128)(2,1)}, u32[]{:S(2)}) copy-start(bf16[128,128]{1,0:T(8,128)(2,1)} %param.19) | copy-start | bytes 98308
  22.4 5.1 %copy-start.9 = (bf16[128,4]{0,1:T(4,128)(2,1)S(1)}, bf16[128,4]{0,1:T(4,128)(2,1)}, u32[]{:S(2)}) copy-start(bf16[128,4]{0,1:T(4,128)(2,1)} %param.20) | copy-start | bytes 3076
  22.5 5.3 %copy-start.11 = (s32[128]{0:T(128)S(1)}, s32[128]{0:T(128)}, u32[]{:S(2)}) copy-start(s32[128]{0:T(128)} %param.22) | copy-start | bytes 1540
  22.5 5.3 %copy-start.12 = (f32[128]{0:T(128)S(1)}, f32[128]{0:T(128)}, u32[]{:S(2)}) copy-start(f32[128]{0:T(128)} %param.21) | copy-start | bytes 1540
  22.5 5.9 %copy-start.6 = (f32[4,128]{1,0:T(4,128)S(1)}, f32[4,128]{1,0:T(4,128)}, u32[]{:S(2)}) copy-start(f32[4,128]{1,0:T(4,128)} %get-tuple-element.102) | copy-start | bytes 6148
  22.6 18.6 %copy-start.8 = (s32[128,1]{0,1:T(1,128)S(1)}, s32[128,1]{0,1:T(1,128)}, u32[]{:S(2)}) copy-start(s32[128,1]{0,1:T(1,128)} %param.23) | copy-start | bytes 1540
  28.4 5.9 %collective-permute-start.1 = (f32[136,128]{1,0:T(8,128)S(1)}, f32[136,128]{1,0:T(8,128)S(1)}, u32[]{:S(2)}, u32[]{:S(2)}) collective-permute-start(f32[136,128]{1,0:T(8,128)S(1)} %pad_maximum_fusion), channel_id=1, source_target_pairs={{0,2},{1,3},{2,0},{3,1},{4,6},{5,7},{6,4},{7,5},{8,10},{9,11},{10,... | collective-permute-start | bytes 208904 | tf_op jit(solution)/shard_map/ppermute | solution.py:285
  31.4 5.5 %collective-permute-start.2 = (f32[136,128]{1,0:T(8,128)S(1)}, f32[136,128]{1,0:T(8,128)S(1)}, u32[]{:S(2)}, u32[]{:S(2)}) collective-permute-start(f32[136,128]{1,0:T(8,128)S(1)} %pad_maximum_fusion), channel_id=1, source_target_pairs={{0,3},{1,2},{2,1},{3,0},{4,7},{5,6},{6,5},{7,4},{8,11},{9,10},{10,... | collective-permute-start | bytes 208904 | tf_op jit(solution)/shard_map/ppermute | solution.py:285
  32.7 4.3 %collective-permute-start = (f32[136,128]{1,0:T(8,128)S(1)}, f32[136,128]{1,0:T(8,128)S(1)}, u32[]{:S(2)}, u32[]{:S(2)}) collective-permute-start(f32[136,128]{1,0:T(8,128)S(1)} %pad_maximum_fusion), channel_id=1, source_target_pairs={{0,1},{1,0},{2,3},{3,2},{4,5},{5,4},{6,7},{7,6},{8,9},{9,8},{10,11... | collective-permute-start | bytes 208904 | tf_op jit(solution)/shard_map/ppermute | solution.py:285
  37.0 6.3 %collective-permute-start.5 = (f32[136,128]{1,0:T(8,128)S(1)}, f32[136,128]{1,0:T(8,128)S(1)}, u32[]{:S(2)}, u32[]{:S(2)}) collective-permute-start(f32[136,128]{1,0:T(8,128)S(1)} %add_add_fusion.1), channel_id=1, source_target_pairs={{0,24},{4,28},{8,16},{12,20},{16,8},{20,12},{24,0},{28,4},{32,56},... | collective-permute-start | bytes 208904 | tf_op jit(solution)/shard_map/ppermute | solution.py:285
  40.2 5.8 %collective-permute-start.4 = (f32[136,128]{1,0:T(8,128)S(1)}, f32[136,128]{1,0:T(8,128)S(1)}, u32[]{:S(2)}, u32[]{:S(2)}) collective-permute-start(f32[136,128]{1,0:T(8,128)S(1)} %add_add_fusion.1), channel_id=1, source_target_pairs={{0,16},{4,20},{8,24},{12,28},{16,0},{20,4},{24,8},{28,12},{32,48},... | collective-permute-start | bytes 208904 | tf_op jit(solution)/shard_map/ppermute | solution.py:285
  40.8 5.1 %collective-permute-start.3 = (f32[136,128]{1,0:T(8,128)S(1)}, f32[136,128]{1,0:T(8,128)S(1)}, u32[]{:S(2)}, u32[]{:S(2)}) collective-permute-start(f32[136,128]{1,0:T(8,128)S(1)} %add_add_fusion.1), channel_id=1, source_target_pairs={{0,8},{4,12},{8,0},{12,4},{16,24},{20,28},{24,16},{28,20},{32,40},... | collective-permute-start | bytes 208904 | tf_op jit(solution)/shard_map/ppermute | solution.py:285
  46.0 1.3 collective-permute-start.6
  47.4 11.4 %collective-permute-start.12 = (f32[18,128]{1,0:T(8,128)S(1)}, f32[18,128]{1,0:T(8,128)S(1)}, u32[]{:S(2)}, u32[]{:S(2)}) collective-permute-start(f32[18,128]{1,0:T(8,128)S(1)} %pad_maximum_fusion.1), channel_id=1, source_target_pairs={{0,192},{4,196},{8,200},{12,204},{16,208},{20,212},{24,216},{28,22... | collective-permute-start | bytes 27656 | tf_op jit(solution)/shard_map/ppermute | solution.py:285
  50.2 9.2 %collective-permute-start.11 = (f32[18,128]{1,0:T(8,128)S(1)}, f32[18,128]{1,0:T(8,128)S(1)}, u32[]{:S(2)}, u32[]{:S(2)}) collective-permute-start(f32[18,128]{1,0:T(8,128)S(1)} %pad_maximum_fusion.1), channel_id=1, source_target_pairs={{0,160},{4,164},{8,168},{12,172},{16,176},{20,180},{24,184},{28,18... | collective-permute-start | bytes 27656 | tf_op jit(solution)/shard_map/ppermute | solution.py:285
  50.9 22.6 %collective-permute-start.10 = (f32[18,128]{1,0:T(8,128)S(1)}, f32[18,128]{1,0:T(8,128)S(1)}, u32[]{:S(2)}, u32[]{:S(2)}) collective-permute-start(f32[18,128]{1,0:T(8,128)S(1)} %pad_maximum_fusion.1), channel_id=1, source_target_pairs={{0,128},{4,132},{8,136},{12,140},{16,144},{20,148},{24,152},{28,15... | collective-permute-start | bytes 27656 | tf_op jit(solution)/shard_map/ppermute | solution.py:285
  56.8 16.7 %collective-permute-start.9 = (f32[18,128]{1,0:T(8,128)S(1)}, f32[18,128]{1,0:T(8,128)S(1)}, u32[]{:S(2)}, u32[]{:S(2)}) collective-permute-start(f32[18,128]{1,0:T(8,128)S(1)} %pad_maximum_fusion.1), channel_id=1, source_target_pairs={{0,96},{4,100},{8,104},{12,108},{16,112},{20,116},{24,120},{28,124... | collective-permute-start | bytes 27656 | tf_op jit(solution)/shard_map/ppermute | solution.py:285
  57.4 16.2 %collective-permute-start.8 = (f32[18,128]{1,0:T(8,128)S(1)}, f32[18,128]{1,0:T(8,128)S(1)}, u32[]{:S(2)}, u32[]{:S(2)}) collective-permute-start(f32[18,128]{1,0:T(8,128)S(1)} %pad_maximum_fusion.1), channel_id=1, source_target_pairs={{0,64},{4,68},{8,72},{12,76},{16,80},{20,84},{24,88},{28,92},{32,9... | collective-permute-start | bytes 27656 | tf_op jit(solution)/shard_map/ppermute | solution.py:285
  58.8 14.7 %collective-permute-start.13 = (f32[18,128]{1,0:T(8,128)S(1)}, f32[18,128]{1,0:T(8,128)S(1)}, u32[]{:S(2)}, u32[]{:S(2)}) collective-permute-start(f32[18,128]{1,0:T(8,128)S(1)} %pad_maximum_fusion.1), channel_id=1, source_target_pairs={{0,224},{4,228},{8,232},{12,236},{16,240},{20,244},{24,248},{28,25... | collective-permute-start | bytes 27656 | tf_op jit(solution)/shard_map/ppermute | solution.py:285
  59.4 14.2 %collective-permute-start.7 = (f32[18,128]{1,0:T(8,128)S(1)}, f32[18,128]{1,0:T(8,128)S(1)}, u32[]{:S(2)}, u32[]{:S(2)}) collective-permute-start(f32[18,128]{1,0:T(8,128)S(1)} %pad_maximum_fusion.1), channel_id=1, source_target_pairs={{0,32},{4,36},{8,40},{12,44},{16,48},{20,52},{24,56},{28,60},{32,0... | collective-permute-start | bytes 27656 | tf_op jit(solution)/shard_map/ppermute | solution.py:285
  73.6 114.2 %all-to-all-start.2 = ((bf16[64,104,256]{2,1,0:T(8,128)(2,1)}), bf16[64,104,256]{2,1,0:T(8,128)(2,1)}, u32[]{:S(2)}, u32[]{:S(2)}) async-start(bf16[64,104,256]{2,1,0:T(8,128)(2,1)} %pack_direct.3), calls=%async_computation.2 | async-start | bytes 6815744 | tf_op jit(solution)/shard_map/all_to_all | solution.py:275
  110.4 5.4 %collective-permute-start.14 = (bf16[768,256]{1,0:T(8,128)(2,1)}, bf16[768,256]{1,0:T(8,128)(2,1)}, u32[]{:S(2)}, u32[]{:S(2)}) collective-permute-start(bf16[768,256]{1,0:T(8,128)(2,1)} %get-tuple-element.106), channel_id=1, source_target_pairs={{0,4},{4,0},{8,12},{12,8},{16,20},{20,16},{24,28},{28,24},{32,36},... | collective-permute-start | bytes 1179656 | tf_op jit(solution)/shard_map/ppermute | solution.py:376
  110.5 23.9 %collective-permute-start.15 = (bf16[768,256]{1,0:T(8,128)(2,1)}, bf16[768,256]{1,0:T(8,128)(2,1)}, u32[]{:S(2)}, u32[]{:S(2)}) collective-permute-start(bf16[768,256]{1,0:T(8,128)(2,1)} %get-tuple-element.107), channel_id=1, source_target_pairs={{0,8},{4,12},{8,16},{12,20},{16,24},{20,28},{24,0},{28,4},{32,40},... | collective-permute-start | bytes 1179656 | tf_op jit(solution)/shard_map/ppermute | solution.py:376
  110.7 60.0 %collective-permute-start.16 = (bf16[768,256]{1,0:T(8,128)(2,1)}, bf16[768,256]{1,0:T(8,128)(2,1)}, u32[]{:S(2)}, u32[]{:S(2)}) collective-permute-start(bf16[768,256]{1,0:T(8,128)(2,1)} %get-tuple-element.108), channel_id=1, source_target_pairs={{0,12},{4,8},{8,20},{12,16},{16,28},{20,24},{24,4},{28,0},{32,44},... | collective-permute-start | bytes 1179656 | tf_op jit(solution)/shard_map/ppermute | solution.py:376
  112.2 58.4 %collective-permute-start.17 = (bf16[768,256]{1,0:T(8,128)(2,1)}, bf16[768,256]{1,0:T(8,128)(2,1)}, u32[]{:S(2)}, u32[]{:S(2)}) collective-permute-start(bf16[768,256]{1,0:T(8,128)(2,1)} %get-tuple-element.109), channel_id=1, source_target_pairs={{0,16},{4,20},{8,24},{12,28},{16,0},{20,4},{24,8},{28,12},{32,48},... | collective-permute-start | bytes 1179656 | tf_op jit(solution)/shard_map/ppermute | solution.py:376
  115.0 55.6 %collective-permute-start.18 = (bf16[768,256]{1,0:T(8,128)(2,1)}, bf16[768,256]{1,0:T(8,128)(2,1)}, u32[]{:S(2)}, u32[]{:S(2)}) collective-permute-start(bf16[768,256]{1,0:T(8,128)(2,1)} %get-tuple-element.110), channel_id=1, source_target_pairs={{0,20},{4,16},{8,28},{12,24},{16,4},{20,0},{24,12},{28,8},{32,52},... | collective-permute-start | bytes 1179656 | tf_op jit(solution)/shard_map/ppermute | solution.py:376
  115.8 54.9 %collective-permute-start.19 = (bf16[768,256]{1,0:T(8,128)(2,1)}, bf16[768,256]{1,0:T(8,128)(2,1)}, u32[]{:S(2)}, u32[]{:S(2)}) collective-permute-start(bf16[768,256]{1,0:T(8,128)(2,1)} %get-tuple-element.111), channel_id=1, source_target_pairs={{0,24},{4,28},{8,0},{12,4},{16,8},{20,12},{24,16},{28,20},{32,56},... | collective-permute-start | bytes 1179656 | tf_op jit(solution)/shard_map/ppermute | solution.py:376
  134.4 37.0 %collective-permute-start.20 = (bf16[768,256]{1,0:T(8,128)(2,1)}, bf16[768,256]{1,0:T(8,128)(2,1)}, u32[]{:S(2)}, u32[]{:S(2)}) collective-permute-start(bf16[768,256]{1,0:T(8,128)(2,1)} %get-tuple-element.112), channel_id=1, source_target_pairs={{0,28},{4,24},{8,4},{12,0},{16,12},{20,8},{24,20},{28,16},{32,60},... | collective-permute-start | bytes 1179656 | tf_op jit(solution)/shard_map/ppermute | solution.py:376
  171.4 12.4 %collective-permute-start.26 = (f32[17,128]{1,0:T(8,128)S(1)}, f32[17,128]{1,0:T(8,128)S(1)}, u32[]{:S(2)}, u32[]{:S(2)}) collective-permute-start(f32[17,128]{1,0:T(8,128)S(1)} %bitcast.92), channel_id=1, source_target_pairs={{0,24},{4,28},{8,0},{12,4},{16,8},{20,12},{24,16},{28,20},{32,56},... | collective-permute-start | bytes 26120 | tf_op jit(solution)/shard_map/ppermute | solution.py:376
  173.6 10.2 %collective-permute-start.25 = (f32[17,128]{1,0:T(8,128)S(1)}, f32[17,128]{1,0:T(8,128)S(1)}, u32[]{:S(2)}, u32[]{:S(2)}) collective-permute-start(f32[17,128]{1,0:T(8,128)S(1)} %bitcast.93), channel_id=1, source_target_pairs={{0,20},{4,16},{8,28},{12,24},{16,4},{20,0},{24,12},{28,8},{32,52},... | collective-permute-start | bytes 26120 | tf_op jit(solution)/shard_map/ppermute | solution.py:376
  175.0 8.8 %collective-permute-start.24 = (f32[17,128]{1,0:T(8,128)S(1)}, f32[17,128]{1,0:T(8,128)S(1)}, u32[]{:S(2)}, u32[]{:S(2)}) collective-permute-start(f32[17,128]{1,0:T(8,128)S(1)} %bitcast.94), channel_id=1, source_target_pairs={{0,16},{4,20},{8,24},{12,28},{16,0},{20,4},{24,8},{28,12},{32,48},... | collective-permute-start | bytes 26120 | tf_op jit(solution)/shard_map/ppermute | solution.py:376
  176.3 7.4 %collective-permute-start.23 = (f32[17,128]{1,0:T(8,128)S(1)}, f32[17,128]{1,0:T(8,128)S(1)}, u32[]{:S(2)}, u32[]{:S(2)}) collective-permute-start(f32[17,128]{1,0:T(8,128)S(1)} %bitcast.95), channel_id=1, source_target_pairs={{0,12},{4,8},{8,20},{12,16},{16,28},{20,24},{24,4},{28,0},{32,44},... | collective-permute-start | bytes 26120 | tf_op jit(solution)/shard_map/ppermute | solution.py:376
  176.5 1.7 collective-permute-start.21
  178.2 5.0 %collective-permute-start.22 = (f32[17,128]{1,0:T(8,128)S(1)}, f32[17,128]{1,0:T(8,128)S(1)}, u32[]{:S(2)}, u32[]{:S(2)}) collective-permute-start(f32[17,128]{1,0:T(8,128)S(1)} %bitcast.97), channel_id=1, source_target_pairs={{0,8},{4,12},{8,16},{12,20},{16,24},{20,28},{24,0},{28,4},{32,40},... | collective-permute-start | bytes 26120 | tf_op jit(solution)/shard_map/ppermute | solution.py:376
  183.2 3.1 %collective-permute-start.27 = (f32[17,128]{1,0:T(8,128)S(1)}, f32[17,128]{1,0:T(8,128)S(1)}, u32[]{:S(2)}, u32[]{:S(2)}) collective-permute-start(f32[17,128]{1,0:T(8,128)S(1)} %bitcast.98), channel_id=1, source_target_pairs={{0,28},{4,24},{8,4},{12,0},{16,12},{20,8},{24,20},{28,16},{32,60},... | collective-permute-start | bytes 26120 | tf_op jit(solution)/shard_map/ppermute | solution.py:376
  196.9 0.6 copy-start.10

commit v3 on v2

--- a/solution.py
+++ b/solution.py
@@ -19,7 +19,7 @@
 RELAY = 8
 DIRECT = 2 * LEVELS + 8
 PIECE = RELAY * LEVELS + 8
-LAST = 2 * PLANES * LEVELS
+LAST = 2 * PLANES * LEVELS + 8
 ANY = pl.BlockSpec(memory_space=pl.ANY)
 SMEM = pl.BlockSpec(memory_space=pltpu.SMEM)
 
@@ -83,7 +83,7 @@
         ref[i] = 0
 
 
-def relay_kernel(dest, cache, out, over, count, filled, meta, held, rows_sem, out_sem):
+def relay_kernel(dest, cache, out, count, filled, meta, held, rows_sem, out_sem):
     cleared(count, PEERS)
     cleared(filled, PLANES + 1)
     meta[...] = jnp.full(meta.shape, -1.0, jnp.float32)
@@ -114,9 +114,10 @@
     most = filled[0]
     for plane in range(1, PLANES):
         most = jnp.maximum(most, filled[plane])
-    over[...] = jnp.full(over.shape, jnp.where(most > RELAY, 1.0, 0.0), jnp.float32)
+    over = jnp.where(most > RELAY, 1.0, 0.0)
     for plane in range(PLANES):
-        held[plane, RELAY * LEVELS :, :] = meta[plane].astype(jnp.bfloat16)
+        tile = jnp.where(lane == RELAY, over, meta[plane])
+        held[plane, RELAY * LEVELS :, :] = tile.astype(jnp.bfloat16)
 
     @pl.loop(0, filled[PLANES])
     def _(i):
@@ -158,14 +159,18 @@
 
 
 def forward_kernel(codes, side, got, *refs):
-    outs, (source, zero, rows_sem) = refs[:SIDE], refs[SIDE:]
+    outs, (source, held, zero, tile, rows_sem, tile_sem, got_sem) = refs[:SIDE], refs[SIDE:]
+    load = pltpu.make_async_copy(got, held, got_sem)
+    load.start()
     zero[...] = jnp.zeros(zero.shape, zero.dtype)
 
     @pl.loop(0, SIDE * 2 * PLANES)
     def _(i):
         source[i] = -1
 
+    over = codes[0, RELAY]
     for plane in range(PLANES):
+        over = jnp.maximum(over, codes[plane, RELAY])
         for at in range(RELAY):
             code = codes[plane, at]
 
@@ -173,7 +178,10 @@
             def _():
                 source[code * PLANES + plane] = at
 
+    tile[...] = jnp.full(tile.shape, over.astype(jnp.float32)).astype(jnp.bfloat16)
+    load.wait()
     for k, out in enumerate(outs):
+        pltpu.make_async_copy(tile, out.at[pl.ds(LAST - 8, 8)], tile_sem.at[k]).start()
         peer = side[k]
 
         @pl.loop(0, 2 * PLANES)
@@ -187,7 +195,7 @@
             def _():
                 start = pl.multiple_of(at * LEVELS, LEVELS)
                 pltpu.make_async_copy(
-                    got.at[plane, pl.ds(start, LEVELS)], to, rows_sem.at[k]
+                    held.at[plane, pl.ds(start, LEVELS)], to, rows_sem.at[k]
                 ).start()
 
             @pl.when(at < 0)
@@ -195,7 +203,16 @@
                 pltpu.make_async_copy(zero, to, rows_sem.at[k]).start()
 
     for k, out in enumerate(outs):
-        pltpu.make_async_copy(out, out, rows_sem.at[k]).wait()
+        whole = out.at[pl.ds(0, LAST - 8)]
+        pltpu.make_async_copy(whole, whole, rows_sem.at[k]).wait()
+        pltpu.make_async_copy(tile, out.at[pl.ds(LAST - 8, 8)], tile_sem.at[k]).wait()
+
+
+def flag_kernel(*refs):
+    most = refs[0][...].astype(jnp.float32)
+    for ref in refs[1:SIDE]:
+        most = jnp.maximum(most, ref[...].astype(jnp.float32))
+    refs[SIDE][0] = jnp.where(jnp.max(most) > 0, 1, 0).astype(jnp.int32)
 
 
 def chosen_rows(count, size, pick):
@@ -251,6 +268,7 @@
         ),
         scratch_shapes=[pltpu.VMEM((SIDE, 2 * LEVELS, WIDTH), jnp.bfloat16)],
         compiler_params=pltpu.CompilerParams(vmem_limit_bytes=24 << 20),
+        cost_estimate=pl.CostEstimate(flops=2 << 30, bytes_accessed=14 << 20, transcendentals=0),
         name="settle",
     )(side, direct, *lasts)
 
@@ -267,6 +285,7 @@
             pltpu.SemaphoreType.DMA,
             pltpu.SemaphoreType.DMA,
         ],
+        cost_estimate=pl.CostEstimate(flops=0, bytes_accessed=10 << 20, transcendentals=0),
         name="pack_direct",
     )(dest, cache, tiles)
 
@@ -302,14 +321,11 @@
     me = lax.axis_index("sample")
     y, core = lax.rem(lax.div(me, 2), 4), lax.rem(me, 2)
 
-    relay, over = pl.pallas_call(
+    relay = pl.pallas_call(
         relay_kernel,
-        out_shape=(
-            jax.ShapeDtypeStruct((PLANES, PIECE, WIDTH), jnp.bfloat16),
-            jax.ShapeDtypeStruct((4, 128), jnp.float32),
-        ),
+        out_shape=jax.ShapeDtypeStruct((PLANES, PIECE, WIDTH), jnp.bfloat16),
         in_specs=[SMEM, ANY],
-        out_specs=(ANY, pl.BlockSpec(memory_space=pltpu.VMEM)),
+        out_specs=ANY,
         scratch_shapes=[
             pltpu.SMEM((PEERS,), jnp.int32),
             pltpu.SMEM((PLANES + 1,), jnp.int32),
@@ -325,14 +341,12 @@
     both, logp, grad_out, grad_head = decode_rows(
         tokens, cache, coef, chosen, gain, w_query, w_key, w_value, w_out, w_head
     )
-    sums = jnp.concatenate([grad_out, grad_head, over], 0)
+    sums = jnp.pad(jnp.concatenate([grad_out, grad_head], 0), ((0, OUTCOMES), (0, 0)))
     sums = tree_sum(sums, "rep", 4, (1, 2, 3))
     sums = tree_sum(sums, "sample", PEERS, (2, 4, 6))
     sums = tree_sum(sums, "sample", PEERS, (1,))
-    share = sums.shape[0] // SIDE
-    piece = lax.dynamic_slice_in_dim(sums, (y * 2 + core) * share, share, 0)
-    piece = jnp.concatenate([piece, sums[-1:]], 0)
-    piece = tree_sum(piece, "sample", PEERS, [SIDE * k for k in range(1, PLANES)])
+    share = sums.shape[0] // 4
+    piece = lax.dynamic_slice_in_dim(sums, y * share, share, 0)
 
     rows = jnp.arange(ROWS, dtype=jnp.int32)
     same = (target[:, None] == target[None, :]) & (rows[:, None] < rows[None, :])
@@ -349,7 +363,7 @@
     packed, piece = lax.optimization_barrier((pack_direct(0, target, cache, tiles), piece))
     direct = exchanged(packed)
 
-    codes = relayed[:, RELAY * LEVELS, :RELAY].astype(jnp.int32)
+    codes = relayed[:, RELAY * LEVELS, : 2 * RELAY].astype(jnp.int32)
     shifts = [(dy, dc) for dy in range(4) for dc in range(2)]
     onto = jnp.stack([lax.rem(y + dy, 4) * 2 + (core ^ dc) for dy, dc in shifts])
     came = jnp.stack([lax.rem(y - dy + 4, 4) * 2 + (core ^ dc) for dy, dc in shifts])
@@ -360,9 +374,14 @@
         out_specs=[ANY] * SIDE,
         scratch_shapes=[
             pltpu.SMEM((SIDE * 2 * PLANES,), jnp.int32),
+            pltpu.VMEM((PLANES, PIECE, WIDTH), jnp.bfloat16),
             pltpu.VMEM((LEVELS, WIDTH), jnp.bfloat16),
+            pltpu.VMEM((8, WIDTH), jnp.bfloat16),
             pltpu.SemaphoreType.DMA((SIDE,)),
+            pltpu.SemaphoreType.DMA((SIDE,)),
+            pltpu.SemaphoreType.DMA,
         ],
+        cost_estimate=pl.CostEstimate(flops=0, bytes_accessed=5 << 20, transcendentals=0),
         name="pack_plane",
     )(codes, onto.astype(jnp.int32), relayed)
     def in_plane(x, k):
@@ -378,25 +397,34 @@
     lasts = [onward[0]] + [in_plane(onward[k], k) for k in range(1, SIDE)]
     piece, lasts = lax.optimization_barrier((piece, lasts))
     came = came.astype(jnp.int32)
-    shares = jnp.stack([piece[:share]] + [in_plane(piece[:share], k) for k in range(1, SIDE)])
-    peers = jnp.arange(SIDE, dtype=jnp.int32)
-    order = lax.rem(y - lax.div(peers, 2) + 4, 4) * 2 + (core ^ lax.rem(peers, 2))
-    ours = (order[:, None] == peers[None, :])[..., None, None]
-    grads = jnp.sum(jnp.where(ours, shares[None], 0.0), 1).reshape(sums.shape)
-
-    def by_relay(direct, lasts):
-        return settle(came, direct, lasts)
-
-    def by_pairs(direct, lasts):
+    piece = tree_sum(piece, "sample", PEERS, [SIDE * k for k in range(1, PLANES)])
+    over = pl.pallas_call(
+        flag_kernel,
+        grid=(1,),
+        out_shape=jax.ShapeDtypeStruct((1,), jnp.int32),
+        in_specs=[pl.BlockSpec((8, 128), lambda t: (LAST // 8 - 1, 0))] * SIDE,
+        out_specs=SMEM,
+        name="flag",
+    )(*lasts)
+
+    def by_relay(lasts):
+        return lasts
+
+    def by_pairs(lasts):
         high = exchanged(pack_direct(2, target, cache, jnp.zeros_like(tiles)))
         high = high[:, : 2 * LEVELS].reshape(PLANES, SIDE, 2 * LEVELS, WIDTH)
         high = jnp.swapaxes(high, 0, 1).reshape(SIDE, 2 * PLANES * LEVELS, WIDTH)
-        high = [
-            lax.dynamic_index_in_dim(high, came[k], 0, keepdims=False) for k in range(SIDE)
-        ]
-        return settle(came, direct, high)
-
-    new_cache, log_probs = lax.cond(piece[share, 0] > 0, by_pairs, by_relay, direct, lasts)
+        high = jnp.pad(high, ((0, 0), (0, LAST - 2 * PLANES * LEVELS), (0, 0)))
+        return [lax.dynamic_index_in_dim(high, came[k], 0, keepdims=False) for k in range(SIDE)]
+
+    direct, lasts, piece = lax.optimization_barrier((direct, lasts, piece))
+    lasts = lax.cond(over[0] > 0, by_pairs, by_relay, lasts)
+    piece, lasts = lax.optimization_barrier((piece, lasts))
+    shares = jnp.stack([piece] + [in_plane(piece, k) for k in range(2, SIDE, 2)])
+    rows_y = jnp.arange(4, dtype=jnp.int32)
+    ours = (lax.rem(y - rows_y + 4, 4)[:, None] == rows_y[None, :])[..., None, None]
+    grads = jnp.sum(jnp.where(ours, shares[None], 0.0), 1).reshape(sums.shape)
+    new_cache, log_probs = settle(came, direct, lasts)
     return (
         jnp.swapaxes(new_cache, 0, 1),
         log_probs[:, :OUTCOMES],

time: 199 us -> 182 us (0.915)
  the two profiles are of different devices: /device:TPU:96 before, /device:TPU:1 now
where the time goes in v3:
time: 182 us; the launch traced here: 179 us
  waiting for transfers between devices  65.6 us (36%)
  starting transfers between devices  55.2 us (30%)
  Pallas kernels  29.5 us (16%)
  local copies, waits for them, and re-layouts  14.8 us (8%)
  other arithmetic  10.1 us (6%)
  matrix products  1.83 us (1%)
  between operations  1.82 us (1%)
    ppermute x10, waiting for transfers between devices, in_plane(): return lax.ppermute(x, 'sample', pairs)  59.6 us
    ppermute x14, starting transfers between devices, tree_sum(): terms = [x] + [lax.ppermute(x, axis, xor_pairs(size, bit)) for bit in bits]  22.8 us
    all_to_all x2, starting transfers between devices, exchanged(): lax.all_to_all(x, 'sample', split_axis=0, concat_axis=0, tiled=True, axis...  18.5 us
    ppermute x10, starting transfers between devices, in_plane(): return lax.ppermute(x, 'sample', pairs)  13.9 us
    pallas_call x1, Pallas kernels, pack_direct(): pl.pallas_call(functools.partial(direct_kernel, low), out_shape=jax.Shape...  10 us
    unnamed x30, local copies, waits for them, and re-layouts  8.6 us
    pallas_call x1, Pallas kernels, settle(): pl.pallas_call(settle_kernel, grid=(PLANES,), out_shape=(jax.ShapeDtypeSt...  8.36 us
    ppermute x14, waiting for transfers between devices, tree_sum(): terms = [x] + [lax.ppermute(x, axis, xor_pairs(size, bit)) for bit in bits]  6.02 us
  transfers between devices with their start and end apart: 26, of which 8 were waited for; matrix products, arithmetic and copies ran while one was open for 13% of the time, Pallas kernels for 13%

profile of v3, /device:TPU:1, one launch (start us, length us, event | category | flops | bytes accessed | tf_op | source)
XLA Modules:
  0.0 178.8 jit_solution(14281719046165085497)
XLA Ops:
  0.7 5.4 %pack_relay.1 = bf16[8,392,256]{2,1,0:T(8,128)(2,1)} custom-call(s32[128]{0:T(128)} %bitcast.82, bf16[128,48,256]{2,1,0:T(8,128)(2,1)} %cache.3), custom_call_target="tpu_custom_call" | custom-call | tf_op jit(solution)/shard_map/pack_relay/pallas_call | solution.py:324
  6.1 9.1 %all-to-all-start.2 = ((bf16[8,392,256]{2,1,0:T(8,128)(2,1)}), bf16[8,392,256]{2,1,0:T(8,128)(2,1)}, u32[]{:S(2)}, u32[]{:S(2)}) async-start(bf16[8,392,256]{2,1,0:T(8,128)(2,1)} %pack_relay.1), calls=%async_computation.2 | async-start | bytes 3211264 | tf_op jit(solution)/shard_map/all_to_all | solution.py:294
  15.3 2.2 %fusion.37 = (bf16[128,48,128]{2,1,0:T(8,128)(2,1)}, bf16[128,48,128]{2,1,0:T(8,128)(2,1)}) fusion(bf16[128,48,256]{2,1,0:T(8,128)(2,1)S(1)} %copy-done.2), kind=kLoop, calls=%fused_computation.85 | loop fusion | bytes 6291456 | tf_op jit(solution)/shard_map/slice | solution.py:42
  17.6 0.2 convolution_convert_fusion.2
  17.9 0.2 convolution_convert_fusion.1
  18.1 2.9 %copy.52 = bf16[128,48,128]{0,2,1:T(8,128)(2,1)} copy(bf16[128,48,128]{2,1,0:T(8,128)(2,1)} %get-tuple-element.167) | data formatting | bytes 3145728
  21.0 0.2 bitcast_convert_fusion
  21.3 2.8 %copy.51 = bf16[128,48,128]{0,2,1:T(8,128)(2,1)} copy(bf16[128,48,128]{2,1,0:T(8,128)(2,1)} %get-tuple-element.166) | data formatting | bytes 3145728
  24.1 2.0 %multiply_reduce_fusion.1 = f32[128,4,48]{0,1,2:T(4,128)S(1)} fusion(f32[128,4,32]{0,2,1:T(8,128)S(1)} %get-tuple-element.173, bf16[128,48,128]{0,2,1:T(8,128)(2,1)} %copy.51), kind=kLoop, calls=%fused_computation.17 | loop fusion | flops 2334720 | bytes 1736704
  26.3 1.8 multiply_reduce_fusion
  28.1 0.2 fusion.9
  28.3 0.1 fusion.38
  28.7 0.3 fusion.26
  29.0 0.2 fusion.39
  29.2 2.7 %collective-permute-start.1 = (f32[136,128]{1,0:T(8,128)S(1)}, f32[136,128]{1,0:T(8,128)S(1)}, u32[]{:S(2)}, u32[]{:S(2)}) collective-permute-start(f32[136,128]{1,0:T(8,128)S(1)} %select_maximum_fusion), channel_id=1, source_target_pairs={{0,2},{1,3},{2,0},{3,1},{4,6},{5,7},{6,4},{7,5},{8,10},{9,11},{10,... | collective-permute-start | bytes 208904 | tf_op jit(solution)/shard_map/ppermute | solution.py:304
  31.8 0.9 collective-permute-start.2
  33.0 1.2 collective-permute-done.1
  34.2 2.5 %collective-permute-done.2 = f32[136,128]{1,0:T(8,128)} collective-permute-done((f32[136,128]{1,0:T(8,128)S(1)}, f32[136,128]{1,0:T(8,128)}, u32[]{:S(2)}, u32[]{:S(2)}) %collective-permute-start.2) | collective-permute-done | bytes 69664 | tf_op jit(solution)/shard_map/ppermute | solution.py:304
  36.6 0.9 add_add_fusion.1
  37.5 3.2 %collective-permute-start.4 = (f32[136,128]{1,0:T(8,128)S(1)}, f32[136,128]{1,0:T(8,128)}, u32[]{:S(2)}, u32[]{:S(2)}) collective-permute-start(f32[136,128]{1,0:T(8,128)S(1)} %add_add_fusion.1), channel_id=1, source_target_pairs={{0,16},{4,20},{8,24},{12,28},{16,0},{20,4},{24,8},{28,12},{32,48},... | collective-permute-start | bytes 208904 | tf_op jit(solution)/shard_map/ppermute | solution.py:304
  40.7 0.8 collective-permute-start.5
  41.5 0.2 convolution_convert_fusion
  41.7 0.7 slice.36
  42.4 0.1 copy.33
  42.6 1.0 copy.32
  43.7 2.4 %collective-permute-done.5 = f32[136,128]{1,0:T(8,128)} collective-permute-done((f32[136,128]{1,0:T(8,128)S(1)}, f32[136,128]{1,0:T(8,128)}, u32[]{:S(2)}, u32[]{:S(2)}) %collective-permute-start.5) | collective-permute-done | bytes 69664 | tf_op jit(solution)/shard_map/ppermute | solution.py:304
  46.1 1.0 add_add_fusion
  47.0 2.7 %collective-permute-start.6 = (f32[136,128]{1,0:T(8,128)S(1)}, f32[136,128]{1,0:T(8,128)}, u32[]{:S(2)}, u32[]{:S(2)}) collective-permute-start(f32[136,128]{1,0:T(8,128)S(1)} %add_add_fusion), channel_id=1, source_target_pairs={{0,4},{4,0},{8,12},{12,8},{16,20},{20,16},{24,28},{28,24},{32,36},... | collective-permute-start | bytes 208904 | tf_op jit(solution)/shard_map/ppermute | solution.py:304
  49.7 0.8 fusion.11.tiles
  50.5 10.0 %pack_direct.3 = bf16[64,104,256]{2,1,0:T(8,128)(2,1)} custom-call(s32[128]{0:T(128)S(1)} %bitcast.84, bf16[128,48,256]{2,1,0:T(8,128)(2,1)S(1)} %copy-done.2, bf16[64,8,256]{2,1,0:T(8,128)(2,1)} %fusion.11.tiles), custom_call_target="tpu_custom_call" | custom-call | bytes 10485760 | tf_op jit(solution)/shard_map/pack_direct/pallas_call | solution.py:277
  60.5 0.8 dynamic-slice_add_fusion
  61.3 9.3 %all-to-all-start.1 = ((bf16[64,104,256]{2,1,0:T(8,128)(2,1)}), bf16[64,104,256]{2,1,0:T(8,128)(2,1)S(1)}, u32[]{:S(2)}, u32[]{:S(2)}) async-start(bf16[64,104,256]{2,1,0:T(8,128)(2,1)} %pack_direct.3), calls=%async_computation.1 | async-start | bytes 6815744 | tf_op jit(solution)/shard_map/all_to_all | solution.py:294
  70.7 0.6 stack.68.side
  71.3 1.3 slice_convert_fusion
  72.6 4.3 %pack_plane.1 = (bf16[776,256]{1,0:T(8,128)(2,1)}, bf16[776,256]{1,0:T(8,128)(2,1)}, bf16[776,256]{1,0:T(8,128)(2,1)}, bf16[776,256]{1,0:T(8,128)(2,1)}, bf16[77...) custom-call(s32[8,16]{1,0:T(8,128)} %bitcast.81, ...), custom_call_target="tpu_custom_call" | custom-call | bytes 5242880 | tf_op jit(solution)/shard_map/pack_plane/pallas_call | solution.py:370
  76.9 0.5 collective-permute-start.7
  77.5 1.3 collective-permute-start.8
  78.8 1.5 collective-permute-start.9
  80.3 1.3 collective-permute-start.10
  81.6 1.9 %collective-permute-start.11 = (bf16[776,256]{1,0:T(8,128)(2,1)}, bf16[776,256]{1,0:T(8,128)(2,1)}, u32[]{:S(2)}, u32[]{:S(2)}) collective-permute-start(bf16[776,256]{1,0:T(8,128)(2,1)} %get-tuple-element.105), channel_id=1, source_target_pairs={{0,20},{4,16},{8,28},{12,24},{16,4},{20,0},{24,12},{28,8},{32,52},... | collective-permute-start | bytes 1191944 | tf_op jit(solution)/shard_map/ppermute | solution.py:395
  83.5 1.5 collective-permute-start.12
  85.0 9.7 %collective-permute-done.8.refs_2_ = bf16[776,256]{1,0:T(8,128)(2,1)} collective-permute-done((bf16[776,256]{1,0:T(8,128)(2,1)}, bf16[776,256]{1,0:T(8,128)(2,1)}, u32[]{:S(2)}, u32[]{:S(2)}) %collective-permute-start.8) | collective-permute-done | bytes 397344 | tf_op jit(solution)/shard_map/ppermute | solution.py:395
  94.7 3.8 %collective-permute-start.13 = (bf16[776,256]{1,0:T(8,128)(2,1)}, bf16[776,256]{1,0:T(8,128)(2,1)}, u32[]{:S(2)}, u32[]{:S(2)}) collective-permute-start(bf16[776,256]{1,0:T(8,128)(2,1)} %get-tuple-element.107), channel_id=1, source_target_pairs={{0,28},{4,24},{8,4},{12,0},{16,12},{20,8},{24,20},{28,16},{32,60},... | collective-permute-start | bytes 1191944 | tf_op jit(solution)/shard_map/ppermute | solution.py:395
  98.5 13.0 %collective-permute-done.9.refs_3_ = bf16[776,256]{1,0:T(8,128)(2,1)} collective-permute-done((bf16[776,256]{1,0:T(8,128)(2,1)}, bf16[776,256]{1,0:T(8,128)(2,1)}, u32[]{:S(2)}, u32[]{:S(2)}) %collective-permute-start.9) | collective-permute-done | bytes 397344 | tf_op jit(solution)/shard_map/ppermute | solution.py:395
  111.5 17.9 %collective-permute-done.10.refs_4_ = bf16[776,256]{1,0:T(8,128)(2,1)} collective-permute-done((bf16[776,256]{1,0:T(8,128)(2,1)}, bf16[776,256]{1,0:T(8,128)(2,1)}, u32[]{:S(2)}, u32[]{:S(2)}) %collective-permute-start.10) | collective-permute-done | bytes 397344 | tf_op jit(solution)/shard_map/ppermute | solution.py:395
  129.4 18.2 %collective-permute-done.11.refs_5_ = bf16[776,256]{1,0:T(8,128)(2,1)} collective-permute-done((bf16[776,256]{1,0:T(8,128)(2,1)}, bf16[776,256]{1,0:T(8,128)(2,1)}, u32[]{:S(2)}, u32[]{:S(2)}) %collective-permute-start.11) | collective-permute-done | bytes 397344 | tf_op jit(solution)/shard_map/ppermute | solution.py:395
  147.6 0.8 collective-permute-done.13.refs_7_
  148.4 3.2 %collective-permute-start.19 = (f32[34,128]{1,0:T(8,128)S(1)}, f32[34,128]{1,0:T(8,128)S(1)}, u32[]{:S(2)}, u32[]{:S(2)}) collective-permute-start(f32[34,128]{1,0:T(8,128)S(1)} %dynamic-slice_add_fusion), channel_id=1, source_target_pairs={{0,192},{4,196},{8,200},{12,204},{16,208},{20,212},{24,216},{28,22... | collective-permute-start | bytes 52232 | tf_op jit(solution)/shard_map/ppermute | solution.py:304
  151.6 0.7 collective-permute-start.20
  152.3 2.8 %collective-permute-start.17 = (f32[34,128]{1,0:T(8,128)S(1)}, f32[34,128]{1,0:T(8,128)S(1)}, u32[]{:S(2)}, u32[]{:S(2)}) collective-permute-start(f32[34,128]{1,0:T(8,128)S(1)} %dynamic-slice_add_fusion), channel_id=1, source_target_pairs={{0,128},{4,132},{8,136},{12,140},{16,144},{20,148},{24,152},{28,15... | collective-permute-start | bytes 52232 | tf_op jit(solution)/shard_map/ppermute | solution.py:304
  155.1 2.2 %collective-permute-start.18 = (f32[34,128]{1,0:T(8,128)S(1)}, f32[34,128]{1,0:T(8,128)S(1)}, u32[]{:S(2)}, u32[]{:S(2)}) collective-permute-start(f32[34,128]{1,0:T(8,128)S(1)} %dynamic-slice_add_fusion), channel_id=1, source_target_pairs={{0,160},{4,164},{8,168},{12,172},{16,176},{20,180},{24,184},{28,18... | collective-permute-start | bytes 52232 | tf_op jit(solution)/shard_map/ppermute | solution.py:304
  157.3 3.3 %collective-permute-start.16 = (f32[34,128]{1,0:T(8,128)S(1)}, f32[34,128]{1,0:T(8,128)}, u32[]{:S(2)}, u32[]{:S(2)}) collective-permute-start(f32[34,128]{1,0:T(8,128)S(1)} %dynamic-slice_add_fusion), channel_id=1, source_target_pairs={{0,96},{4,100},{8,104},{12,108},{16,112},{20,116},{24,120},{28,124... | collective-permute-start | bytes 52232 | tf_op jit(solution)/shard_map/ppermute | solution.py:304
  160.6 0.4 collective-permute-start.14
  161.2 1.4 flag.1
  163.2 0.6 copy-done.7
  163.8 0.8 add_add_fusion.2
  164.7 1.2 collective-permute-start.22
  165.9 0.8 collective-permute-start.21
  166.7 8.4 %settle.1 = (bf16[49,256,256]{2,1,0:T(8,128)(2,1)}, f32[256,128]{1,0:T(8,128)S(1)}) custom-call(s32[8]{0:T(128)S(1)} %stack.65.side, bf16[64,104,256]{2,1,0:T(8,128)(2,1)S(1)} %all-to-all-done.1.direct, bf16[776,256]{1,0:T(8,128)(2,1)} %get-tuple-element.135.refs_0_, bf16[776,256]{1,0:T(8,128)(2,1)} %get-tuple-element.136.refs_1_, ...), custom_call_target="tpu_custom_call" | custom-call | flops 2147483648 | bytes 14680064 | tf_op jit(solution)/shard_map/settle/pallas_call | solution.py:256
  175.1 0.6 copy-done.1
  175.7 1.6 copy.36
  177.3 0.2 select_reduce_fusion
  177.6 0.6 slice.39
  178.2 0.6 slice_bitcast_fusion
  (74 shorter events, 1.3 us)
Async XLA Ops:
  0.6 20.3 %copy-start = (bf16[128,128]{1,0:T(8,128)(2,1)S(1)}, bf16[128,128]{1,0:T(8,128)(2,1)}, u32[]{:S(2)}) copy-start(bf16[128,128]{1,0:T(8,128)(2,1)} %param.16) | copy-start | bytes 98308
  0.6 14.6 %copy-start.2 = (bf16[128,48,256]{2,1,0:T(8,128)(2,1)S(1)}, bf16[128,48,256]{2,1,0:T(8,128)(2,1)}, u32[]{:S(2)}) copy-start(bf16[128,48,256]{2,1,0:T(8,128)(2,1)} %cache.3) | copy-start | bytes 9437188
  6.1 55.2 %all-to-all-start.2 = ((bf16[8,392,256]{2,1,0:T(8,128)(2,1)}), bf16[8,392,256]{2,1,0:T(8,128)(2,1)}, u32[]{:S(2)}, u32[]{:S(2)}) async-start(bf16[8,392,256]{2,1,0:T(8,128)(2,1)} %pack_relay.1), calls=%async_computation.2 | async-start | bytes 3211264 | tf_op jit(solution)/shard_map/all_to_all | solution.py:294
  15.2 2.3 %copy-start.3 = (bf16[128,128]{1,0:T(8,128)(2,1)S(1)}, bf16[128,128]{1,0:T(8,128)(2,1)}, u32[]{:S(2)}) copy-start(bf16[128,128]{1,0:T(8,128)(2,1)} %param.13) | copy-start | bytes 98308
  15.2 2.4 %copy-start.4 = (bf16[128,128]{1,0:T(8,128)(2,1)S(1)}, bf16[128,128]{1,0:T(8,128)(2,1)}, u32[]{:S(2)}) copy-start(bf16[128,128]{1,0:T(8,128)(2,1)} %param.17) | copy-start | bytes 98308
  15.2 2.4 %copy-start.8 = (f32[128]{0:T(128)S(1)}, f32[128]{0:T(128)}, u32[]{:S(2)}) copy-start(f32[128]{0:T(128)} %param.15) | copy-start | bytes 1540
  15.2 2.6 %copy-start.5 = (bf16[128,128]{1,0:T(8,128)(2,1)S(1)}, bf16[128,128]{1,0:T(8,128)(2,1)}, u32[]{:S(2)}) copy-start(bf16[128,128]{1,0:T(8,128)(2,1)} %param.18) | copy-start | bytes 98308
  21.2 6.9 %copy-start.6 = (bf16[128,128]{1,0:T(8,128)(2,1)S(1)}, bf16[128,128]{1,0:T(8,128)(2,1)}, u32[]{:S(2)}) copy-start(bf16[128,128]{1,0:T(8,128)(2,1)} %param.19) | copy-start | bytes 98308
  21.2 7.1 %copy-start.10 = (bf16[128,4]{0,1:T(4,128)(2,1)S(1)}, bf16[128,4]{0,1:T(4,128)(2,1)}, u32[]{:S(2)}) copy-start(bf16[128,4]{0,1:T(4,128)(2,1)} %param.20) | copy-start | bytes 3076
  21.2 7.3 %copy-start.11 = (s32[128]{0:T(128)S(1)}, s32[128]{0:T(128)}, u32[]{:S(2)}) copy-start(s32[128]{0:T(128)} %param.22) | copy-start | bytes 1540
  21.3 7.3 %copy-start.12 = (f32[128]{0:T(128)S(1)}, f32[128]{0:T(128)}, u32[]{:S(2)}) copy-start(f32[128]{0:T(128)} %param.21) | copy-start | bytes 1540
  24.1 8.7 %copy-start.9 = (s32[128,1]{0,1:T(1,128)S(1)}, s32[128,1]{0,1:T(1,128)}, u32[]{:S(2)}) copy-start(s32[128,1]{0,1:T(1,128)} %param.23) | copy-start | bytes 1540
  29.2 5.0 %collective-permute-start.1 = (f32[136,128]{1,0:T(8,128)S(1)}, f32[136,128]{1,0:T(8,128)S(1)}, u32[]{:S(2)}, u32[]{:S(2)}) collective-permute-start(f32[136,128]{1,0:T(8,128)S(1)} %select_maximum_fusion), channel_id=1, source_target_pairs={{0,2},{1,3},{2,0},{3,1},{4,6},{5,7},{6,4},{7,5},{8,10},{9,11},{10,... | collective-permute-start | bytes 208904 | tf_op jit(solution)/shard_map/ppermute | solution.py:304
  31.8 4.8 %collective-permute-start.2 = (f32[136,128]{1,0:T(8,128)S(1)}, f32[136,128]{1,0:T(8,128)}, u32[]{:S(2)}, u32[]{:S(2)}) collective-permute-start(f32[136,128]{1,0:T(8,128)S(1)} %select_maximum_fusion), channel_id=1, source_target_pairs={{0,3},{1,2},{2,1},{3,0},{4,7},{5,6},{6,5},{7,4},{8,11},{9,10},{10,... | collective-permute-start | bytes 208904 | tf_op jit(solution)/shard_map/ppermute | solution.py:304
  32.8 3.8 %collective-permute-start = (f32[136,128]{1,0:T(8,128)S(1)}, f32[136,128]{1,0:T(8,128)}, u32[]{:S(2)}, u32[]{:S(2)}) collective-permute-start(f32[136,128]{1,0:T(8,128)S(1)} %select_maximum_fusion), channel_id=1, source_target_pairs={{0,1},{1,0},{2,3},{3,2},{4,5},{5,4},{6,7},{7,6},{8,9},{9,8},{10,11... | collective-permute-start | bytes 208904 | tf_op jit(solution)/shard_map/ppermute | solution.py:304
  37.5 6.1 %collective-permute-start.4 = (f32[136,128]{1,0:T(8,128)S(1)}, f32[136,128]{1,0:T(8,128)}, u32[]{:S(2)}, u32[]{:S(2)}) collective-permute-start(f32[136,128]{1,0:T(8,128)S(1)} %add_add_fusion.1), channel_id=1, source_target_pairs={{0,16},{4,20},{8,24},{12,28},{16,0},{20,4},{24,8},{28,12},{32,48},... | collective-permute-start | bytes 208904 | tf_op jit(solution)/shard_map/ppermute | solution.py:304
  40.7 5.3 %collective-permute-start.5 = (f32[136,128]{1,0:T(8,128)S(1)}, f32[136,128]{1,0:T(8,128)}, u32[]{:S(2)}, u32[]{:S(2)}) collective-permute-start(f32[136,128]{1,0:T(8,128)S(1)} %add_add_fusion.1), channel_id=1, source_target_pairs={{0,24},{4,28},{8,16},{12,20},{16,8},{20,12},{24,0},{28,4},{32,56},... | collective-permute-start | bytes 208904 | tf_op jit(solution)/shard_map/ppermute | solution.py:304
  41.5 4.6 %collective-permute-start.3 = (f32[136,128]{1,0:T(8,128)S(1)}, f32[136,128]{1,0:T(8,128)}, u32[]{:S(2)}, u32[]{:S(2)}) collective-permute-start(f32[136,128]{1,0:T(8,128)S(1)} %add_add_fusion.1), channel_id=1, source_target_pairs={{0,8},{4,12},{8,0},{12,4},{16,24},{20,28},{24,16},{28,20},{32,40},... | collective-permute-start | bytes 208904 | tf_op jit(solution)/shard_map/ppermute | solution.py:304
  47.0 13.5 %collective-permute-start.6 = (f32[136,128]{1,0:T(8,128)S(1)}, f32[136,128]{1,0:T(8,128)}, u32[]{:S(2)}, u32[]{:S(2)}) collective-permute-start(f32[136,128]{1,0:T(8,128)S(1)} %add_add_fusion), channel_id=1, source_target_pairs={{0,4},{4,0},{8,12},{12,8},{16,20},{20,16},{24,28},{28,24},{32,36},... | collective-permute-start | bytes 208904 | tf_op jit(solution)/shard_map/ppermute | solution.py:304
  61.3 103.3 %all-to-all-start.1 = ((bf16[64,104,256]{2,1,0:T(8,128)(2,1)}), bf16[64,104,256]{2,1,0:T(8,128)(2,1)S(1)}, u32[]{:S(2)}, u32[]{:S(2)}) async-start(bf16[64,104,256]{2,1,0:T(8,128)(2,1)} %pack_direct.3), calls=%async_computation.1 | async-start | bytes 6815744 | tf_op jit(solution)/shard_map/all_to_all | solution.py:294
  76.9 6.6 %collective-permute-start.7 = (bf16[776,256]{1,0:T(8,128)(2,1)}, bf16[776,256]{1,0:T(8,128)(2,1)}, u32[]{:S(2)}, u32[]{:S(2)}) collective-permute-start(bf16[776,256]{1,0:T(8,128)(2,1)} %get-tuple-element.101), channel_id=1, source_target_pairs={{0,4},{4,0},{8,12},{12,8},{16,20},{20,16},{24,28},{28,24},{32,36},... | collective-permute-start | bytes 1191944 | tf_op jit(solution)/shard_map/ppermute | solution.py:395
  77.5 17.2 %collective-permute-start.8 = (bf16[776,256]{1,0:T(8,128)(2,1)}, bf16[776,256]{1,0:T(8,128)(2,1)}, u32[]{:S(2)}, u32[]{:S(2)}) collective-permute-start(bf16[776,256]{1,0:T(8,128)(2,1)} %get-tuple-element.102), channel_id=1, source_target_pairs={{0,8},{4,12},{8,16},{12,20},{16,24},{20,28},{24,0},{28,4},{32,40},... | collective-permute-start | bytes 1191944 | tf_op jit(solution)/shard_map/ppermute | solution.py:395
  78.8 32.7 %collective-permute-start.9 = (bf16[776,256]{1,0:T(8,128)(2,1)}, bf16[776,256]{1,0:T(8,128)(2,1)}, u32[]{:S(2)}, u32[]{:S(2)}) collective-permute-start(bf16[776,256]{1,0:T(8,128)(2,1)} %get-tuple-element.103), channel_id=1, source_target_pairs={{0,12},{4,8},{8,20},{12,16},{16,28},{20,24},{24,4},{28,0},{32,44},... | collective-permute-start | bytes 1191944 | tf_op jit(solution)/shard_map/ppermute | solution.py:395
  80.3 49.1 %collective-permute-start.10 = (bf16[776,256]{1,0:T(8,128)(2,1)}, bf16[776,256]{1,0:T(8,128)(2,1)}, u32[]{:S(2)}, u32[]{:S(2)}) collective-permute-start(bf16[776,256]{1,0:T(8,128)(2,1)} %get-tuple-element.104), channel_id=1, source_target_pairs={{0,16},{4,20},{8,24},{12,28},{16,0},{20,4},{24,8},{28,12},{32,48},... | collective-permute-start | bytes 1191944 | tf_op jit(solution)/shard_map/ppermute | solution.py:395
  81.6 66.0 %collective-permute-start.11 = (bf16[776,256]{1,0:T(8,128)(2,1)}, bf16[776,256]{1,0:T(8,128)(2,1)}, u32[]{:S(2)}, u32[]{:S(2)}) collective-permute-start(bf16[776,256]{1,0:T(8,128)(2,1)} %get-tuple-element.105), channel_id=1, source_target_pairs={{0,20},{4,16},{8,28},{12,24},{16,4},{20,0},{24,12},{28,8},{32,52},... | collective-permute-start | bytes 1191944 | tf_op jit(solution)/shard_map/ppermute | solution.py:395
  83.5 64.1 %collective-permute-start.12 = (bf16[776,256]{1,0:T(8,128)(2,1)}, bf16[776,256]{1,0:T(8,128)(2,1)}, u32[]{:S(2)}, u32[]{:S(2)}) collective-permute-start(bf16[776,256]{1,0:T(8,128)(2,1)} %get-tuple-element.106), channel_id=1, source_target_pairs={{0,24},{4,28},{8,0},{12,4},{16,8},{20,12},{24,16},{28,20},{32,56},... | collective-permute-start | bytes 1191944 | tf_op jit(solution)/shard_map/ppermute | solution.py:395
  94.7 53.7 %collective-permute-start.13 = (bf16[776,256]{1,0:T(8,128)(2,1)}, bf16[776,256]{1,0:T(8,128)(2,1)}, u32[]{:S(2)}, u32[]{:S(2)}) collective-permute-start(bf16[776,256]{1,0:T(8,128)(2,1)} %get-tuple-element.107), channel_id=1, source_target_pairs={{0,28},{4,24},{8,4},{12,0},{16,12},{20,8},{24,20},{28,16},{32,60},... | collective-permute-start | bytes 1191944 | tf_op jit(solution)/shard_map/ppermute | solution.py:395
  148.4 9.0 %collective-permute-start.19 = (f32[34,128]{1,0:T(8,128)S(1)}, f32[34,128]{1,0:T(8,128)S(1)}, u32[]{:S(2)}, u32[]{:S(2)}) collective-permute-start(f32[34,128]{1,0:T(8,128)S(1)} %dynamic-slice_add_fusion), channel_id=1, source_target_pairs={{0,192},{4,196},{8,200},{12,204},{16,208},{20,212},{24,216},{28,22... | collective-permute-start | bytes 52232 | tf_op jit(solution)/shard_map/ppermute | solution.py:304
  151.6 9.0 %collective-permute-start.20 = (f32[34,128]{1,0:T(8,128)S(1)}, f32[34,128]{1,0:T(8,128)S(1)}, u32[]{:S(2)}, u32[]{:S(2)}) collective-permute-start(f32[34,128]{1,0:T(8,128)S(1)} %dynamic-slice_add_fusion), channel_id=1, source_target_pairs={{0,224},{4,228},{8,232},{12,236},{16,240},{20,244},{24,248},{28,25... | collective-permute-start | bytes 52232 | tf_op jit(solution)/shard_map/ppermute | solution.py:304
  152.3 10.8 %collective-permute-start.17 = (f32[34,128]{1,0:T(8,128)S(1)}, f32[34,128]{1,0:T(8,128)S(1)}, u32[]{:S(2)}, u32[]{:S(2)}) collective-permute-start(f32[34,128]{1,0:T(8,128)S(1)} %dynamic-slice_add_fusion), channel_id=1, source_target_pairs={{0,128},{4,132},{8,136},{12,140},{16,144},{20,148},{24,152},{28,15... | collective-permute-start | bytes 52232 | tf_op jit(solution)/shard_map/ppermute | solution.py:304
  155.1 8.1 %collective-permute-start.18 = (f32[34,128]{1,0:T(8,128)S(1)}, f32[34,128]{1,0:T(8,128)S(1)}, u32[]{:S(2)}, u32[]{:S(2)}) collective-permute-start(f32[34,128]{1,0:T(8,128)S(1)} %dynamic-slice_add_fusion), channel_id=1, source_target_pairs={{0,160},{4,164},{8,168},{12,172},{16,176},{20,180},{24,184},{28,18... | collective-permute-start | bytes 52232 | tf_op jit(solution)/shard_map/ppermute | solution.py:304
  157.3 5.9 %collective-permute-start.15 = (f32[34,128]{1,0:T(8,128)S(1)}, f32[34,128]{1,0:T(8,128)}, u32[]{:S(2)}, u32[]{:S(2)}) collective-permute-start(f32[34,128]{1,0:T(8,128)S(1)} %dynamic-slice_add_fusion), channel_id=1, source_target_pairs={{0,64},{4,68},{8,72},{12,76},{16,80},{20,84},{24,88},{28,92},{32,9... | collective-permute-start | bytes 52232 | tf_op jit(solution)/shard_map/ppermute | solution.py:304
  157.3 5.9 %collective-permute-start.16 = (f32[34,128]{1,0:T(8,128)S(1)}, f32[34,128]{1,0:T(8,128)}, u32[]{:S(2)}, u32[]{:S(2)}) collective-permute-start(f32[34,128]{1,0:T(8,128)S(1)} %dynamic-slice_add_fusion), channel_id=1, source_target_pairs={{0,96},{4,100},{8,104},{12,108},{16,112},{20,116},{24,120},{28,124... | collective-permute-start | bytes 52232 | tf_op jit(solution)/shard_map/ppermute | solution.py:304
  160.6 3.2 %collective-permute-start.14 = (f32[34,128]{1,0:T(8,128)S(1)}, f32[34,128]{1,0:T(8,128)}, u32[]{:S(2)}, u32[]{:S(2)}) collective-permute-start(f32[34,128]{1,0:T(8,128)S(1)} %dynamic-slice_add_fusion), channel_id=1, source_target_pairs={{0,32},{4,36},{8,40},{12,44},{16,48},{20,52},{24,56},{28,60},{32,0... | collective-permute-start | bytes 52232 | tf_op jit(solution)/shard_map/ppermute | solution.py:304
  163.2 0.6 copy-start.7
  164.6 12.7 %collective-permute-start.23 = (f32[34,128]{1,0:T(8,128)S(1)}, f32[34,128]{1,0:T(8,128)S(1)}, u32[]{:S(2)}, u32[]{:S(2)}) collective-permute-start(f32[34,128]{1,0:T(8,128)S(1)} %add_add_fusion.2), channel_id=1, source_target_pairs={{0,24},{4,28},{8,0},{12,4},{16,8},{20,12},{24,16},{28,20},{32,56},... | collective-permute-start | bytes 52232 | tf_op jit(solution)/shard_map/ppermute | solution.py:395
  164.7 12.6 %collective-permute-start.22 = (f32[34,128]{1,0:T(8,128)S(1)}, f32[34,128]{1,0:T(8,128)S(1)}, u32[]{:S(2)}, u32[]{:S(2)}) collective-permute-start(f32[34,128]{1,0:T(8,128)S(1)} %add_add_fusion.2), channel_id=1, source_target_pairs={{0,16},{4,20},{8,24},{12,28},{16,0},{20,4},{24,8},{28,12},{32,48},... | collective-permute-start | bytes 52232 | tf_op jit(solution)/shard_map/ppermute | solution.py:395
  165.9 11.3 %collective-permute-start.21 = (f32[34,128]{1,0:T(8,128)S(1)}, f32[34,128]{1,0:T(8,128)S(1)}, u32[]{:S(2)}, u32[]{:S(2)}) collective-permute-start(f32[34,128]{1,0:T(8,128)S(1)} %add_add_fusion.2), channel_id=1, source_target_pairs={{0,8},{4,12},{8,16},{12,20},{16,24},{20,28},{24,0},{28,4},{32,40},... | collective-permute-start | bytes 52232 | tf_op jit(solution)/shard_map/ppermute | solution.py:395
  175.1 0.6 copy-start.1

commit v4 on v3

--- a/solution.py
+++ b/solution.py
@@ -10,6 +10,7 @@
 
 HEADS = 4
 OUTCOMES = 4
+HEAD = 64
 ROWS = 128
 LEVELS = 48
 WIDTH = 256
@@ -128,11 +129,9 @@
     whole.wait()
 
 
-def direct_kernel(low, dest, cache, tiles, out, count, zero, rows_sem, tile_sem):
+def direct_kernel(low, dest, cache, out, count, zero, rows_sem):
     cleared(count, PEERS)
     zero[...] = jnp.zeros(zero.shape, zero.dtype)
-    last = pltpu.make_async_copy(tiles, out.at[:, pl.ds(2 * LEVELS, 8)], tile_sem)
-    last.start()
 
     @pl.loop(0, ROWS)
     def _(i):
@@ -155,7 +154,18 @@
 
     whole = out.at[:, pl.ds(0, 2 * LEVELS)]
     pltpu.make_async_copy(whole, whole, rows_sem).wait()
-    last.wait()
+
+
+def tile_kernel(tiles, rows, out, sem):
+    copy = pltpu.make_async_copy(tiles, out.at[:, pl.ds(2 * LEVELS, 8)], sem)
+    copy.start()
+    copy.wait()
+
+
+def plane_sum_kernel(tiles, out, head):
+    x = jnp.sum(tiles[...].astype(jnp.float32).reshape(PLANES, SIDE, 8, WIDTH), 0)
+    out[...] = x[:, 5, :] + (x[:, 6, :] + x[:, 7, :])
+    head[...] = x[:, 4, :]
 
 
 def forward_kernel(codes, side, got, *refs):
@@ -273,21 +283,20 @@
     )(side, direct, *lasts)
 
 
-def pack_direct(low, dest, cache, tiles):
+def pack_direct(low, dest, cache):
     return pl.pallas_call(
         functools.partial(direct_kernel, low),
         out_shape=jax.ShapeDtypeStruct((PEERS, DIRECT, WIDTH), jnp.bfloat16),
-        in_specs=[SMEM, ANY, ANY],
+        in_specs=[SMEM, ANY],
         out_specs=ANY,
         scratch_shapes=[
             pltpu.SMEM((PEERS,), jnp.int32),
             pltpu.VMEM((LEVELS, WIDTH), jnp.bfloat16),
             pltpu.SemaphoreType.DMA,
-            pltpu.SemaphoreType.DMA,
         ],
         cost_estimate=pl.CostEstimate(flops=0, bytes_accessed=10 << 20, transcendentals=0),
         name="pack_direct",
-    )(dest, cache, tiles)
+    )(dest, cache)
 
 
 def exchanged(x, groups=None):
@@ -341,13 +350,13 @@
     both, logp, grad_out, grad_head = decode_rows(
         tokens, cache, coef, chosen, gain, w_query, w_key, w_value, w_out, w_head
     )
-    sums = jnp.pad(jnp.concatenate([grad_out, grad_head], 0), ((0, OUTCOMES), (0, 0)))
+    sums = jnp.concatenate([grad_out, grad_head], 0)
+    target_now, sums = lax.optimization_barrier((target, sums))
+    packed = pack_direct(0, target_now, cache)
     sums = tree_sum(sums, "rep", 4, (1, 2, 3))
+    packed, sums = lax.optimization_barrier((packed, sums))
     sums = tree_sum(sums, "sample", PEERS, (2, 4, 6))
     sums = tree_sum(sums, "sample", PEERS, (1,))
-    share = sums.shape[0] // 4
-    piece = lax.dynamic_slice_in_dim(sums, y * share, share, 0)
-
     rows = jnp.arange(ROWS, dtype=jnp.int32)
     same = (target[:, None] == target[None, :]) & (rows[:, None] < rows[None, :])
     place = target * 4 + jnp.sum(same.astype(jnp.int32), 0)
@@ -355,12 +364,27 @@
     small = jnp.concatenate([both] + bf16_terms(logp), -1)
     slotted = jnp.dot(slot, small, preferred_element_type=jnp.float32).astype(jnp.bfloat16)
     new_rows = slotted[:, :WIDTH].reshape(PEERS, 4, WIDTH)
-    logp_row = jnp.pad(
-        slotted[:, WIDTH:].reshape(PEERS, 1, 4 * 3 * OUTCOMES),
-        ((0, 0), (0, 3), (0, WIDTH - 12 * OUTCOMES)),
-    )
-    tiles = jnp.concatenate([new_rows, logp_row], 1)
-    packed, piece = lax.optimization_barrier((pack_direct(0, target, cache, tiles), piece))
+    mine = y * 2 + core
+    share = sums[:ROWS].reshape(SIDE, SIDE, WIDTH)
+    share = lax.dynamic_index_in_dim(share, mine, 1, keepdims=False)
+    share = jnp.stack(bf16_terms(share), 1)[None]
+    share = jnp.broadcast_to(share, (PLANES, SIDE, 3, WIDTH)).reshape(PEERS, 3, WIDTH)
+    head = sums[ROWS:].reshape(SIDE, HEAD)
+    head = lax.dynamic_index_in_dim(head, mine, 0, keepdims=False)
+    head = jnp.broadcast_to(jnp.concatenate(bf16_terms(head)), (PEERS, 3 * HEAD))
+    logp_row = slotted[:, WIDTH:].reshape(PEERS, 12 * OUTCOMES)
+    gap = jnp.zeros((PEERS, WIDTH - 12 * OUTCOMES - 3 * HEAD), jnp.bfloat16)
+    mixed = jnp.concatenate([logp_row, gap, head], -1)[:, None]
+    tiles = jnp.concatenate([new_rows, mixed, share], 1)
+    packed = pl.pallas_call(
+        tile_kernel,
+        out_shape=jax.ShapeDtypeStruct(packed.shape, packed.dtype),
+        in_specs=[ANY, ANY],
+        out_specs=ANY,
+        scratch_shapes=[pltpu.SemaphoreType.DMA],
+        input_output_aliases={1: 0},
+        name="pack_tiles",
+    )(tiles, packed)
     direct = exchanged(packed)
 
     codes = relayed[:, RELAY * LEVELS, : 2 * RELAY].astype(jnp.int32)
@@ -395,9 +419,7 @@
         return lax.ppermute(x, "sample", pairs)
 
     lasts = [onward[0]] + [in_plane(onward[k], k) for k in range(1, SIDE)]
-    piece, lasts = lax.optimization_barrier((piece, lasts))
     came = came.astype(jnp.int32)
-    piece = tree_sum(piece, "sample", PEERS, [SIDE * k for k in range(1, PLANES)])
     over = pl.pallas_call(
         flag_kernel,
         grid=(1,),
@@ -411,26 +433,36 @@
         return lasts
 
     def by_pairs(lasts):
-        high = exchanged(pack_direct(2, target, cache, jnp.zeros_like(tiles)))
+        high = exchanged(pack_direct(2, target, cache))
         high = high[:, : 2 * LEVELS].reshape(PLANES, SIDE, 2 * LEVELS, WIDTH)
         high = jnp.swapaxes(high, 0, 1).reshape(SIDE, 2 * PLANES * LEVELS, WIDTH)
         high = jnp.pad(high, ((0, 0), (0, LAST - 2 * PLANES * LEVELS), (0, 0)))
         return [lax.dynamic_index_in_dim(high, came[k], 0, keepdims=False) for k in range(SIDE)]
 
+    piece, head = pl.pallas_call(
+        plane_sum_kernel,
+        grid=(1,),
+        out_shape=(jax.ShapeDtypeStruct((SIDE, WIDTH), jnp.float32),) * 2,
+        in_specs=[pl.BlockSpec((PEERS, 8, WIDTH), lambda t: (0, 2 * LEVELS // 8, 0))],
+        out_specs=(pl.BlockSpec((SIDE, WIDTH), lambda t: (0, 0)),) * 2,
+        name="plane_sum",
+    )(direct)
+    piece = piece.reshape(2 * SIDE, ROWS)
+    other = lax.ppermute(piece, "sample", xor_pairs(PEERS, 1))
+    piece = jnp.where(
+        core == 0, jnp.concatenate([piece, other], 0), jnp.concatenate([other, piece], 0)
+    )
     direct, lasts, piece = lax.optimization_barrier((direct, lasts, piece))
     lasts = lax.cond(over[0] > 0, by_pairs, by_relay, lasts)
     piece, lasts = lax.optimization_barrier((piece, lasts))
     shares = jnp.stack([piece] + [in_plane(piece, k) for k in range(2, SIDE, 2)])
     rows_y = jnp.arange(4, dtype=jnp.int32)
     ours = (lax.rem(y - rows_y + 4, 4)[:, None] == rows_y[None, :])[..., None, None]
-    grads = jnp.sum(jnp.where(ours, shares[None], 0.0), 1).reshape(sums.shape)
+    grad_out = jnp.sum(jnp.where(ours, shares[None], 0.0), 1).reshape(ROWS, ROWS)
+    head = head[:, WIDTH - 3 * HEAD :].reshape(SIDE, 3, HEAD)
+    grad_head = (head[:, 0] + (head[:, 1] + head[:, 2])).reshape(OUTCOMES, ROWS).T
     new_cache, log_probs = settle(came, direct, lasts)
-    return (
-        jnp.swapaxes(new_cache, 0, 1),
-        log_probs[:, :OUTCOMES],
-        grads[:ROWS],
-        grads[ROWS : ROWS + OUTCOMES].T,
-    )
+    return (jnp.swapaxes(new_cache, 0, 1), log_probs[:, :OUTCOMES], grad_out, grad_head)
 
 
 def solution(mesh):

time: 182 us -> 172 us (0.945)
  starting transfers between devices: 55.2 us -> 44.3 us
  Pallas kernels: 29.5 us -> 33.6 us
    ppermute x14 -> x7, starting transfers between devices: 22.8 us -> 10.1 us  [tree_sum(): terms = [x] + [lax.ppermute(x, axis, xor_pairs(size, bit)) for bit in bits]]
    pallas_call x0 -> x2, Pallas kernels: none -> 10.7 us  [the longest x1 9.05 us: on_device(): pl.pallas_call(tile_kernel, out_shape=jax.ShapeDtypeStruct(packed.shape,...]
    pallas_call x1, Pallas kernels: 10 us -> 3.44 us  [pack_direct(): pl.pallas_call(functools.partial(direct_kernel, low), out_shape=jax.Shape...]
    add x4 -> x3, other arithmetic: 3.46 us -> 0.93 us  [tree_sum(): terms = [terms[i] + terms[i + 1] for i in range(0, len(terms), 2)]]
    unnamed x30 -> x32, local copies, waits for them, and re-layouts: 8.6 us -> 9.78 us
    ppermute x14 -> x7, waiting for transfers between devices: 6.02 us -> 4.98 us  [tree_sum(): terms = [x] + [lax.ppermute(x, axis, xor_pairs(size, bit)) for bit in bits]]
  transfers between devices with their start and end apart: 26 -> 20, of which waited for: 8 -> 10; matrix products, arithmetic and copies ran while one was open for 13% -> 12% of each run, Pallas kernels for 13% -> 16%
where the time goes in v4:
time: 172 us; the launch traced here: 170 us
  waiting for transfers between devices  64.7 us (38%)
  starting transfers between devices  44.3 us (26%)
  Pallas kernels  33.6 us (20%)
  local copies, waits for them, and re-layouts  15.7 us (9%)
  other arithmetic  8.29 us (5%)
  between operations  1.87 us (1%)
  matrix products  1.83 us (1%)
    ppermute x10, waiting for transfers between devices, in_plane(): return lax.ppermute(x, 'sample', pairs)  59.4 us
    all_to_all x2, starting transfers between devices, exchanged(): lax.all_to_all(x, 'sample', split_axis=0, concat_axis=0, tiled=True, axis...  18.6 us
    ppermute x10, starting transfers between devices, in_plane(): return lax.ppermute(x, 'sample', pairs)  15.2 us
    ppermute x7, starting transfers between devices, tree_sum(): terms = [x] + [lax.ppermute(x, axis, xor_pairs(size, bit)) for bit in bits]  10.1 us
    unnamed x32, local copies, waits for them, and re-layouts  9.78 us
    pallas_call x1, Pallas kernels, on_device(): pl.pallas_call(tile_kernel, out_shape=jax.ShapeDtypeStruct(packed.shape,...  9.05 us
    pallas_call x1, Pallas kernels, settle(): pl.pallas_call(settle_kernel, grid=(PLANES,), out_shape=(jax.ShapeDtypeSt...  8.38 us
    pallas_call x1, Pallas kernels, on_device(): pl.pallas_call(relay_kernel, out_shape=jax.ShapeDtypeStruct((PLANES, PIEC...  5.49 us
  transfers between devices with their start and end apart: 20, of which 10 were waited for; matrix products, arithmetic and copies ran while one was open for 12% of the time, Pallas kernels for 16%

profile of v4, /device:TPU:1, one launch (start us, length us, event | category | flops | bytes accessed | tf_op | source)
XLA Modules:
  0.0 170.2 jit_solution(9872766285244527515)
XLA Ops:
  0.7 5.5 %pack_relay.1 = bf16[8,392,256]{2,1,0:T(8,128)(2,1)} custom-call(s32[128]{0:T(128)} %bitcast.94, bf16[128,48,256]{2,1,0:T(8,128)(2,1)} %cache.3), custom_call_target="tpu_custom_call" | custom-call | tf_op jit(solution)/shard_map/pack_relay/pallas_call | solution.py:333
  6.2 9.1 %all-to-all-start.2 = ((bf16[8,392,256]{2,1,0:T(8,128)(2,1)}), bf16[8,392,256]{2,1,0:T(8,128)(2,1)}, u32[]{:S(2)}, u32[]{:S(2)}) async-start(bf16[8,392,256]{2,1,0:T(8,128)(2,1)} %pack_relay.1), calls=%async_computation.2 | async-start | bytes 3211264 | tf_op jit(solution)/shard_map/all_to_all | solution.py:303
  15.3 2.2 %fusion.41 = (bf16[128,48,128]{2,1,0:T(8,128)(2,1)}, bf16[128,48,128]{2,1,0:T(8,128)(2,1)}) fusion(bf16[128,48,256]{2,1,0:T(8,128)(2,1)S(1)} %copy-done.4), kind=kLoop, calls=%fused_computation.101 | loop fusion | bytes 6291456 | tf_op jit(solution)/shard_map/slice | solution.py:43
  17.5 0.1 fusion.12
  17.7 0.2 convolution_convert_fusion.1
  17.9 0.2 convolution_convert_fusion.2
  18.2 0.2 bitcast_convert_fusion
  18.4 2.9 %copy.68 = bf16[128,48,128]{0,2,1:T(8,128)(2,1)} copy(bf16[128,48,128]{2,1,0:T(8,128)(2,1)} %get-tuple-element.164) | data formatting | bytes 3145728
  21.3 2.0 %multiply_reduce_fusion.1 = f32[128,4,48]{0,1,2:T(4,128)S(1)} fusion(f32[128,4,32]{0,2,1:T(8,128)S(1)} %get-tuple-element.177, bf16[128,48,128]{0,2,1:T(8,128)(2,1)} %copy.68), kind=kLoop, calls=%fused_computation.17 | loop fusion | flops 2334720 | bytes 1736704
  23.6 2.8 %copy.69 = bf16[128,48,128]{0,2,1:T(8,128)(2,1)} copy(bf16[128,48,128]{2,1,0:T(8,128)(2,1)} %get-tuple-element.165) | data formatting | bytes 3145728
  26.4 1.7 %multiply_reduce_fusion = f32[128,4,32]{0,2,1:T(8,128)S(1)} fusion(bf16[128,4,48,32]{0,3,1,2:T(8,128)(2,1)} %bitcast.83, f32[128,4,48]{0,1,2:T(4,128)S(1)} %copy.72), kind=kLoop, calls=%fused_computation.16 | loop fusion | flops 2342912 | bytes 1736704 | tf_op jit(solution)/shard_map/jat,jtaf->jaf/dot_general | solution.py:58
  28.2 0.2 fusion.9
  28.4 0.1 fusion.42
  28.6 0.3 fusion.28
  28.9 0.1 fusion.27
  29.0 0.2 fusion.43
  29.2 2.5 %collective-permute-start.2 = (f32[132,128]{1,0:T(8,128)S(1)}, f32[132,128]{1,0:T(8,128)S(1)}, u32[]{:S(2)}, u32[]{:S(2)}) collective-permute-start(f32[132,128]{1,0:T(8,128)S(1)} %pad_maximum_fusion.1), channel_id=1, source_target_pairs={{0,3},{1,2},{2,1},{3,0},{4,7},{5,6},{6,5},{7,4},{8,11},{9,10},{10,... | collective-permute-start | bytes 202760 | tf_op jit(solution)/shard_map/ppermute | solution.py:313
  31.7 0.5 collective-permute-start.1
  32.2 0.3 collective-permute-start
  32.6 3.4 %pack_direct.3.rows = bf16[64,104,256]{2,1,0:T(8,128)(2,1)} custom-call(s32[128]{0:T(128)S(1)} %bitcast.95, bf16[128,48,256]{2,1,0:T(8,128)(2,1)S(1)} %copy-done.4), custom_call_target="tpu_custom_call" | custom-call | bytes 10485760 | tf_op jit(solution)/shard_map/pack_direct/pallas_call | solution.py:287
  36.1 0.7 collective-permute-done.1
  36.8 0.9 add_add_fusion.1
  37.7 2.8 %collective-permute-start.5 = (f32[132,128]{1,0:T(8,128)S(1)}, f32[132,128]{1,0:T(8,128)S(1)}, u32[]{:S(2)}, u32[]{:S(2)}) collective-permute-start(f32[132,128]{1,0:T(8,128)S(1)} %add_add_fusion.1), channel_id=1, source_target_pairs={{0,24},{4,28},{8,16},{12,20},{16,8},{20,12},{24,0},{28,4},{32,56},... | collective-permute-start | bytes 202760 | tf_op jit(solution)/shard_map/ppermute | solution.py:313
  40.5 0.4 collective-permute-start.4
  40.9 0.3 collective-permute-start.3
  41.3 1.3 collective-permute-done.5
  42.6 2.8 %collective-permute-done.4 = f32[132,128]{1,0:T(8,128)S(1)} collective-permute-done((f32[132,128]{1,0:T(8,128)S(1)}, f32[132,128]{1,0:T(8,128)S(1)}, u32[]{:S(2)}, u32[]{:S(2)}) %collective-permute-start.4) | collective-permute-done | bytes 67616 | tf_op jit(solution)/shard_map/ppermute | solution.py:313
  45.4 3.3 %collective-permute-start.6 = (f32[132,128]{1,0:T(8,128)S(1)}, f32[132,128]{1,0:T(8,128)S(1)}, u32[]{:S(2)}, u32[]{:S(2)}) collective-permute-start(f32[132,128]{1,0:T(8,128)S(1)} %add_add_fusion), channel_id=1, source_target_pairs={{0,4},{4,0},{8,12},{12,8},{16,20},{20,16},{24,28},{28,24},{32,36},... | collective-permute-start | bytes 202760 | tf_op jit(solution)/shard_map/ppermute | solution.py:313
  48.7 0.2 convolution_convert_fusion
  49.1 0.1 copy.49
  49.5 0.2 collective-permute-done.6
  50.1 0.9 pad_maximum_fusion.tiles
  51.0 9.0 %pack_tiles.1 = bf16[64,104,256]{2,1,0:T(8,128)(2,1)} custom-call(bf16[64,8,256]{2,1,0:T(8,128)(2,1)} %pad_maximum_fusion.tiles, bf16[64,104,256]{2,1,0:T(8,128)(2,1)} %pack_direct.3.rows), custom_call_target="tpu_custom_call", output_to_operand_aliasing={{}: (1, {})} | custom-call | tf_op jit(solution)/shard_map/pack_tiles/pallas_call | solution.py:379
  60.0 9.6 %all-to-all-start.1 = ((bf16[64,104,256]{2,1,0:T(8,128)(2,1)}), bf16[64,104,256]{2,1,0:T(8,128)(2,1)S(1)}, u32[]{:S(2)}, u32[]{:S(2)}) async-start(bf16[64,104,256]{2,1,0:T(8,128)(2,1)} %pack_tiles.1), calls=%async_computation.1 | async-start | bytes 6815744 | tf_op jit(solution)/shard_map/all_to_all | solution.py:303
  69.7 0.6 stack.75.side
  70.3 1.3 slice_convert_fusion
  71.6 4.3 %pack_plane.1 = (bf16[776,256]{1,0:T(8,128)(2,1)}, bf16[776,256]{1,0:T(8,128)(2,1)}, bf16[776,256]{1,0:T(8,128)(2,1)}, bf16[776,256]{1,0:T(8,128)(2,1)}, bf16[77...) custom-call(s32[8,16]{1,0:T(8,128)} %bitcast.90, ...), custom_call_target="tpu_custom_call" | custom-call | bytes 5242880 | tf_op jit(solution)/shard_map/pack_plane/pallas_call | solution.py:394
  75.9 0.5 collective-permute-start.7
  76.5 1.3 collective-permute-start.8
  77.8 1.5 collective-permute-start.9
  79.3 1.3 collective-permute-start.10
  80.6 1.9 %collective-permute-start.11 = (bf16[776,256]{1,0:T(8,128)(2,1)}, bf16[776,256]{1,0:T(8,128)(2,1)}, u32[]{:S(2)}, u32[]{:S(2)}) collective-permute-start(bf16[776,256]{1,0:T(8,128)(2,1)} %get-tuple-element.102), channel_id=1, source_target_pairs={{0,20},{4,16},{8,28},{12,24},{16,4},{20,0},{24,12},{28,8},{32,52},... | collective-permute-start | bytes 1191944 | tf_op jit(solution)/shard_map/ppermute | solution.py:419
  82.5 1.5 collective-permute-start.12
  84.0 9.7 %collective-permute-done.8.refs_2_ = bf16[776,256]{1,0:T(8,128)(2,1)} collective-permute-done((bf16[776,256]{1,0:T(8,128)(2,1)}, bf16[776,256]{1,0:T(8,128)(2,1)}, u32[]{:S(2)}, u32[]{:S(2)}) %collective-permute-start.8) | collective-permute-done | bytes 397344 | tf_op jit(solution)/shard_map/ppermute | solution.py:419
  93.7 3.8 %collective-permute-start.13 = (bf16[776,256]{1,0:T(8,128)(2,1)}, bf16[776,256]{1,0:T(8,128)(2,1)}, u32[]{:S(2)}, u32[]{:S(2)}) collective-permute-start(bf16[776,256]{1,0:T(8,128)(2,1)} %get-tuple-element.104), channel_id=1, source_target_pairs={{0,28},{4,24},{8,4},{12,0},{16,12},{20,8},{24,20},{28,16},{32,60},... | collective-permute-start | bytes 1191944 | tf_op jit(solution)/shard_map/ppermute | solution.py:419
  97.6 12.8 %collective-permute-done.9.refs_3_ = bf16[776,256]{1,0:T(8,128)(2,1)} collective-permute-done((bf16[776,256]{1,0:T(8,128)(2,1)}, bf16[776,256]{1,0:T(8,128)(2,1)}, u32[]{:S(2)}, u32[]{:S(2)}) %collective-permute-start.9) | collective-permute-done | bytes 397344 | tf_op jit(solution)/shard_map/ppermute | solution.py:419
  110.5 17.9 %collective-permute-done.10.refs_4_ = bf16[776,256]{1,0:T(8,128)(2,1)} collective-permute-done((bf16[776,256]{1,0:T(8,128)(2,1)}, bf16[776,256]{1,0:T(8,128)(2,1)}, u32[]{:S(2)}, u32[]{:S(2)}) %collective-permute-start.10) | collective-permute-done | bytes 397344 | tf_op jit(solution)/shard_map/ppermute | solution.py:419
  128.4 18.2 %collective-permute-done.11.refs_5_ = bf16[776,256]{1,0:T(8,128)(2,1)} collective-permute-done((bf16[776,256]{1,0:T(8,128)(2,1)}, bf16[776,256]{1,0:T(8,128)(2,1)}, u32[]{:S(2)}, u32[]{:S(2)}) %collective-permute-start.11) | collective-permute-done | bytes 397344 | tf_op jit(solution)/shard_map/ppermute | solution.py:419
  146.6 0.7 collective-permute-done.13.refs_7_
  147.3 1.3 flag.1
  149.4 1.7 %copy-done.1 = bf16[64,104,256]{2,1,0:T(8,128)(2,1)} copy-done((bf16[64,104,256]{2,1,0:T(8,128)(2,1)}, bf16[64,104,256]{2,1,0:T(8,128)(2,1)S(1)}, u32[]{:S(2)}) %copy-start.1) | copy-done | bytes 3407896
  151.1 1.6 plane_sum.1
  152.7 0.7 reshape.166
  153.4 0.8 slice.47
  154.3 0.3 collective-permute-start.14
  154.6 0.7 add.209
  155.2 0.2 collective-permute-done.14
  155.5 2.3 %collective-permute-start.17 = (f32[32,128]{1,0:T(8,128)S(1)}, f32[32,128]{1,0:T(8,128)S(1)}, u32[]{:S(2)}, u32[]{:S(2)}) collective-permute-start(f32[32,128]{1,0:T(8,128)S(1)} %maximum_select_fusion), channel_id=1, source_target_pairs={{0,24},{4,28},{8,0},{12,4},{16,8},{20,12},{24,16},{28,20},{32,56},... | collective-permute-start | bytes 49160 | tf_op jit(solution)/shard_map/ppermute | solution.py:419
  157.7 0.5 collective-permute-start.16
  158.3 0.6 collective-permute-start.15
  158.9 8.4 %settle.1 = (bf16[49,256,256]{2,1,0:T(8,128)(2,1)}, f32[256,128]{1,0:T(8,128)S(1)}) custom-call(s32[8]{0:T(128)S(1)} %stack.71.side, bf16[64,104,256]{2,1,0:T(8,128)(2,1)S(1)} %copy-done.2, bf16[776,256]{1,0:T(8,128)(2,1)} %get-tuple-element.124.refs_0_, bf16[776,256]{1,0:T(8,128)(2,1)} %get-tuple-element.125.refs_1_, ...), custom_call_target="tpu_custom_call" | custom-call | flops 2147483648 | bytes 14680064 | tf_op jit(solution)/shard_map/settle/pallas_call | solution.py:266
  167.2 0.6 copy-done.3
  167.9 1.6 copy.53
  169.5 0.7 select_reduce_fusion
  (82 shorter events, 1.6 us)
Async XLA Ops:
  0.6 17.5 %copy-start = (bf16[128,128]{1,0:T(8,128)(2,1)S(1)}, bf16[128,128]{1,0:T(8,128)(2,1)}, u32[]{:S(2)}) copy-start(bf16[128,128]{1,0:T(8,128)(2,1)} %param.16) | copy-start | bytes 98308
  0.6 14.6 %copy-start.4 = (bf16[128,48,256]{2,1,0:T(8,128)(2,1)S(1)}, bf16[128,48,256]{2,1,0:T(8,128)(2,1)}, u32[]{:S(2)}) copy-start(bf16[128,48,256]{2,1,0:T(8,128)(2,1)} %cache.3) | copy-start | bytes 9437188
  6.2 53.9 %all-to-all-start.2 = ((bf16[8,392,256]{2,1,0:T(8,128)(2,1)}), bf16[8,392,256]{2,1,0:T(8,128)(2,1)}, u32[]{:S(2)}, u32[]{:S(2)}) async-start(bf16[8,392,256]{2,1,0:T(8,128)(2,1)} %pack_relay.1), calls=%async_computation.2 | async-start | bytes 3211264 | tf_op jit(solution)/shard_map/all_to_all | solution.py:303
  15.2 2.3 %copy-start.5 = (bf16[128,128]{1,0:T(8,128)(2,1)S(1)}, bf16[128,128]{1,0:T(8,128)(2,1)}, u32[]{:S(2)}) copy-start(bf16[128,128]{1,0:T(8,128)(2,1)} %param.13) | copy-start | bytes 98308
  15.3 2.4 %copy-start.6 = (bf16[128,128]{1,0:T(8,128)(2,1)S(1)}, bf16[128,128]{1,0:T(8,128)(2,1)}, u32[]{:S(2)}) copy-start(bf16[128,128]{1,0:T(8,128)(2,1)} %param.18) | copy-start | bytes 98308
  15.3 2.4 %copy-start.9 = (f32[128]{0:T(128)S(1)}, f32[128]{0:T(128)}, u32[]{:S(2)}) copy-start(f32[128]{0:T(128)} %param.15) | copy-start | bytes 1540
  15.3 2.6 %copy-start.7 = (bf16[128,128]{1,0:T(8,128)(2,1)S(1)}, bf16[128,128]{1,0:T(8,128)(2,1)}, u32[]{:S(2)}) copy-start(bf16[128,128]{1,0:T(8,128)(2,1)} %param.17) | copy-start | bytes 98308
  23.3 4.9 %copy-start.8 = (bf16[128,128]{1,0:T(8,128)(2,1)S(1)}, bf16[128,128]{1,0:T(8,128)(2,1)}, u32[]{:S(2)}) copy-start(bf16[128,128]{1,0:T(8,128)(2,1)} %param.19) | copy-start | bytes 98308
  23.3 5.1 %copy-start.11 = (bf16[128,4]{0,1:T(4,128)(2,1)S(1)}, bf16[128,4]{0,1:T(4,128)(2,1)}, u32[]{:S(2)}) copy-start(bf16[128,4]{0,1:T(4,128)(2,1)} %param.20) | copy-start | bytes 3076
  23.3 5.3 %copy-start.12 = (s32[128]{0:T(128)S(1)}, s32[128]{0:T(128)}, u32[]{:S(2)}) copy-start(s32[128]{0:T(128)} %param.22) | copy-start | bytes 1540
  23.3 5.3 %copy-start.13 = (f32[128]{0:T(128)S(1)}, f32[128]{0:T(128)}, u32[]{:S(2)}) copy-start(f32[128]{0:T(128)} %param.21) | copy-start | bytes 1540
  23.3 9.2 %copy-start.10 = (s32[128,1]{0,1:T(1,128)S(1)}, s32[128,1]{0,1:T(1,128)}, u32[]{:S(2)}) copy-start(s32[128,1]{0,1:T(1,128)} %param.23) | copy-start | bytes 1540
  29.2 6.9 %collective-permute-start.2 = (f32[132,128]{1,0:T(8,128)S(1)}, f32[132,128]{1,0:T(8,128)S(1)}, u32[]{:S(2)}, u32[]{:S(2)}) collective-permute-start(f32[132,128]{1,0:T(8,128)S(1)} %pad_maximum_fusion.1), channel_id=1, source_target_pairs={{0,3},{1,2},{2,1},{3,0},{4,7},{5,6},{6,5},{7,4},{8,11},{9,10},{10,... | collective-permute-start | bytes 202760 | tf_op jit(solution)/shard_map/ppermute | solution.py:313
  31.7 5.1 %collective-permute-start.1 = (f32[132,128]{1,0:T(8,128)S(1)}, f32[132,128]{1,0:T(8,128)S(1)}, u32[]{:S(2)}, u32[]{:S(2)}) collective-permute-start(f32[132,128]{1,0:T(8,128)S(1)} %pad_maximum_fusion.1), channel_id=1, source_target_pairs={{0,2},{1,3},{2,0},{3,1},{4,6},{5,7},{6,4},{7,5},{8,10},{9,11},{10,... | collective-permute-start | bytes 202760 | tf_op jit(solution)/shard_map/ppermute | solution.py:313
  32.2 4.6 %collective-permute-start = (f32[132,128]{1,0:T(8,128)S(1)}, f32[132,128]{1,0:T(8,128)}, u32[]{:S(2)}, u32[]{:S(2)}) collective-permute-start(f32[132,128]{1,0:T(8,128)S(1)} %pad_maximum_fusion.1), channel_id=1, source_target_pairs={{0,1},{1,0},{2,3},{3,2},{4,5},{5,4},{6,7},{7,6},{8,9},{9,8},{10,11... | collective-permute-start | bytes 202760 | tf_op jit(solution)/shard_map/ppermute | solution.py:313
  37.7 4.9 %collective-permute-start.5 = (f32[132,128]{1,0:T(8,128)S(1)}, f32[132,128]{1,0:T(8,128)S(1)}, u32[]{:S(2)}, u32[]{:S(2)}) collective-permute-start(f32[132,128]{1,0:T(8,128)S(1)} %add_add_fusion.1), channel_id=1, source_target_pairs={{0,24},{4,28},{8,16},{12,20},{16,8},{20,12},{24,0},{28,4},{32,56},... | collective-permute-start | bytes 202760 | tf_op jit(solution)/shard_map/ppermute | solution.py:313
  40.5 4.9 %collective-permute-start.4 = (f32[132,128]{1,0:T(8,128)S(1)}, f32[132,128]{1,0:T(8,128)S(1)}, u32[]{:S(2)}, u32[]{:S(2)}) collective-permute-start(f32[132,128]{1,0:T(8,128)S(1)} %add_add_fusion.1), channel_id=1, source_target_pairs={{0,16},{4,20},{8,24},{12,28},{16,0},{20,4},{24,8},{28,12},{32,48},... | collective-permute-start | bytes 202760 | tf_op jit(solution)/shard_map/ppermute | solution.py:313
  40.9 4.5 %collective-permute-start.3 = (f32[132,128]{1,0:T(8,128)S(1)}, f32[132,128]{1,0:T(8,128)S(1)}, u32[]{:S(2)}, u32[]{:S(2)}) collective-permute-start(f32[132,128]{1,0:T(8,128)S(1)} %add_add_fusion.1), channel_id=1, source_target_pairs={{0,8},{4,12},{8,0},{12,4},{16,24},{20,28},{24,16},{28,20},{32,40},... | collective-permute-start | bytes 202760 | tf_op jit(solution)/shard_map/ppermute | solution.py:313
  45.4 4.2 %collective-permute-start.6 = (f32[132,128]{1,0:T(8,128)S(1)}, f32[132,128]{1,0:T(8,128)S(1)}, u32[]{:S(2)}, u32[]{:S(2)}) collective-permute-start(f32[132,128]{1,0:T(8,128)S(1)} %add_add_fusion), channel_id=1, source_target_pairs={{0,4},{4,0},{8,12},{12,8},{16,20},{20,16},{24,28},{28,24},{32,36},... | collective-permute-start | bytes 202760 | tf_op jit(solution)/shard_map/ppermute | solution.py:313
  60.0 89.3 %all-to-all-start.1 = ((bf16[64,104,256]{2,1,0:T(8,128)(2,1)}), bf16[64,104,256]{2,1,0:T(8,128)(2,1)S(1)}, u32[]{:S(2)}, u32[]{:S(2)}) async-start(bf16[64,104,256]{2,1,0:T(8,128)(2,1)} %pack_tiles.1), calls=%async_computation.1 | async-start | bytes 6815744 | tf_op jit(solution)/shard_map/all_to_all | solution.py:303
  75.9 6.6 %collective-permute-start.7 = (bf16[776,256]{1,0:T(8,128)(2,1)}, bf16[776,256]{1,0:T(8,128)(2,1)}, u32[]{:S(2)}, u32[]{:S(2)}) collective-permute-start(bf16[776,256]{1,0:T(8,128)(2,1)} %get-tuple-element.98), channel_id=1, source_target_pairs={{0,4},{4,0},{8,12},{12,8},{16,20},{20,16},{24,28},{28,24},{32,36},... | collective-permute-start | bytes 1191944 | tf_op jit(solution)/shard_map/ppermute | solution.py:419
  76.5 17.2 %collective-permute-start.8 = (bf16[776,256]{1,0:T(8,128)(2,1)}, bf16[776,256]{1,0:T(8,128)(2,1)}, u32[]{:S(2)}, u32[]{:S(2)}) collective-permute-start(bf16[776,256]{1,0:T(8,128)(2,1)} %get-tuple-element.99), channel_id=1, source_target_pairs={{0,8},{4,12},{8,16},{12,20},{16,24},{20,28},{24,0},{28,4},{32,40},... | collective-permute-start | bytes 1191944 | tf_op jit(solution)/shard_map/ppermute | solution.py:419
  77.8 32.7 %collective-permute-start.9 = (bf16[776,256]{1,0:T(8,128)(2,1)}, bf16[776,256]{1,0:T(8,128)(2,1)}, u32[]{:S(2)}, u32[]{:S(2)}) collective-permute-start(bf16[776,256]{1,0:T(8,128)(2,1)} %get-tuple-element.100), channel_id=1, source_target_pairs={{0,12},{4,8},{8,20},{12,16},{16,28},{20,24},{24,4},{28,0},{32,44},... | collective-permute-start | bytes 1191944 | tf_op jit(solution)/shard_map/ppermute | solution.py:419
  79.3 49.1 %collective-permute-start.10 = (bf16[776,256]{1,0:T(8,128)(2,1)}, bf16[776,256]{1,0:T(8,128)(2,1)}, u32[]{:S(2)}, u32[]{:S(2)}) collective-permute-start(bf16[776,256]{1,0:T(8,128)(2,1)} %get-tuple-element.101), channel_id=1, source_target_pairs={{0,16},{4,20},{8,24},{12,28},{16,0},{20,4},{24,8},{28,12},{32,48},... | collective-permute-start | bytes 1191944 | tf_op jit(solution)/shard_map/ppermute | solution.py:419
  80.6 66.0 %collective-permute-start.11 = (bf16[776,256]{1,0:T(8,128)(2,1)}, bf16[776,256]{1,0:T(8,128)(2,1)}, u32[]{:S(2)}, u32[]{:S(2)}) collective-permute-start(bf16[776,256]{1,0:T(8,128)(2,1)} %get-tuple-element.102), channel_id=1, source_target_pairs={{0,20},{4,16},{8,28},{12,24},{16,4},{20,0},{24,12},{28,8},{32,52},... | collective-permute-start | bytes 1191944 | tf_op jit(solution)/shard_map/ppermute | solution.py:419
  82.5 64.1 %collective-permute-start.12 = (bf16[776,256]{1,0:T(8,128)(2,1)}, bf16[776,256]{1,0:T(8,128)(2,1)}, u32[]{:S(2)}, u32[]{:S(2)}) collective-permute-start(bf16[776,256]{1,0:T(8,128)(2,1)} %get-tuple-element.103), channel_id=1, source_target_pairs={{0,24},{4,28},{8,0},{12,4},{16,8},{20,12},{24,16},{28,20},{32,56},... | collective-permute-start | bytes 1191944 | tf_op jit(solution)/shard_map/ppermute | solution.py:419
  93.7 53.7 %collective-permute-start.13 = (bf16[776,256]{1,0:T(8,128)(2,1)}, bf16[776,256]{1,0:T(8,128)(2,1)}, u32[]{:S(2)}, u32[]{:S(2)}) collective-permute-start(bf16[776,256]{1,0:T(8,128)(2,1)} %get-tuple-element.104), channel_id=1, source_target_pairs={{0,28},{4,24},{8,4},{12,0},{16,12},{20,8},{24,20},{28,16},{32,60},... | collective-permute-start | bytes 1191944 | tf_op jit(solution)/shard_map/ppermute | solution.py:419
  149.4 1.8 %copy-start.1 = (bf16[64,104,256]{2,1,0:T(8,128)(2,1)}, bf16[64,104,256]{2,1,0:T(8,128)(2,1)S(1)}, u32[]{:S(2)}) copy-start(bf16[64,104,256]{2,1,0:T(8,128)(2,1)S(1)} %all-to-all-done.1.tiles.direct) | copy-start | bytes 10223620
  154.3 1.2 collective-permute-start.14
  155.5 3.4 %copy-start.2 = (bf16[64,104,256]{2,1,0:T(8,128)(2,1)S(1)}, bf16[64,104,256]{2,1,0:T(8,128)(2,1)}, u32[]{:S(2)}) copy-start(bf16[64,104,256]{2,1,0:T(8,128)(2,1)} %copy-done.1) | copy-start | bytes 10223620
  155.5 14.0 %collective-permute-start.17 = (f32[32,128]{1,0:T(8,128)S(1)}, f32[32,128]{1,0:T(8,128)S(1)}, u32[]{:S(2)}, u32[]{:S(2)}) collective-permute-start(f32[32,128]{1,0:T(8,128)S(1)} %maximum_select_fusion), channel_id=1, source_target_pairs={{0,24},{4,28},{8,0},{12,4},{16,8},{20,12},{24,16},{28,20},{32,56},... | collective-permute-start | bytes 49160 | tf_op jit(solution)/shard_map/ppermute | solution.py:419
  157.7 11.8 %collective-permute-start.16 = (f32[32,128]{1,0:T(8,128)S(1)}, f32[32,128]{1,0:T(8,128)S(1)}, u32[]{:S(2)}, u32[]{:S(2)}) collective-permute-start(f32[32,128]{1,0:T(8,128)S(1)} %maximum_select_fusion), channel_id=1, source_target_pairs={{0,16},{4,20},{8,24},{12,28},{16,0},{20,4},{24,8},{28,12},{32,48},... | collective-permute-start | bytes 49160 | tf_op jit(solution)/shard_map/ppermute | solution.py:419
  158.3 11.2 %collective-permute-start.15 = (f32[32,128]{1,0:T(8,128)S(1)}, f32[32,128]{1,0:T(8,128)S(1)}, u32[]{:S(2)}, u32[]{:S(2)}) collective-permute-start(f32[32,128]{1,0:T(8,128)S(1)} %maximum_select_fusion), channel_id=1, source_target_pairs={{0,8},{4,12},{8,16},{12,20},{16,24},{20,28},{24,0},{28,4},{32,40},... | collective-permute-start | bytes 49160 | tf_op jit(solution)/shard_map/ppermute | solution.py:419
  167.2 0.7 copy-start.3

commit v5 on v4

--- a/solution.py
+++ b/solution.py
@@ -164,8 +164,10 @@
 
 def plane_sum_kernel(tiles, out, head):
     x = jnp.sum(tiles[...].astype(jnp.float32).reshape(PLANES, SIDE, 8, WIDTH), 0)
-    out[...] = x[:, 5, :] + (x[:, 6, :] + x[:, 7, :])
-    head[...] = x[:, 4, :]
+    piece = x[:, 5, :] + (x[:, 6, :] + x[:, 7, :])
+    out[...] = jnp.concatenate([piece[:, :ROWS], piece[:, ROWS:]], 0)
+    part = x[:, 4, HEAD : 2 * HEAD] + (x[:, 4, 2 * HEAD : 3 * HEAD] + x[:, 4, 3 * HEAD :])
+    head[...] = jnp.concatenate([part[:OUTCOMES], part[OUTCOMES:]], 1)
 
 
 def forward_kernel(codes, side, got, *refs):
@@ -232,7 +234,8 @@
 
 
 def settle_kernel(side, direct, *refs):
-    lasts, (out, logp, held) = refs[:SIDE], refs[SIDE:]
+    lasts, (out, logp, held, kept) = refs[:SIDE], refs[SIDE:]
+    t = pl.program_id(0)
     for k, last in enumerate(lasts):
         held[side[k]] = last[...]
     turn = chosen_rows(WIDTH, WIDTH, lambda i: lax.rem(i, 16) * 16 + lax.div(i, 16))
@@ -255,11 +258,18 @@
     slot = lax.broadcasted_iota(jnp.int32, terms.shape, 0)
     lane = lax.broadcasted_iota(jnp.int32, terms.shape, 1)
     mine = lax.div(lane, 3 * OUTCOMES) == lax.rem(slot, 4)
-    terms = jnp.where(mine, terms, 0.0).astype(jnp.bfloat16)
-    lane = lax.broadcasted_iota(jnp.int32, (WIDTH, 128), 0)
-    outcome = lax.broadcasted_iota(jnp.int32, (WIDTH, 128), 1)
-    gather = (lax.rem(lane, OUTCOMES) == outcome).astype(jnp.float32).astype(jnp.bfloat16)
-    logp[...] = jnp.dot(terms, gather, preferred_element_type=jnp.float32)
+    rows = pl.ds(pl.multiple_of(t * 4 * SIDE, 4 * SIDE), 4 * SIDE)
+    kept[rows, :] = jnp.where(mine, terms, 0.0).astype(jnp.bfloat16)
+
+    @pl.when(t == PLANES - 1)
+    def _():
+        outcome = lax.broadcasted_iota(jnp.int32, (8, WIDTH), 0)
+        lane = lax.broadcasted_iota(jnp.int32, (8, WIDTH), 1)
+        gather = (lax.rem(lane, OUTCOMES) == outcome).astype(jnp.float32).astype(jnp.bfloat16)
+        found = lax.dot_general(
+            gather, kept[...], (((1,), (1,)), ((), ())), preferred_element_type=jnp.float32
+        )
+        logp[...] = found[:OUTCOMES]
 
 
 def settle(side, direct, lasts):
@@ -268,15 +278,18 @@
         grid=(PLANES,),
         out_shape=(
             jax.ShapeDtypeStruct((LEVELS + 1, 4 * PEERS, WIDTH), jnp.bfloat16),
-            jax.ShapeDtypeStruct((4 * PEERS, 128), jnp.float32),
+            jax.ShapeDtypeStruct((OUTCOMES, 4 * PEERS), jnp.float32),
         ),
         in_specs=[SMEM, pl.BlockSpec((SIDE, DIRECT, WIDTH), lambda t: (t, 0, 0))]
         + [pl.BlockSpec((2 * LEVELS, WIDTH), lambda t: (t, 0))] * SIDE,
         out_specs=(
             pl.BlockSpec((LEVELS + 1, 4 * SIDE, WIDTH), lambda t: (0, t, 0)),
-            pl.BlockSpec((4 * SIDE, 128), lambda t: (t, 0)),
+            pl.BlockSpec((OUTCOMES, 4 * PEERS), lambda t: (0, 0)),
         ),
-        scratch_shapes=[pltpu.VMEM((SIDE, 2 * LEVELS, WIDTH), jnp.bfloat16)],
+        scratch_shapes=[
+            pltpu.VMEM((SIDE, 2 * LEVELS, WIDTH), jnp.bfloat16),
+            pltpu.VMEM((4 * PEERS, WIDTH), jnp.bfloat16),
+        ],
         compiler_params=pltpu.CompilerParams(vmem_limit_bytes=24 << 20),
         cost_estimate=pl.CostEstimate(flops=2 << 30, bytes_accessed=14 << 20, transcendentals=0),
         name="settle",
@@ -365,11 +378,11 @@
     slotted = jnp.dot(slot, small, preferred_element_type=jnp.float32).astype(jnp.bfloat16)
     new_rows = slotted[:, :WIDTH].reshape(PEERS, 4, WIDTH)
     mine = y * 2 + core
-    share = sums[:ROWS].reshape(SIDE, SIDE, WIDTH)
-    share = lax.dynamic_index_in_dim(share, mine, 1, keepdims=False)
+    share = sums[:ROWS].reshape(SIDE, 2, SIDE, ROWS)
+    share = lax.dynamic_index_in_dim(share, mine, 2, keepdims=False).reshape(SIDE, WIDTH)
     share = jnp.stack(bf16_terms(share), 1)[None]
     share = jnp.broadcast_to(share, (PLANES, SIDE, 3, WIDTH)).reshape(PEERS, 3, WIDTH)
-    head = sums[ROWS:].reshape(SIDE, HEAD)
+    head = jnp.swapaxes(sums[ROWS:].reshape(OUTCOMES, 2, HEAD), 0, 1).reshape(SIDE, HEAD)
     head = lax.dynamic_index_in_dim(head, mine, 0, keepdims=False)
     head = jnp.broadcast_to(jnp.concatenate(bf16_terms(head)), (PEERS, 3 * HEAD))
     logp_row = slotted[:, WIDTH:].reshape(PEERS, 12 * OUTCOMES)
@@ -379,7 +392,7 @@
     packed = pl.pallas_call(
         tile_kernel,
         out_shape=jax.ShapeDtypeStruct(packed.shape, packed.dtype),
-        in_specs=[ANY, ANY],
+        in_specs=[pl.BlockSpec(memory_space=pltpu.VMEM), ANY],
         out_specs=ANY,
         scratch_shapes=[pltpu.SemaphoreType.DMA],
         input_output_aliases={1: 0},
@@ -442,12 +455,17 @@
     piece, head = pl.pallas_call(
         plane_sum_kernel,
         grid=(1,),
-        out_shape=(jax.ShapeDtypeStruct((SIDE, WIDTH), jnp.float32),) * 2,
+        out_shape=(
+            jax.ShapeDtypeStruct((2 * SIDE, ROWS), jnp.float32),
+            jax.ShapeDtypeStruct((OUTCOMES, ROWS), jnp.float32),
+        ),
         in_specs=[pl.BlockSpec((PEERS, 8, WIDTH), lambda t: (0, 2 * LEVELS // 8, 0))],
-        out_specs=(pl.BlockSpec((SIDE, WIDTH), lambda t: (0, 0)),) * 2,
+        out_specs=(
+            pl.BlockSpec((2 * SIDE, ROWS), lambda t: (0, 0)),
+            pl.BlockSpec((OUTCOMES, ROWS), lambda t: (0, 0)),
+        ),
         name="plane_sum",
     )(direct)
-    piece = piece.reshape(2 * SIDE, ROWS)
     other = lax.ppermute(piece, "sample", xor_pairs(PEERS, 1))
     piece = jnp.where(
         core == 0, jnp.concatenate([piece, other], 0), jnp.concatenate([other, piece], 0)
@@ -459,10 +477,8 @@
     rows_y = jnp.arange(4, dtype=jnp.int32)
     ours = (lax.rem(y - rows_y + 4, 4)[:, None] == rows_y[None, :])[..., None, None]
     grad_out = jnp.sum(jnp.where(ours, shares[None], 0.0), 1).reshape(ROWS, ROWS)
-    head = head[:, WIDTH - 3 * HEAD :].reshape(SIDE, 3, HEAD)
-    grad_head = (head[:, 0] + (head[:, 1] + head[:, 2])).reshape(OUTCOMES, ROWS).T
     new_cache, log_probs = settle(came, direct, lasts)
-    return (jnp.swapaxes(new_cache, 0, 1), log_probs[:, :OUTCOMES], grad_out, grad_head)
+    return (jnp.swapaxes(new_cache, 0, 1), log_probs.T, grad_out, head.T)
 
 
 def solution(mesh):

time: 172 us -> 162 us (0.942)
  Pallas kernels: 33.6 us -> 26.2 us
  local copies, waits for them, and re-layouts: 15.7 us -> 11.3 us
  waiting for transfers between devices: 64.7 us -> 66.7 us
    all_to_all x2, waiting for transfers between devices: 0.01 us -> 52 us  [exchanged(): lax.all_to_all(x, 'sample', split_axis=0, concat_axis=0, tiled=True, axis...]
    ppermute x10, waiting for transfers between devices: 59.4 us -> 9.73 us  [in_plane(): return lax.ppermute(x, 'sample', pairs)]
    pallas_call x1, Pallas kernels: 9.05 us -> 1.66 us  [on_device(): pl.pallas_call(tile_kernel, out_shape=jax.ShapeDtypeStruct(packed.shape,...]
    unnamed x32 -> x31, local copies, waits for them, and re-layouts: 9.78 us -> 7.59 us
  transfers between devices with their start and end apart: 20 -> 20, of which waited for: 10 -> 7; matrix products, arithmetic and copies ran while one was open for 12% -> 12% of each run, Pallas kernels for 16% -> 13%
where the time goes in v5:
time: 162 us; the launch traced here: 160 us
  waiting for transfers between devices  66.7 us (41%)
  starting transfers between devices  44.2 us (27%)
  Pallas kernels  26.2 us (16%)
  local copies, waits for them, and re-layouts  11.3 us (7%)
  other arithmetic  8.31 us (5%)
  matrix products  1.84 us (1%)
  between operations  1.84 us (1%)
    all_to_all x2, waiting for transfers between devices, exchanged(): lax.all_to_all(x, 'sample', split_axis=0, concat_axis=0, tiled=True, axis...  52 us
    all_to_all x2, starting transfers between devices, exchanged(): lax.all_to_all(x, 'sample', split_axis=0, concat_axis=0, tiled=True, axis...  17 us
    ppermute x10, starting transfers between devices, in_plane(): return lax.ppermute(x, 'sample', pairs)  15.4 us
    ppermute x7, starting transfers between devices, tree_sum(): terms = [x] + [lax.ppermute(x, axis, xor_pairs(size, bit)) for bit in bits]  9.98 us
    ppermute x10, waiting for transfers between devices, in_plane(): return lax.ppermute(x, 'sample', pairs)  9.73 us
    pallas_call x1, Pallas kernels, settle(): pl.pallas_call(settle_kernel, grid=(PLANES,), out_shape=(jax.ShapeDtypeSt...  8.14 us
    unnamed x31, local copies, waits for them, and re-layouts  7.59 us
    pallas_call x1, Pallas kernels, on_device(): pl.pallas_call(relay_kernel, out_shape=jax.ShapeDtypeStruct((PLANES, PIEC...  5.5 us
  transfers between devices with their start and end apart: 20, of which 7 were waited for; matrix products, arithmetic and copies ran while one was open for 12% of the time, Pallas kernels for 13%

profile of v5, /device:TPU:1, one launch (start us, length us, event | category | flops | bytes accessed | tf_op | source)
XLA Modules:
  0.0 160.4 jit_solution(11600816760152033634)
XLA Ops:
  0.7 5.5 %pack_relay.1 = bf16[8,392,256]{2,1,0:T(8,128)(2,1)} custom-call(s32[128]{0:T(128)} %bitcast.109, bf16[128,48,256]{2,1,0:T(8,128)(2,1)} %cache.3), custom_call_target="tpu_custom_call" | custom-call | tf_op jit(solution)/shard_map/pack_relay/pallas_call | solution.py:346
  6.2 9.1 %all-to-all-start.2 = ((bf16[8,392,256]{2,1,0:T(8,128)(2,1)}), bf16[8,392,256]{2,1,0:T(8,128)(2,1)}, u32[]{:S(2)}, u32[]{:S(2)}) async-start(bf16[8,392,256]{2,1,0:T(8,128)(2,1)} %pack_relay.1), calls=%async_computation.2 | async-start | bytes 3211264 | tf_op jit(solution)/shard_map/all_to_all | solution.py:316
  15.2 2.3 %fusion.39 = (bf16[128,48,128]{2,1,0:T(8,128)(2,1)}, bf16[128,48,128]{2,1,0:T(8,128)(2,1)}) fusion(bf16[128,48,256]{2,1,0:T(8,128)(2,1)S(1)} %copy-done.3), kind=kLoop, calls=%fused_computation.99 | loop fusion | bytes 6291456 | tf_op jit(solution)/shard_map/slice | solution.py:43
  17.5 2.9 %copy.61 = bf16[128,48,128]{0,2,1:T(8,128)(2,1)} copy(bf16[128,48,128]{2,1,0:T(8,128)(2,1)} %get-tuple-element.145) | data formatting | bytes 3145728
  20.4 0.1 fusion.12
  20.5 2.9 %copy.60 = bf16[128,48,128]{0,2,1:T(8,128)(2,1)} copy(bf16[128,48,128]{2,1,0:T(8,128)(2,1)} %get-tuple-element.144) | data formatting | bytes 3145728
  23.4 0.2 bitcast_convert_fusion
  23.7 0.2 convolution_convert_fusion.2
  23.9 2.0 %multiply_reduce_fusion.1 = f32[128,4,48]{0,1,2:T(4,128)S(1)} fusion(f32[128,4,32]{0,2,1:T(8,128)S(1)} %get-tuple-element.157, bf16[128,48,128]{0,2,1:T(8,128)(2,1)} %copy.60), kind=kLoop, calls=%fused_computation.17 | loop fusion | flops 2334720 | bytes 1736704
  26.0 0.1 reduce_max.19
  26.2 0.2 convolution_convert_fusion.1
  26.4 1.8 %multiply_reduce_fusion = f32[128,4,32]{0,2,1:T(8,128)S(1)} fusion(bf16[128,4,48,32]{0,3,1,2:T(8,128)(2,1)} %bitcast.95, f32[128,4,48]{0,1,2:T(4,128)S(1)} %copy.64), kind=kLoop, calls=%fused_computation.16 | loop fusion | flops 2342912 | bytes 1736704 | tf_op jit(solution)/shard_map/jat,jtaf->jaf/dot_general | solution.py:58
  28.2 0.2 fusion.9
  28.4 0.1 fusion.40
  28.6 0.3 fusion.26
  28.9 0.1 fusion.25
  29.0 0.2 fusion.41
  29.3 2.8 %collective-permute-start.1 = (f32[132,128]{1,0:T(8,128)S(1)}, f32[132,128]{1,0:T(8,128)S(1)}, u32[]{:S(2)}, u32[]{:S(2)}) collective-permute-start(f32[132,128]{1,0:T(8,128)S(1)} %pad_maximum_fusion.1), channel_id=1, source_target_pairs={{0,2},{1,3},{2,0},{3,1},{4,6},{5,7},{6,4},{7,5},{8,10},{9,11},{10,... | collective-permute-start | bytes 202760 | tf_op jit(solution)/shard_map/ppermute | solution.py:326
  32.0 0.9 collective-permute-start.2
  32.9 3.5 %pack_direct.3.rows = bf16[64,104,256]{2,1,0:T(8,128)(2,1)} custom-call(s32[128]{0:T(128)S(1)} %bitcast.110, bf16[128,48,256]{2,1,0:T(8,128)(2,1)S(1)} %copy-done.3), custom_call_target="tpu_custom_call" | custom-call | bytes 10485760 | tf_op jit(solution)/shard_map/pack_direct/pallas_call | solution.py:300
  36.4 0.1 convert_reduce_fusion
  36.5 0.3 collective-permute-done.2
  36.8 0.9 add_add_fusion.1
  37.7 3.0 %collective-permute-start.4 = (f32[132,128]{1,0:T(8,128)S(1)}, f32[132,128]{1,0:T(8,128)S(1)}, u32[]{:S(2)}, u32[]{:S(2)}) collective-permute-start(f32[132,128]{1,0:T(8,128)S(1)} %add_add_fusion.1), channel_id=1, source_target_pairs={{0,16},{4,20},{8,24},{12,28},{16,0},{20,4},{24,8},{28,12},{32,48},... | collective-permute-start | bytes 202760 | tf_op jit(solution)/shard_map/ppermute | solution.py:326
  40.7 0.8 collective-permute-start.5
  41.5 0.1 concatenate.21
  41.6 1.2 collective-permute-done.4
  42.7 3.4 %collective-permute-done.5 = f32[132,128]{1,0:T(8,128)S(1)} collective-permute-done((f32[132,128]{1,0:T(8,128)S(1)}, f32[132,128]{1,0:T(8,128)S(1)}, u32[]{:S(2)}, u32[]{:S(2)}) %collective-permute-start.5) | collective-permute-done | bytes 67616 | tf_op jit(solution)/shard_map/ppermute | solution.py:326
  46.1 2.5 %collective-permute-start.6 = (f32[132,128]{1,0:T(8,128)S(1)}, f32[132,128]{1,0:T(8,128)S(1)}, u32[]{:S(2)}, u32[]{:S(2)}) collective-permute-start(f32[132,128]{1,0:T(8,128)S(1)} %add_add_fusion), channel_id=1, source_target_pairs={{0,4},{4,0},{8,12},{12,8},{16,20},{20,16},{24,28},{28,24},{32,36},... | collective-permute-start | bytes 202760 | tf_op jit(solution)/shard_map/ppermute | solution.py:326
  48.7 0.2 convolution_convert_fusion
  48.9 0.1 copy.41
  49.1 0.1 reshape.205
  49.2 0.1 copy.40
  49.3 0.1 pad.19.clone
  49.4 0.2 collective-permute-done.6
  49.7 0.1 reshape.206
  49.8 0.1 pad_maximum_fusion.4
  50.0 0.9 pad_maximum_fusion.tiles
  50.9 1.7 %pack_tiles.1 = bf16[64,104,256]{2,1,0:T(8,128)(2,1)} custom-call(bf16[64,8,256]{2,1,0:T(8,128)(2,1)} %pad_maximum_fusion.tiles, bf16[64,104,256]{2,1,0:T(8,128)(2,1)} %pack_direct.3.rows), custom_call_target="tpu_custom_call", output_to_operand_aliasing={{}: (1, {})} | custom-call | tf_op jit(solution)/shard_map/pack_tiles/pallas_call | solution.py:392
  52.6 1.7 %all-to-all-done.2.got = bf16[8,392,256]{2,1,0:T(8,128)(2,1)} async-done(((bf16[8,392,256]{2,1,0:T(8,128)(2,1)}), bf16[8,392,256]{2,1,0:T(8,128)(2,1)}, u32[]{:S(2)}, u32[]{:S(2)}) %all-to-all-start.2) | async-done | bytes 1605664 | tf_op jit(solution)/shard_map/all_to_all | solution.py:316
  54.2 7.9 %all-to-all-start.1 = ((bf16[64,104,256]{2,1,0:T(8,128)(2,1)}), bf16[64,104,256]{2,1,0:T(8,128)(2,1)S(1)}, u32[]{:S(2)}, u32[]{:S(2)}) async-start(bf16[64,104,256]{2,1,0:T(8,128)(2,1)} %pack_tiles.1), calls=%async_computation.1 | async-start | bytes 6815744 | tf_op jit(solution)/shard_map/all_to_all | solution.py:316
  62.2 0.6 stack.75.side
  62.8 1.3 slice_convert_fusion
  64.1 4.3 %pack_plane.1 = (bf16[776,256]{1,0:T(8,128)(2,1)}, bf16[776,256]{1,0:T(8,128)(2,1)}, bf16[776,256]{1,0:T(8,128)(2,1)}, bf16[776,256]{1,0:T(8,128)(2,1)}, bf16[77...) custom-call(s32[8,16]{1,0:T(8,128)} %bitcast.103, ...), custom_call_target="tpu_custom_call" | custom-call | bytes 5242880 | tf_op jit(solution)/shard_map/pack_plane/pallas_call | solution.py:407
  68.5 0.5 collective-permute-start.7
  69.0 1.3 collective-permute-start.8
  70.3 1.5 collective-permute-start.9
  71.8 1.3 collective-permute-start.10
  73.1 1.9 %collective-permute-start.11 = (bf16[776,256]{1,0:T(8,128)(2,1)}, bf16[776,256]{1,0:T(8,128)(2,1)}, u32[]{:S(2)}, u32[]{:S(2)}) collective-permute-start(bf16[776,256]{1,0:T(8,128)(2,1)} %get-tuple-element.102), channel_id=1, source_target_pairs={{0,20},{4,16},{8,28},{12,24},{16,4},{20,0},{24,12},{28,8},{32,52},... | collective-permute-start | bytes 1191944 | tf_op jit(solution)/shard_map/ppermute | solution.py:432
  75.0 1.5 collective-permute-start.12
  76.5 9.7 %collective-permute-done.8.refs_2_ = bf16[776,256]{1,0:T(8,128)(2,1)} collective-permute-done((bf16[776,256]{1,0:T(8,128)(2,1)}, bf16[776,256]{1,0:T(8,128)(2,1)}, u32[]{:S(2)}, u32[]{:S(2)}) %collective-permute-start.8) | collective-permute-done | bytes 397344 | tf_op jit(solution)/shard_map/ppermute | solution.py:432
  86.2 3.8 %collective-permute-start.13 = (bf16[776,256]{1,0:T(8,128)(2,1)}, bf16[776,256]{1,0:T(8,128)(2,1)}, u32[]{:S(2)}, u32[]{:S(2)}) collective-permute-start(bf16[776,256]{1,0:T(8,128)(2,1)} %get-tuple-element.104), channel_id=1, source_target_pairs={{0,28},{4,24},{8,4},{12,0},{16,12},{20,8},{24,20},{28,16},{32,60},... | collective-permute-start | bytes 1191944 | tf_op jit(solution)/shard_map/ppermute | solution.py:432
  90.0 50.3 %all-to-all-done.1.tiles.direct = bf16[64,104,256]{2,1,0:T(8,128)(2,1)S(1)} async-done(((bf16[64,104,256]{2,1,0:T(8,128)(2,1)}), bf16[64,104,256]{2,1,0:T(8,128)(2,1)S(1)}, u32[]{:S(2)}, u32[]{:S(2)}) %all-to-all-start.1) | async-done | bytes 3407904 | tf_op jit(solution)/shard_map/all_to_all | solution.py:316
  140.3 1.7 %copy-done.1 = bf16[64,104,256]{2,1,0:T(8,128)(2,1)} copy-done((bf16[64,104,256]{2,1,0:T(8,128)(2,1)}, bf16[64,104,256]{2,1,0:T(8,128)(2,1)S(1)}, u32[]{:S(2)}) %copy-start.1) | copy-done | bytes 3407896
  142.1 1.7 %plane_sum.1 = (f32[16,128]{1,0:T(8,128)}, f32[4,128]{1,0:T(4,128)}) custom-call(bf16[64,104,256]{2,1,0:T(8,128)(2,1)} %copy-done.1), custom_call_target="tpu_custom_call" | custom-call | tf_op jit(solution)/shard_map/plane_sum/pallas_call | solution.py:455
  143.8 1.8 %collective-permute-start.14 = (f32[16,128]{1,0:T(8,128)}, f32[16,128]{1,0:T(8,128)S(1)}, u32[]{:S(2)}, u32[]{:S(2)}) collective-permute-start(f32[16,128]{1,0:T(8,128)} %get-tuple-element.105), channel_id=1, source_target_pairs={{0,4},{4,0},{8,12},{12,8},{16,20},{20,16},{24,28},{28,24},{32,36},... | collective-permute-start | bytes 24584 | tf_op jit(solution)/shard_map/ppermute | solution.py:469
  145.7 0.1 iota_compare_fusion.3
  145.7 0.1 stack.71.side
  145.8 1.4 flag.1
  147.9 2.4 %collective-permute-start.17 = (f32[32,128]{1,0:T(8,128)S(1)}, f32[32,128]{1,0:T(8,128)S(1)}, u32[]{:S(2)}, u32[]{:S(2)}) collective-permute-start(f32[32,128]{1,0:T(8,128)S(1)} %maximum_select_fusion), channel_id=1, source_target_pairs={{0,24},{4,28},{8,0},{12,4},{16,8},{20,12},{24,16},{28,20},{32,56},... | collective-permute-start | bytes 49160 | tf_op jit(solution)/shard_map/ppermute | solution.py:432
  150.3 0.5 collective-permute-start.16
  150.9 0.6 collective-permute-start.15
  151.5 8.1 %settle.1 = (bf16[49,256,256]{2,1,0:T(8,128)(2,1)}, f32[4,256]{1,0:T(4,128)}) custom-call(s32[8]{0:T(128)S(1)} %stack.71.side, bf16[64,104,256]{2,1,0:T(8,128)(2,1)S(1)} %copy-done.2, bf16[776,256]{1,0:T(8,128)(2,1)} %get-tuple-element.124.refs_0_, bf16[776,256]{1,0:T(8,128)(2,1)} %get-tuple-element.125.refs_1_, ...), custom_call_target="tpu_custom_call" | custom-call | flops 2147483648 | bytes 14680064 | tf_op jit(solution)/shard_map/settle/pallas_call | solution.py:276
  159.7 0.7 select_reduce_fusion
  (76 shorter events, 0.6 us)
Async XLA Ops:
  0.6 22.8 %copy-start = (bf16[128,128]{1,0:T(8,128)(2,1)S(1)}, bf16[128,128]{1,0:T(8,128)(2,1)}, u32[]{:S(2)}) copy-start(bf16[128,128]{1,0:T(8,128)(2,1)} %param.16) | copy-start | bytes 98308
  0.6 14.6 %copy-start.3 = (bf16[128,48,256]{2,1,0:T(8,128)(2,1)S(1)}, bf16[128,48,256]{2,1,0:T(8,128)(2,1)}, u32[]{:S(2)}) copy-start(bf16[128,48,256]{2,1,0:T(8,128)(2,1)} %cache.3) | copy-start | bytes 9437188
  6.2 48.1 %all-to-all-start.2 = ((bf16[8,392,256]{2,1,0:T(8,128)(2,1)}), bf16[8,392,256]{2,1,0:T(8,128)(2,1)}, u32[]{:S(2)}, u32[]{:S(2)}) async-start(bf16[8,392,256]{2,1,0:T(8,128)(2,1)} %pack_relay.1), calls=%async_computation.2 | async-start | bytes 3211264 | tf_op jit(solution)/shard_map/all_to_all | solution.py:316
  17.5 2.9 %copy-start.4 = (bf16[128,128]{1,0:T(8,128)(2,1)S(1)}, bf16[128,128]{1,0:T(8,128)(2,1)}, u32[]{:S(2)}) copy-start(bf16[128,128]{1,0:T(8,128)(2,1)} %param.13) | copy-start | bytes 98308
  17.5 5.9 %copy-start.9 = (f32[128]{0:T(128)S(1)}, f32[128]{0:T(128)}, u32[]{:S(2)}) copy-start(f32[128]{0:T(128)} %param.15) | copy-start | bytes 1540
  17.5 6.2 %copy-start.5 = (bf16[128,128]{1,0:T(8,128)(2,1)S(1)}, bf16[128,128]{1,0:T(8,128)(2,1)}, u32[]{:S(2)}) copy-start(bf16[128,128]{1,0:T(8,128)(2,1)} %param.17) | copy-start | bytes 98308
  20.4 5.8 %copy-start.6 = (bf16[128,128]{1,0:T(8,128)(2,1)S(1)}, bf16[128,128]{1,0:T(8,128)(2,1)}, u32[]{:S(2)}) copy-start(bf16[128,128]{1,0:T(8,128)(2,1)} %param.18) | copy-start | bytes 98308
  20.5 7.7 %copy-start.7 = (bf16[128,128]{1,0:T(8,128)(2,1)S(1)}, bf16[128,128]{1,0:T(8,128)(2,1)}, u32[]{:S(2)}) copy-start(bf16[128,128]{1,0:T(8,128)(2,1)} %param.19) | copy-start | bytes 98308
  23.4 5.0 %copy-start.11 = (bf16[128,4]{0,1:T(4,128)(2,1)S(1)}, bf16[128,4]{0,1:T(4,128)(2,1)}, u32[]{:S(2)}) copy-start(bf16[128,4]{0,1:T(4,128)(2,1)} %param.20) | copy-start | bytes 3076
  23.4 5.2 %copy-start.12 = (s32[128]{0:T(128)S(1)}, s32[128]{0:T(128)}, u32[]{:S(2)}) copy-start(s32[128]{0:T(128)} %param.22) | copy-start | bytes 1540
  23.4 5.2 %copy-start.13 = (f32[128]{0:T(128)S(1)}, f32[128]{0:T(128)}, u32[]{:S(2)}) copy-start(f32[128]{0:T(128)} %param.21) | copy-start | bytes 1540
  23.4 9.5 %copy-start.10 = (s32[128,1]{0,1:T(1,128)S(1)}, s32[128,1]{0,1:T(1,128)}, u32[]{:S(2)}) copy-start(s32[128,1]{0,1:T(1,128)} %param.23) | copy-start | bytes 1540
  29.3 7.3 %collective-permute-start.1 = (f32[132,128]{1,0:T(8,128)S(1)}, f32[132,128]{1,0:T(8,128)S(1)}, u32[]{:S(2)}, u32[]{:S(2)}) collective-permute-start(f32[132,128]{1,0:T(8,128)S(1)} %pad_maximum_fusion.1), channel_id=1, source_target_pairs={{0,2},{1,3},{2,0},{3,1},{4,6},{5,7},{6,4},{7,5},{8,10},{9,11},{10,... | collective-permute-start | bytes 202760 | tf_op jit(solution)/shard_map/ppermute | solution.py:326
  32.0 4.8 %collective-permute-start.2 = (f32[132,128]{1,0:T(8,128)S(1)}, f32[132,128]{1,0:T(8,128)S(1)}, u32[]{:S(2)}, u32[]{:S(2)}) collective-permute-start(f32[132,128]{1,0:T(8,128)S(1)} %pad_maximum_fusion.1), channel_id=1, source_target_pairs={{0,3},{1,2},{2,1},{3,0},{4,7},{5,6},{6,5},{7,4},{8,11},{9,10},{10,... | collective-permute-start | bytes 202760 | tf_op jit(solution)/shard_map/ppermute | solution.py:326
  32.9 3.9 %collective-permute-start = (f32[132,128]{1,0:T(8,128)S(1)}, f32[132,128]{1,0:T(8,128)}, u32[]{:S(2)}, u32[]{:S(2)}) collective-permute-start(f32[132,128]{1,0:T(8,128)S(1)} %pad_maximum_fusion.1), channel_id=1, source_target_pairs={{0,1},{1,0},{2,3},{3,2},{4,5},{5,4},{6,7},{7,6},{8,9},{9,8},{10,11... | collective-permute-start | bytes 202760 | tf_op jit(solution)/shard_map/ppermute | solution.py:326
  37.7 5.0 %collective-permute-start.4 = (f32[132,128]{1,0:T(8,128)S(1)}, f32[132,128]{1,0:T(8,128)S(1)}, u32[]{:S(2)}, u32[]{:S(2)}) collective-permute-start(f32[132,128]{1,0:T(8,128)S(1)} %add_add_fusion.1), channel_id=1, source_target_pairs={{0,16},{4,20},{8,24},{12,28},{16,0},{20,4},{24,8},{28,12},{32,48},... | collective-permute-start | bytes 202760 | tf_op jit(solution)/shard_map/ppermute | solution.py:326
  40.7 5.4 %collective-permute-start.5 = (f32[132,128]{1,0:T(8,128)S(1)}, f32[132,128]{1,0:T(8,128)S(1)}, u32[]{:S(2)}, u32[]{:S(2)}) collective-permute-start(f32[132,128]{1,0:T(8,128)S(1)} %add_add_fusion.1), channel_id=1, source_target_pairs={{0,24},{4,28},{8,16},{12,20},{16,8},{20,12},{24,0},{28,4},{32,56},... | collective-permute-start | bytes 202760 | tf_op jit(solution)/shard_map/ppermute | solution.py:326
  41.5 4.6 %collective-permute-start.3 = (f32[132,128]{1,0:T(8,128)S(1)}, f32[132,128]{1,0:T(8,128)S(1)}, u32[]{:S(2)}, u32[]{:S(2)}) collective-permute-start(f32[132,128]{1,0:T(8,128)S(1)} %add_add_fusion.1), channel_id=1, source_target_pairs={{0,8},{4,12},{8,0},{12,4},{16,24},{20,28},{24,16},{28,20},{32,40},... | collective-permute-start | bytes 202760 | tf_op jit(solution)/shard_map/ppermute | solution.py:326
  46.1 3.4 %collective-permute-start.6 = (f32[132,128]{1,0:T(8,128)S(1)}, f32[132,128]{1,0:T(8,128)S(1)}, u32[]{:S(2)}, u32[]{:S(2)}) collective-permute-start(f32[132,128]{1,0:T(8,128)S(1)} %add_add_fusion), channel_id=1, source_target_pairs={{0,4},{4,0},{8,12},{12,8},{16,20},{20,16},{24,28},{28,24},{32,36},... | collective-permute-start | bytes 202760 | tf_op jit(solution)/shard_map/ppermute | solution.py:326
  54.2 86.1 %all-to-all-start.1 = ((bf16[64,104,256]{2,1,0:T(8,128)(2,1)}), bf16[64,104,256]{2,1,0:T(8,128)(2,1)S(1)}, u32[]{:S(2)}, u32[]{:S(2)}) async-start(bf16[64,104,256]{2,1,0:T(8,128)(2,1)} %pack_tiles.1), calls=%async_computation.1 | async-start | bytes 6815744 | tf_op jit(solution)/shard_map/all_to_all | solution.py:316
  68.5 6.6 %collective-permute-start.7 = (bf16[776,256]{1,0:T(8,128)(2,1)}, bf16[776,256]{1,0:T(8,128)(2,1)}, u32[]{:S(2)}, u32[]{:S(2)}) collective-permute-start(bf16[776,256]{1,0:T(8,128)(2,1)} %get-tuple-element.98), channel_id=1, source_target_pairs={{0,4},{4,0},{8,12},{12,8},{16,20},{20,16},{24,28},{28,24},{32,36},... | collective-permute-start | bytes 1191944 | tf_op jit(solution)/shard_map/ppermute | solution.py:432
  69.0 17.2 %collective-permute-start.8 = (bf16[776,256]{1,0:T(8,128)(2,1)}, bf16[776,256]{1,0:T(8,128)(2,1)}, u32[]{:S(2)}, u32[]{:S(2)}) collective-permute-start(bf16[776,256]{1,0:T(8,128)(2,1)} %get-tuple-element.99), channel_id=1, source_target_pairs={{0,8},{4,12},{8,16},{12,20},{16,24},{20,28},{24,0},{28,4},{32,40},... | collective-permute-start | bytes 1191944 | tf_op jit(solution)/shard_map/ppermute | solution.py:432
  70.3 73.5 %collective-permute-start.9 = (bf16[776,256]{1,0:T(8,128)(2,1)}, bf16[776,256]{1,0:T(8,128)(2,1)}, u32[]{:S(2)}, u32[]{:S(2)}) collective-permute-start(bf16[776,256]{1,0:T(8,128)(2,1)} %get-tuple-element.100), channel_id=1, source_target_pairs={{0,12},{4,8},{8,20},{12,16},{16,28},{20,24},{24,4},{28,0},{32,44},... | collective-permute-start | bytes 1191944 | tf_op jit(solution)/shard_map/ppermute | solution.py:432
  71.8 74.0 %collective-permute-start.10 = (bf16[776,256]{1,0:T(8,128)(2,1)}, bf16[776,256]{1,0:T(8,128)(2,1)}, u32[]{:S(2)}, u32[]{:S(2)}) collective-permute-start(bf16[776,256]{1,0:T(8,128)(2,1)} %get-tuple-element.101), channel_id=1, source_target_pairs={{0,16},{4,20},{8,24},{12,28},{16,0},{20,4},{24,8},{28,12},{32,48},... | collective-permute-start | bytes 1191944 | tf_op jit(solution)/shard_map/ppermute | solution.py:432
  73.1 72.7 %collective-permute-start.11 = (bf16[776,256]{1,0:T(8,128)(2,1)}, bf16[776,256]{1,0:T(8,128)(2,1)}, u32[]{:S(2)}, u32[]{:S(2)}) collective-permute-start(bf16[776,256]{1,0:T(8,128)(2,1)} %get-tuple-element.102), channel_id=1, source_target_pairs={{0,20},{4,16},{8,28},{12,24},{16,4},{20,0},{24,12},{28,8},{32,52},... | collective-permute-start | bytes 1191944 | tf_op jit(solution)/shard_map/ppermute | solution.py:432
  75.0 70.8 %collective-permute-start.12 = (bf16[776,256]{1,0:T(8,128)(2,1)}, bf16[776,256]{1,0:T(8,128)(2,1)}, u32[]{:S(2)}, u32[]{:S(2)}) collective-permute-start(bf16[776,256]{1,0:T(8,128)(2,1)} %get-tuple-element.103), channel_id=1, source_target_pairs={{0,24},{4,28},{8,0},{12,4},{16,8},{20,12},{24,16},{28,20},{32,56},... | collective-permute-start | bytes 1191944 | tf_op jit(solution)/shard_map/ppermute | solution.py:432
  86.2 59.6 %collective-permute-start.13 = (bf16[776,256]{1,0:T(8,128)(2,1)}, bf16[776,256]{1,0:T(8,128)(2,1)}, u32[]{:S(2)}, u32[]{:S(2)}) collective-permute-start(bf16[776,256]{1,0:T(8,128)(2,1)} %get-tuple-element.104), channel_id=1, source_target_pairs={{0,28},{4,24},{8,4},{12,0},{16,12},{20,8},{24,20},{28,16},{32,60},... | collective-permute-start | bytes 1191944 | tf_op jit(solution)/shard_map/ppermute | solution.py:432
  140.3 1.8 %copy-start.1 = (bf16[64,104,256]{2,1,0:T(8,128)(2,1)}, bf16[64,104,256]{2,1,0:T(8,128)(2,1)S(1)}, u32[]{:S(2)}) copy-start(bf16[64,104,256]{2,1,0:T(8,128)(2,1)S(1)} %all-to-all-done.1.tiles.direct) | copy-start | bytes 10223620
  143.8 4.0 %copy-start.8 = (f32[16,128]{1,0:T(8,128)S(1)}, f32[16,128]{1,0:T(8,128)}, u32[]{:S(2)}) copy-start(f32[16,128]{1,0:T(8,128)} %get-tuple-element.105) | copy-start | bytes 24580
  143.8 4.0 %collective-permute-start.14 = (f32[16,128]{1,0:T(8,128)}, f32[16,128]{1,0:T(8,128)S(1)}, u32[]{:S(2)}, u32[]{:S(2)}) collective-permute-start(f32[16,128]{1,0:T(8,128)} %get-tuple-element.105), channel_id=1, source_target_pairs={{0,4},{4,0},{8,12},{12,8},{16,20},{20,16},{24,28},{28,24},{32,36},... | collective-permute-start | bytes 24584 | tf_op jit(solution)/shard_map/ppermute | solution.py:469
  147.9 3.6 %copy-start.2 = (bf16[64,104,256]{2,1,0:T(8,128)(2,1)S(1)}, bf16[64,104,256]{2,1,0:T(8,128)(2,1)}, u32[]{:S(2)}) copy-start(bf16[64,104,256]{2,1,0:T(8,128)(2,1)} %copy-done.1) | copy-start | bytes 10223620
  147.9 11.7 %collective-permute-start.17 = (f32[32,128]{1,0:T(8,128)S(1)}, f32[32,128]{1,0:T(8,128)S(1)}, u32[]{:S(2)}, u32[]{:S(2)}) collective-permute-start(f32[32,128]{1,0:T(8,128)S(1)} %maximum_select_fusion), channel_id=1, source_target_pairs={{0,24},{4,28},{8,0},{12,4},{16,8},{20,12},{24,16},{28,20},{32,56},... | collective-permute-start | bytes 49160 | tf_op jit(solution)/shard_map/ppermute | solution.py:432
  150.3 9.3 %collective-permute-start.16 = (f32[32,128]{1,0:T(8,128)S(1)}, f32[32,128]{1,0:T(8,128)S(1)}, u32[]{:S(2)}, u32[]{:S(2)}) collective-permute-start(f32[32,128]{1,0:T(8,128)S(1)} %maximum_select_fusion), channel_id=1, source_target_pairs={{0,16},{4,20},{8,24},{12,28},{16,0},{20,4},{24,8},{28,12},{32,48},... | collective-permute-start | bytes 49160 | tf_op jit(solution)/shard_map/ppermute | solution.py:432
  150.9 8.8 %collective-permute-start.15 = (f32[32,128]{1,0:T(8,128)S(1)}, f32[32,128]{1,0:T(8,128)S(1)}, u32[]{:S(2)}, u32[]{:S(2)}) collective-permute-start(f32[32,128]{1,0:T(8,128)S(1)} %maximum_select_fusion), channel_id=1, source_target_pairs={{0,8},{4,12},{8,16},{12,20},{16,24},{20,28},{24,0},{28,4},{32,40},... | collective-permute-start | bytes 49160 | tf_op jit(solution)/shard_map/ppermute | solution.py:432

commit v6 on v5

--- a/solution.py
+++ b/solution.py
@@ -290,7 +290,7 @@
             pltpu.VMEM((SIDE, 2 * LEVELS, WIDTH), jnp.bfloat16),
             pltpu.VMEM((4 * PEERS, WIDTH), jnp.bfloat16),
         ],
-        compiler_params=pltpu.CompilerParams(vmem_limit_bytes=24 << 20),
+        compiler_params=pltpu.CompilerParams(vmem_limit_bytes=12 << 20),
         cost_estimate=pl.CostEstimate(flops=2 << 30, bytes_accessed=14 << 20, transcendentals=0),
         name="settle",
     )(side, direct, *lasts)
@@ -300,7 +300,7 @@
     return pl.pallas_call(
         functools.partial(direct_kernel, low),
         out_shape=jax.ShapeDtypeStruct((PEERS, DIRECT, WIDTH), jnp.bfloat16),
-        in_specs=[SMEM, ANY],
+        in_specs=[SMEM, pl.BlockSpec(memory_space=pltpu.VMEM)],
         out_specs=ANY,
         scratch_shapes=[
             pltpu.SMEM((PEERS,), jnp.int32),
@@ -308,6 +308,7 @@
             pltpu.SemaphoreType.DMA,
         ],
         cost_estimate=pl.CostEstimate(flops=0, bytes_accessed=10 << 20, transcendentals=0),
+        compiler_params=pltpu.CompilerParams(vmem_limit_bytes=8 << 20),
         name="pack_direct",
     )(dest, cache)
 
@@ -356,6 +357,7 @@
             pltpu.SemaphoreType.DMA,
             pltpu.SemaphoreType.DMA,
         ],
+        compiler_params=pltpu.CompilerParams(vmem_limit_bytes=4 << 20),
         name="pack_relay",
     )(target, cache)
     relayed = exchanged(relay, [[z * SIDE + i for z in range(PLANES)] for i in range(SIDE)])
@@ -396,12 +398,13 @@
         out_specs=ANY,
         scratch_shapes=[pltpu.SemaphoreType.DMA],
         input_output_aliases={1: 0},
+        compiler_params=pltpu.CompilerParams(vmem_limit_bytes=2 << 20),
         name="pack_tiles",
     )(tiles, packed)
     direct = exchanged(packed)
 
     codes = relayed[:, RELAY * LEVELS, : 2 * RELAY].astype(jnp.int32)
-    shifts = [(dy, dc) for dy in range(4) for dc in range(2)]
+    shifts = [(0, 0), (1, 0), (3, 0), (2, 0), (2, 1), (1, 1), (3, 1), (0, 1)]
     onto = jnp.stack([lax.rem(y + dy, 4) * 2 + (core ^ dc) for dy, dc in shifts])
     came = jnp.stack([lax.rem(y - dy + 4, 4) * 2 + (core ^ dc) for dy, dc in shifts])
     onward = pl.pallas_call(
@@ -419,6 +422,7 @@
             pltpu.SemaphoreType.DMA,
         ],
         cost_estimate=pl.CostEstimate(flops=0, bytes_accessed=5 << 20, transcendentals=0),
+        compiler_params=pltpu.CompilerParams(vmem_limit_bytes=4 << 20),
         name="pack_plane",
     )(codes, onto.astype(jnp.int32), relayed)
     def in_plane(x, k):
@@ -439,6 +443,7 @@
         out_shape=jax.ShapeDtypeStruct((1,), jnp.int32),
         in_specs=[pl.BlockSpec((8, 128), lambda t: (LAST // 8 - 1, 0))] * SIDE,
         out_specs=SMEM,
+        compiler_params=pltpu.CompilerParams(vmem_limit_bytes=2 << 20),
         name="flag",
     )(*lasts)
 
@@ -464,6 +469,7 @@
             pl.BlockSpec((2 * SIDE, ROWS), lambda t: (0, 0)),
             pl.BlockSpec((OUTCOMES, ROWS), lambda t: (0, 0)),
         ),
+        compiler_params=pltpu.CompilerParams(vmem_limit_bytes=4 << 20),
         name="plane_sum",
     )(direct)
     other = lax.ppermute(piece, "sample", xor_pairs(PEERS, 1))
@@ -473,7 +479,7 @@
     direct, lasts, piece = lax.optimization_barrier((direct, lasts, piece))
     lasts = lax.cond(over[0] > 0, by_pairs, by_relay, lasts)
     piece, lasts = lax.optimization_barrier((piece, lasts))
-    shares = jnp.stack([piece] + [in_plane(piece, k) for k in range(2, SIDE, 2)])
+    shares = jnp.stack([piece] + [in_plane(piece, shifts.index((dy, 0))) for dy in (1, 2, 3)])
     rows_y = jnp.arange(4, dtype=jnp.int32)
     ours = (lax.rem(y - rows_y + 4, 4)[:, None] == rows_y[None, :])[..., None, None]
     grad_out = jnp.sum(jnp.where(ours, shares[None], 0.0), 1).reshape(ROWS, ROWS)

time: 162 us -> 159 us (0.981)
  starting transfers between devices: 44.2 us -> 56 us
  waiting for transfers between devices: 66.7 us -> 57.4 us
  other arithmetic: 8.31 us -> 3.37 us
  local copies, waits for them, and re-layouts: 11.3 us -> 8.25 us
  matrix products: 1.84 us -> 3.95 us
    all_to_all x2, waiting for transfers between devices: 52 us -> 26.4 us  [exchanged(): lax.all_to_all(x, 'sample', split_axis=0, concat_axis=0, tiled=True, axis...]
    ppermute x10, waiting for transfers between devices: 9.73 us -> 26.6 us  [in_plane(): return lax.ppermute(x, 'sample', pairs)]
    ppermute x10, starting transfers between devices: 15.4 us -> 27.4 us  [in_plane(): return lax.ppermute(x, 'sample', pairs)]
    unnamed x31 -> x23, local copies, waits for them, and re-layouts: 7.59 us -> 5.1 us
  transfers between devices with their start and end apart: 20 -> 20, of which waited for: 7 -> 8; matrix products, arithmetic and copies ran while one was open for 12% -> 9% of each run, Pallas kernels for 13% -> 14%
where the time goes in v6:
time: 159 us; the launch traced here: 158 us
  waiting for transfers between devices  57.4 us (36%)
  starting transfers between devices  56 us (35%)
  Pallas kernels  26.9 us (17%)
  local copies, waits for them, and re-layouts  8.25 us (5%)
  matrix products  3.95 us (2%)
  other arithmetic  3.37 us (2%)
  between operations  1.87 us (1%)
    ppermute x10, starting transfers between devices, in_plane(): return lax.ppermute(x, 'sample', pairs)  27.4 us
    ppermute x10, waiting for transfers between devices, in_plane(): return lax.ppermute(x, 'sample', pairs)  26.6 us
    all_to_all x2, waiting for transfers between devices, exchanged(): lax.all_to_all(x, 'sample', split_axis=0, concat_axis=0, tiled=True, axis...  26.4 us
    all_to_all x2, starting transfers between devices, exchanged(): lax.all_to_all(x, 'sample', split_axis=0, concat_axis=0, tiled=True, axis...  17 us
    ppermute x7, starting transfers between devices, tree_sum(): terms = [x] + [lax.ppermute(x, axis, xor_pairs(size, bit)) for bit in bits]  9.84 us
    pallas_call x1, Pallas kernels, settle(): pl.pallas_call(settle_kernel, grid=(PLANES,), out_shape=(jax.ShapeDtypeSt...  8.13 us
    pallas_call x1, Pallas kernels, on_device(): pl.pallas_call(relay_kernel, out_shape=jax.ShapeDtypeStruct((PLANES, PIEC...  5.56 us
    pallas_call x1, Pallas kernels, on_device(): pl.pallas_call(forward_kernel, out_shape=[jax.ShapeDtypeStruct((LAST, WID...  5.52 us
  transfers between devices with their start and end apart: 20, of which 8 were waited for; matrix products, arithmetic and copies ran while one was open for 9% of the time, Pallas kernels for 14%

profile of v6, /device:TPU:1, one launch (start us, length us, event | category | flops | bytes accessed | tf_op | source)
XLA Modules:
  0.0 157.8 jit_solution(11278749638515654853)
XLA Ops:
  0.6 5.6 %pack_relay.1 = bf16[8,392,256]{2,1,0:T(8,128)(2,1)} custom-call(s32[128]{0:T(128)} %bitcast.109, bf16[128,48,256]{2,1,0:T(8,128)(2,1)} %cache.3), custom_call_target="tpu_custom_call" | custom-call | tf_op jit(solution)/shard_map/pack_relay/pallas_call | solution.py:347
  6.2 9.3 %all-to-all-start.2 = ((bf16[8,392,256]{2,1,0:T(8,128)(2,1)}), bf16[8,392,256]{2,1,0:T(8,128)(2,1)}, u32[]{:S(2)}, u32[]{:S(2)}) async-start(bf16[8,392,256]{2,1,0:T(8,128)(2,1)} %pack_relay.1), calls=%async_computation.2 | async-start | bytes 3211264 | tf_op jit(solution)/shard_map/all_to_all | solution.py:317
  15.5 2.2 %fusion.39 = (bf16[128,48,128]{2,1,0:T(8,128)(2,1)}, bf16[128,48,128]{2,1,0:T(8,128)(2,1)}) fusion(bf16[128,48,256]{2,1,0:T(8,128)(2,1)S(1)} %copy-done.2), kind=kLoop, calls=%fused_computation.99 | loop fusion | bytes 6291456 | tf_op jit(solution)/shard_map/slice | solution.py:43
  17.7 2.1 %copy.61 = bf16[128,48,128]{0,2,1:T(8,128)(2,1)S(1)} copy(bf16[128,48,128]{2,1,0:T(8,128)(2,1)} %get-tuple-element.145) | data formatting | bytes 3145728
  19.9 0.1 fusion.12
  20.0 2.1 %copy.60 = bf16[128,48,128]{0,2,1:T(8,128)(2,1)S(1)} copy(bf16[128,48,128]{2,1,0:T(8,128)(2,1)} %get-tuple-element.144) | data formatting | bytes 3145728
  22.2 0.2 bitcast_convert_fusion
  22.5 0.2 convolution_convert_fusion.2
  22.7 0.6 multiply_reduce_fusion.1
  23.3 0.1 reduce_max.19
  23.5 0.2 convolution_convert_fusion.1
  23.8 0.4 multiply_reduce_fusion
  24.2 0.9 fusion.9
  25.2 0.1 fusion.40
  25.4 0.9 fusion.26
  26.3 0.8 fusion.25
  27.1 0.2 fusion.41
  27.3 2.9 %collective-permute-start.1 = (f32[132,128]{1,0:T(8,128)S(1)}, f32[132,128]{1,0:T(8,128)S(1)}, u32[]{:S(2)}, u32[]{:S(2)}) collective-permute-start(f32[132,128]{1,0:T(8,128)S(1)} %pad_maximum_fusion.1), channel_id=1, source_target_pairs={{0,2},{1,3},{2,0},{3,1},{4,6},{5,7},{6,4},{7,5},{8,10},{9,11},{10,... | collective-permute-start | bytes 202760 | tf_op jit(solution)/shard_map/ppermute | solution.py:327
  30.2 0.8 collective-permute-start.2
  31.1 4.8 %pack_direct.3.rows = bf16[64,104,256]{2,1,0:T(8,128)(2,1)} custom-call(s32[128]{0:T(128)S(1)} %bitcast.110, bf16[128,48,256]{2,1,0:T(8,128)(2,1)} %cache.3), custom_call_target="tpu_custom_call" | custom-call | bytes 10485760 | tf_op jit(solution)/shard_map/pack_direct/pallas_call | solution.py:300
  35.9 0.1 convert_reduce_fusion
  36.0 3.0 %collective-permute-start.4 = (f32[132,128]{1,0:T(8,128)S(1)}, f32[132,128]{1,0:T(8,128)S(1)}, u32[]{:S(2)}, u32[]{:S(2)}) collective-permute-start(f32[132,128]{1,0:T(8,128)S(1)} %add_add_fusion.1), channel_id=1, source_target_pairs={{0,16},{4,20},{8,24},{12,28},{16,0},{20,4},{24,8},{28,12},{32,48},... | collective-permute-start | bytes 202760 | tf_op jit(solution)/shard_map/ppermute | solution.py:327
  39.1 0.7 collective-permute-start.5
  39.8 0.1 concatenate.21
  39.9 1.3 collective-permute-done.4
  41.2 2.7 %collective-permute-done.5 = f32[132,128]{1,0:T(8,128)S(1)} collective-permute-done((f32[132,128]{1,0:T(8,128)S(1)}, f32[132,128]{1,0:T(8,128)S(1)}, u32[]{:S(2)}, u32[]{:S(2)}) %collective-permute-start.5) | collective-permute-done | bytes 67616 | tf_op jit(solution)/shard_map/ppermute | solution.py:327
  43.9 0.2 collective-permute-done.3
  44.1 2.3 %collective-permute-start.6 = (f32[132,128]{1,0:T(8,128)S(1)}, f32[132,128]{1,0:T(8,128)S(1)}, u32[]{:S(2)}, u32[]{:S(2)}) collective-permute-start(f32[132,128]{1,0:T(8,128)S(1)} %add_add_fusion), channel_id=1, source_target_pairs={{0,4},{4,0},{8,12},{12,8},{16,20},{20,16},{24,28},{28,24},{32,36},... | collective-permute-start | bytes 202760 | tf_op jit(solution)/shard_map/ppermute | solution.py:327
  46.5 0.2 convolution_convert_fusion
  46.7 0.1 copy.41
  46.9 0.1 reshape.205
  47.0 0.1 copy.40
  47.1 0.1 pad.19.clone
  47.2 0.2 collective-permute-done.6
  47.5 0.1 reshape.206
  47.6 0.1 pad_maximum_fusion.4
  47.7 0.1 copy.45
  47.8 0.2 pad_maximum_fusion.tiles
  48.0 0.7 pack_tiles.1
  48.7 5.7 %all-to-all-done.2.got = bf16[8,392,256]{2,1,0:T(8,128)(2,1)} async-done(((bf16[8,392,256]{2,1,0:T(8,128)(2,1)}), bf16[8,392,256]{2,1,0:T(8,128)(2,1)}, u32[]{:S(2)}, u32[]{:S(2)}) %all-to-all-start.2) | async-done | bytes 1605664 | tf_op jit(solution)/shard_map/all_to_all | solution.py:317
  54.5 7.8 %all-to-all-start.1 = ((bf16[64,104,256]{2,1,0:T(8,128)(2,1)}), bf16[64,104,256]{2,1,0:T(8,128)(2,1)S(1)}, u32[]{:S(2)}, u32[]{:S(2)}) async-start(bf16[64,104,256]{2,1,0:T(8,128)(2,1)} %pack_tiles.1), calls=%async_computation.1 | async-start | bytes 6815744 | tf_op jit(solution)/shard_map/all_to_all | solution.py:317
  62.3 0.1 stack.75.side
  62.4 0.7 slice_convert_fusion
  63.1 5.5 %pack_plane.1 = (bf16[776,256]{1,0:T(8,128)(2,1)}, bf16[776,256]{1,0:T(8,128)(2,1)S(1)}, bf16[776,256]{1,0:T(8,128)(2,1)S(1)}, bf16[776,256]{1,0:T(8,128)(2,1)},...) custom-call(s32[8,16]{1,0:T(8,128)S(1)} %bitcast.93, ...), custom_call_target="tpu_custom_call" | custom-call | bytes 5242880 | tf_op jit(solution)/shard_map/pack_plane/pallas_call | solution.py:410
  68.6 1.5 collective-permute-start.7
  70.1 1.3 collective-permute-start.8
  71.4 1.7 %collective-permute-start.9 = (bf16[776,256]{1,0:T(8,128)(2,1)}, bf16[776,256]{1,0:T(8,128)(2,1)}, u32[]{:S(2)}, u32[]{:S(2)}) collective-permute-start(bf16[776,256]{1,0:T(8,128)(2,1)} %get-tuple-element.100), channel_id=1, source_target_pairs={{0,16},{4,20},{8,24},{12,28},{16,0},{20,4},{24,8},{28,12},{32,48},... | collective-permute-start | bytes 1191944 | tf_op jit(solution)/shard_map/ppermute | solution.py:436
  73.1 2.5 %collective-permute-start.10 = (bf16[776,256]{1,0:T(8,128)(2,1)}, bf16[776,256]{1,0:T(8,128)(2,1)}, u32[]{:S(2)}, u32[]{:S(2)}) collective-permute-start(bf16[776,256]{1,0:T(8,128)(2,1)} %get-tuple-element.101), channel_id=1, source_target_pairs={{0,20},{4,16},{8,28},{12,24},{16,4},{20,0},{24,12},{28,8},{32,52},... | collective-permute-start | bytes 1191944 | tf_op jit(solution)/shard_map/ppermute | solution.py:436
  75.6 10.0 %collective-permute-done.7.refs_1_ = bf16[776,256]{1,0:T(8,128)(2,1)S(1)} collective-permute-done((bf16[776,256]{1,0:T(8,128)(2,1)S(1)}, bf16[776,256]{1,0:T(8,128)(2,1)S(1)}, u32[]{:S(2)}, u32[]{:S(2)}) %collective-permute-start.7) | collective-permute-done | bytes 397344 | tf_op jit(solution)/shard_map/ppermute | solution.py:436
  85.6 4.1 %collective-permute-start.12 = (bf16[776,256]{1,0:T(8,128)(2,1)}, bf16[776,256]{1,0:T(8,128)(2,1)}, u32[]{:S(2)}, u32[]{:S(2)}) collective-permute-start(bf16[776,256]{1,0:T(8,128)(2,1)} %get-tuple-element.103), channel_id=1, source_target_pairs={{0,28},{4,24},{8,4},{12,0},{16,12},{20,8},{24,20},{28,16},{32,60},... | collective-permute-start | bytes 1191944 | tf_op jit(solution)/shard_map/ppermute | solution.py:436
  89.7 16.6 %collective-permute-done.8.refs_2_ = bf16[776,256]{1,0:T(8,128)(2,1)S(1)} collective-permute-done((bf16[776,256]{1,0:T(8,128)(2,1)S(1)}, bf16[776,256]{1,0:T(8,128)(2,1)S(1)}, u32[]{:S(2)}, u32[]{:S(2)}) %collective-permute-start.8) | collective-permute-done | bytes 397344 | tf_op jit(solution)/shard_map/ppermute | solution.py:436
  106.3 0.7 copy-done.5
  107.0 12.8 %collective-permute-start.13 = (bf16[776,256]{1,0:T(8,128)(2,1)}, bf16[776,256]{1,0:T(8,128)(2,1)}, u32[]{:S(2)}, u32[]{:S(2)}) collective-permute-start(bf16[776,256]{1,0:T(8,128)(2,1)} %get-tuple-element.104), channel_id=1, source_target_pairs={{0,4},{4,0},{8,12},{12,8},{16,20},{20,16},{24,28},{28,24},{32,36},... | collective-permute-start | bytes 1191944 | tf_op jit(solution)/shard_map/ppermute | solution.py:436
  119.8 20.6 %all-to-all-done.1.tiles.direct = bf16[64,104,256]{2,1,0:T(8,128)(2,1)S(1)} async-done(((bf16[64,104,256]{2,1,0:T(8,128)(2,1)}), bf16[64,104,256]{2,1,0:T(8,128)(2,1)S(1)}, u32[]{:S(2)}, u32[]{:S(2)}) %all-to-all-start.1) | async-done | bytes 3407904 | tf_op jit(solution)/shard_map/all_to_all | solution.py:317
  140.4 0.8 plane_sum.1
  141.2 1.8 %collective-permute-start.14 = (f32[16,128]{1,0:T(8,128)S(1)}, f32[16,128]{1,0:T(8,128)S(1)}, u32[]{:S(2)}, u32[]{:S(2)}) collective-permute-start(f32[16,128]{1,0:T(8,128)S(1)} %get-tuple-element.105), channel_id=1, source_target_pairs={{0,4},{4,0},{8,12},{12,8},{16,20},{20,16},{24,28},{28,24},{32,36},... | collective-permute-start | bytes 24584 | tf_op jit(solution)/shard_map/ppermute | solution.py:475
  143.0 0.1 iota_compare_fusion.3
  143.1 0.1 stack.71.side
  143.2 1.4 flag.1
  145.3 2.4 %collective-permute-start.17 = (f32[32,128]{1,0:T(8,128)S(1)}, f32[32,128]{1,0:T(8,128)S(1)}, u32[]{:S(2)}, u32[]{:S(2)}) collective-permute-start(f32[32,128]{1,0:T(8,128)S(1)} %maximum_select_fusion), channel_id=1, source_target_pairs={{0,24},{4,28},{8,0},{12,4},{16,8},{20,12},{24,16},{28,20},{32,56},... | collective-permute-start | bytes 49160 | tf_op jit(solution)/shard_map/ppermute | solution.py:436
  147.7 0.5 collective-permute-start.16
  148.3 0.6 collective-permute-start.15
  148.9 8.1 %settle.1 = (bf16[49,256,256]{2,1,0:T(8,128)(2,1)}, f32[4,256]{1,0:T(4,128)}) custom-call(s32[8]{0:T(128)S(1)} %stack.71.side, bf16[64,104,256]{2,1,0:T(8,128)(2,1)S(1)} %all-to-all-done.1.tiles.direct, bf16[776,256]{1,0:T(8,128)(2,1)} %get-tuple-element.124.refs_0_, bf16[776,256]{1,0:T(8,128)(2,1)} %get-tuple-element.125.refs_1_, ...), custom_call_target="tpu_custom_call" | custom-call | flops 2147483648 | bytes 14680064 | tf_op jit(solution)/shard_map/settle/pallas_call | solution.py:276
  157.0 0.7 select_reduce_fusion
  (68 shorter events, 0.6 us)
Async XLA Ops:
  0.6 21.5 %copy-start = (bf16[128,128]{1,0:T(8,128)(2,1)S(1)}, bf16[128,128]{1,0:T(8,128)(2,1)}, u32[]{:S(2)}) copy-start(bf16[128,128]{1,0:T(8,128)(2,1)} %param.16) | copy-start | bytes 98308
  6.2 9.3 %copy-start.2 = (bf16[128,48,256]{2,1,0:T(8,128)(2,1)S(1)}, bf16[128,48,256]{2,1,0:T(8,128)(2,1)}, u32[]{:S(2)}) copy-start(bf16[128,48,256]{2,1,0:T(8,128)(2,1)} %cache.3) | copy-start | bytes 9437188
  6.2 48.3 %all-to-all-start.2 = ((bf16[8,392,256]{2,1,0:T(8,128)(2,1)}), bf16[8,392,256]{2,1,0:T(8,128)(2,1)}, u32[]{:S(2)}, u32[]{:S(2)}) async-start(bf16[8,392,256]{2,1,0:T(8,128)(2,1)} %pack_relay.1), calls=%async_computation.2 | async-start | bytes 3211264 | tf_op jit(solution)/shard_map/all_to_all | solution.py:317
  17.7 2.2 %copy-start.3 = (bf16[128,128]{1,0:T(8,128)(2,1)S(1)}, bf16[128,128]{1,0:T(8,128)(2,1)}, u32[]{:S(2)}) copy-start(bf16[128,128]{1,0:T(8,128)(2,1)} %param.13) | copy-start | bytes 98308
  17.7 4.4 %copy-start.8 = (f32[128]{0:T(128)S(1)}, f32[128]{0:T(128)}, u32[]{:S(2)}) copy-start(f32[128]{0:T(128)} %param.15) | copy-start | bytes 1540
  17.7 4.7 %copy-start.6 = (bf16[128,128]{1,0:T(8,128)(2,1)S(1)}, bf16[128,128]{1,0:T(8,128)(2,1)}, u32[]{:S(2)}) copy-start(bf16[128,128]{1,0:T(8,128)(2,1)} %param.17) | copy-start | bytes 98308
  19.9 3.6 %copy-start.7 = (bf16[128,128]{1,0:T(8,128)(2,1)S(1)}, bf16[128,128]{1,0:T(8,128)(2,1)}, u32[]{:S(2)}) copy-start(bf16[128,128]{1,0:T(8,128)(2,1)} %param.18) | copy-start | bytes 98308
  22.2 3.0 %copy-start.10 = (bf16[128,4]{0,1:T(4,128)(2,1)S(1)}, bf16[128,4]{0,1:T(4,128)(2,1)}, u32[]{:S(2)}) copy-start(bf16[128,4]{0,1:T(4,128)(2,1)} %param.20) | copy-start | bytes 3076
  22.2 8.9 %copy-start.9 = (s32[128,1]{0,1:T(1,128)S(1)}, s32[128,1]{0,1:T(1,128)}, u32[]{:S(2)}) copy-start(s32[128,1]{0,1:T(1,128)} %param.23) | copy-start | bytes 1540
  27.3 8.6 %collective-permute-start.1 = (f32[132,128]{1,0:T(8,128)S(1)}, f32[132,128]{1,0:T(8,128)S(1)}, u32[]{:S(2)}, u32[]{:S(2)}) collective-permute-start(f32[132,128]{1,0:T(8,128)S(1)} %pad_maximum_fusion.1), channel_id=1, source_target_pairs={{0,2},{1,3},{2,0},{3,1},{4,6},{5,7},{6,4},{7,5},{8,10},{9,11},{10,... | collective-permute-start | bytes 202760 | tf_op jit(solution)/shard_map/ppermute | solution.py:327
  30.2 5.8 %collective-permute-start.2 = (f32[132,128]{1,0:T(8,128)S(1)}, f32[132,128]{1,0:T(8,128)S(1)}, u32[]{:S(2)}, u32[]{:S(2)}) collective-permute-start(f32[132,128]{1,0:T(8,128)S(1)} %pad_maximum_fusion.1), channel_id=1, source_target_pairs={{0,3},{1,2},{2,1},{3,0},{4,7},{5,6},{6,5},{7,4},{8,11},{9,10},{10,... | collective-permute-start | bytes 202760 | tf_op jit(solution)/shard_map/ppermute | solution.py:327
  31.1 5.0 %collective-permute-start = (f32[132,128]{1,0:T(8,128)S(1)}, f32[132,128]{1,0:T(8,128)S(1)}, u32[]{:S(2)}, u32[]{:S(2)}) collective-permute-start(f32[132,128]{1,0:T(8,128)S(1)} %pad_maximum_fusion.1), channel_id=1, source_target_pairs={{0,1},{1,0},{2,3},{3,2},{4,5},{5,4},{6,7},{7,6},{8,9},{9,8},{10,11... | collective-permute-start | bytes 202760 | tf_op jit(solution)/shard_map/ppermute | solution.py:327
  36.0 5.2 %collective-permute-start.4 = (f32[132,128]{1,0:T(8,128)S(1)}, f32[132,128]{1,0:T(8,128)S(1)}, u32[]{:S(2)}, u32[]{:S(2)}) collective-permute-start(f32[132,128]{1,0:T(8,128)S(1)} %add_add_fusion.1), channel_id=1, source_target_pairs={{0,16},{4,20},{8,24},{12,28},{16,0},{20,4},{24,8},{28,12},{32,48},... | collective-permute-start | bytes 202760 | tf_op jit(solution)/shard_map/ppermute | solution.py:327
  39.1 4.8 %collective-permute-start.5 = (f32[132,128]{1,0:T(8,128)S(1)}, f32[132,128]{1,0:T(8,128)S(1)}, u32[]{:S(2)}, u32[]{:S(2)}) collective-permute-start(f32[132,128]{1,0:T(8,128)S(1)} %add_add_fusion.1), channel_id=1, source_target_pairs={{0,24},{4,28},{8,16},{12,20},{16,8},{20,12},{24,0},{28,4},{32,56},... | collective-permute-start | bytes 202760 | tf_op jit(solution)/shard_map/ppermute | solution.py:327
  39.8 4.3 %collective-permute-start.3 = (f32[132,128]{1,0:T(8,128)S(1)}, f32[132,128]{1,0:T(8,128)S(1)}, u32[]{:S(2)}, u32[]{:S(2)}) collective-permute-start(f32[132,128]{1,0:T(8,128)S(1)} %add_add_fusion.1), channel_id=1, source_target_pairs={{0,8},{4,12},{8,0},{12,4},{16,24},{20,28},{24,16},{28,20},{32,40},... | collective-permute-start | bytes 202760 | tf_op jit(solution)/shard_map/ppermute | solution.py:327
  44.1 3.3 %collective-permute-start.6 = (f32[132,128]{1,0:T(8,128)S(1)}, f32[132,128]{1,0:T(8,128)S(1)}, u32[]{:S(2)}, u32[]{:S(2)}) collective-permute-start(f32[132,128]{1,0:T(8,128)S(1)} %add_add_fusion), channel_id=1, source_target_pairs={{0,4},{4,0},{8,12},{12,8},{16,20},{20,16},{24,28},{28,24},{32,36},... | collective-permute-start | bytes 202760 | tf_op jit(solution)/shard_map/ppermute | solution.py:327
  54.5 85.9 %all-to-all-start.1 = ((bf16[64,104,256]{2,1,0:T(8,128)(2,1)}), bf16[64,104,256]{2,1,0:T(8,128)(2,1)S(1)}, u32[]{:S(2)}, u32[]{:S(2)}) async-start(bf16[64,104,256]{2,1,0:T(8,128)(2,1)} %pack_tiles.1), calls=%async_computation.1 | async-start | bytes 6815744 | tf_op jit(solution)/shard_map/all_to_all | solution.py:317
  68.6 17.0 %collective-permute-start.7 = (bf16[776,256]{1,0:T(8,128)(2,1)S(1)}, bf16[776,256]{1,0:T(8,128)(2,1)S(1)}, u32[]{:S(2)}, u32[]{:S(2)}) collective-permute-start(bf16[776,256]{1,0:T(8,128)(2,1)S(1)} %get-tuple-element.98), channel_id=1, source_target_pairs={{0,8},{4,12},{8,16},{12,20},{16,24},{20,28},{24,0},{28,4},{32,40},... | collective-permute-start | bytes 1191944 | tf_op jit(solution)/shard_map/ppermute | solution.py:436
  70.1 36.2 %collective-permute-start.8 = (bf16[776,256]{1,0:T(8,128)(2,1)S(1)}, bf16[776,256]{1,0:T(8,128)(2,1)S(1)}, u32[]{:S(2)}, u32[]{:S(2)}) collective-permute-start(bf16[776,256]{1,0:T(8,128)(2,1)S(1)} %get-tuple-element.99), channel_id=1, source_target_pairs={{0,24},{4,28},{8,0},{12,4},{16,8},{20,12},{24,16},{28,20},{32,56},... | collective-permute-start | bytes 1191944 | tf_op jit(solution)/shard_map/ppermute | solution.py:436
  71.4 69.8 %collective-permute-start.9 = (bf16[776,256]{1,0:T(8,128)(2,1)}, bf16[776,256]{1,0:T(8,128)(2,1)}, u32[]{:S(2)}, u32[]{:S(2)}) collective-permute-start(bf16[776,256]{1,0:T(8,128)(2,1)} %get-tuple-element.100), channel_id=1, source_target_pairs={{0,16},{4,20},{8,24},{12,28},{16,0},{20,4},{24,8},{28,12},{32,48},... | collective-permute-start | bytes 1191944 | tf_op jit(solution)/shard_map/ppermute | solution.py:436
  73.1 70.1 %collective-permute-start.10 = (bf16[776,256]{1,0:T(8,128)(2,1)}, bf16[776,256]{1,0:T(8,128)(2,1)}, u32[]{:S(2)}, u32[]{:S(2)}) collective-permute-start(bf16[776,256]{1,0:T(8,128)(2,1)} %get-tuple-element.101), channel_id=1, source_target_pairs={{0,20},{4,16},{8,28},{12,24},{16,4},{20,0},{24,12},{28,8},{32,52},... | collective-permute-start | bytes 1191944 | tf_op jit(solution)/shard_map/ppermute | solution.py:436
  75.6 67.6 %collective-permute-start.11 = (bf16[776,256]{1,0:T(8,128)(2,1)}, bf16[776,256]{1,0:T(8,128)(2,1)}, u32[]{:S(2)}, u32[]{:S(2)}) collective-permute-start(bf16[776,256]{1,0:T(8,128)(2,1)} %get-tuple-element.102), channel_id=1, source_target_pairs={{0,12},{4,8},{8,20},{12,16},{16,28},{20,24},{24,4},{28,0},{32,44},... | collective-permute-start | bytes 1191944 | tf_op jit(solution)/shard_map/ppermute | solution.py:436
  85.6 20.7 %copy-start.4 = (bf16[776,256]{1,0:T(8,128)(2,1)}, bf16[776,256]{1,0:T(8,128)(2,1)S(1)}, u32[]{:S(2)}) copy-start(bf16[776,256]{1,0:T(8,128)(2,1)S(1)} %collective-permute-done.7.refs_1_) | copy-start | bytes 1191940
  85.6 57.6 %collective-permute-start.12 = (bf16[776,256]{1,0:T(8,128)(2,1)}, bf16[776,256]{1,0:T(8,128)(2,1)}, u32[]{:S(2)}, u32[]{:S(2)}) collective-permute-start(bf16[776,256]{1,0:T(8,128)(2,1)} %get-tuple-element.103), channel_id=1, source_target_pairs={{0,28},{4,24},{8,4},{12,0},{16,12},{20,8},{24,20},{28,16},{32,60},... | collective-permute-start | bytes 1191944 | tf_op jit(solution)/shard_map/ppermute | solution.py:436
  106.3 0.7 copy-start.5
  107.0 36.2 %collective-permute-start.13 = (bf16[776,256]{1,0:T(8,128)(2,1)}, bf16[776,256]{1,0:T(8,128)(2,1)}, u32[]{:S(2)}, u32[]{:S(2)}) collective-permute-start(bf16[776,256]{1,0:T(8,128)(2,1)} %get-tuple-element.104), channel_id=1, source_target_pairs={{0,4},{4,0},{8,12},{12,8},{16,20},{20,16},{24,28},{28,24},{32,36},... | collective-permute-start | bytes 1191944 | tf_op jit(solution)/shard_map/ppermute | solution.py:436
  141.2 4.0 %collective-permute-start.14 = (f32[16,128]{1,0:T(8,128)S(1)}, f32[16,128]{1,0:T(8,128)S(1)}, u32[]{:S(2)}, u32[]{:S(2)}) collective-permute-start(f32[16,128]{1,0:T(8,128)S(1)} %get-tuple-element.105), channel_id=1, source_target_pairs={{0,4},{4,0},{8,12},{12,8},{16,20},{20,16},{24,28},{28,24},{32,36},... | collective-permute-start | bytes 24584 | tf_op jit(solution)/shard_map/ppermute | solution.py:475
  145.3 11.7 %collective-permute-start.17 = (f32[32,128]{1,0:T(8,128)S(1)}, f32[32,128]{1,0:T(8,128)S(1)}, u32[]{:S(2)}, u32[]{:S(2)}) collective-permute-start(f32[32,128]{1,0:T(8,128)S(1)} %maximum_select_fusion), channel_id=1, source_target_pairs={{0,24},{4,28},{8,0},{12,4},{16,8},{20,12},{24,16},{28,20},{32,56},... | collective-permute-start | bytes 49160 | tf_op jit(solution)/shard_map/ppermute | solution.py:436
  147.7 9.3 %collective-permute-start.16 = (f32[32,128]{1,0:T(8,128)S(1)}, f32[32,128]{1,0:T(8,128)S(1)}, u32[]{:S(2)}, u32[]{:S(2)}) collective-permute-start(f32[32,128]{1,0:T(8,128)S(1)} %maximum_select_fusion), channel_id=1, source_target_pairs={{0,16},{4,20},{8,24},{12,28},{16,0},{20,4},{24,8},{28,12},{32,48},... | collective-permute-start | bytes 49160 | tf_op jit(solution)/shard_map/ppermute | solution.py:436
  148.3 8.7 %collective-permute-start.15 = (f32[32,128]{1,0:T(8,128)S(1)}, f32[32,128]{1,0:T(8,128)S(1)}, u32[]{:S(2)}, u32[]{:S(2)}) collective-permute-start(f32[32,128]{1,0:T(8,128)S(1)} %maximum_select_fusion), channel_id=1, source_target_pairs={{0,8},{4,12},{8,16},{12,20},{16,24},{20,28},{24,0},{28,4},{32,40},... | collective-permute-start | bytes 49160 | tf_op jit(solution)/shard_map/ppermute | solution.py:436

commit v7 on v6

--- a/solution.py
+++ b/solution.py
@@ -79,8 +79,7 @@
 
 
 def cleared(ref, count):
-    @pl.loop(0, count)
-    def _(i):
+    for i in range(count):
         ref[i] = 0
 
 
@@ -90,7 +89,7 @@
     meta[...] = jnp.full(meta.shape, -1.0, jnp.float32)
     lane = lax.broadcasted_iota(jnp.int32, (8, WIDTH), 1)
 
-    @pl.loop(0, ROWS)
+    @pl.loop(0, ROWS, unroll=8)
     def _(i):
         d = dest[i]
         rank = count[d]
@@ -457,6 +456,7 @@
         high = jnp.pad(high, ((0, 0), (0, LAST - 2 * PLANES * LEVELS), (0, 0)))
         return [lax.dynamic_index_in_dim(high, came[k], 0, keepdims=False) for k in range(SIDE)]
 
+    direct, over = lax.optimization_barrier((direct, over))
     piece, head = pl.pallas_call(
         plane_sum_kernel,
         grid=(1,),

time: 159 us -> 157 us (0.987)
  starting transfers between devices: 56 us -> 46.6 us
  waiting for transfers between devices: 57.4 us -> 63.1 us
    ppermute x10, waiting for transfers between devices: 26.6 us -> 52.7 us  [in_plane(): return lax.ppermute(x, 'sample', pairs)]
    all_to_all x2, waiting for transfers between devices: 26.4 us -> 6.06 us  [exchanged(): lax.all_to_all(x, 'sample', split_axis=0, concat_axis=0, tiled=True, axis...]
    ppermute x10, starting transfers between devices: 27.4 us -> 18.4 us  [in_plane(): return lax.ppermute(x, 'sample', pairs)]
    pallas_call x1, Pallas kernels: 5.52 us -> 9.08 us  [on_device(): pl.pallas_call(forward_kernel, out_shape=[jax.ShapeDtypeStruct((LAST, WID...]
    unnamed x23 -> x35, local copies, waits for them, and re-layouts: 5.1 us -> 5.21 us
  transfers between devices with their start and end apart: 20 -> 20, of which waited for: 8 -> 10; matrix products, arithmetic and copies ran while one was open for 9% -> 9% of each run, Pallas kernels for 14% -> 15%
where the time goes in v7:
time: 157 us; the launch traced here: 156 us
  waiting for transfers between devices  63.1 us (40%)
  starting transfers between devices  46.6 us (30%)
  Pallas kernels  28.4 us (18%)
  local copies, waits for them, and re-layouts  8.37 us (5%)
  matrix products  3.95 us (3%)
  other arithmetic  3.37 us (2%)
  between operations  1.96 us (1%)
    ppermute x10, waiting for transfers between devices, in_plane(): return lax.ppermute(x, 'sample', pairs)  52.7 us
    ppermute x10, starting transfers between devices, in_plane(): return lax.ppermute(x, 'sample', pairs)  18.4 us
    all_to_all x2, starting transfers between devices, exchanged(): lax.all_to_all(x, 'sample', split_axis=0, concat_axis=0, tiled=True, axis...  17.1 us
    ppermute x7, starting transfers between devices, tree_sum(): terms = [x] + [lax.ppermute(x, axis, xor_pairs(size, bit)) for bit in bits]  9.94 us
    pallas_call x1, Pallas kernels, on_device(): pl.pallas_call(forward_kernel, out_shape=[jax.ShapeDtypeStruct((LAST, WID...  9.08 us
    pallas_call x1, Pallas kernels, settle(): pl.pallas_call(settle_kernel, grid=(PLANES,), out_shape=(jax.ShapeDtypeSt...  8.13 us
    all_to_all x2, waiting for transfers between devices, exchanged(): lax.all_to_all(x, 'sample', split_axis=0, concat_axis=0, tiled=True, axis...  6.06 us
    unnamed x35, local copies, waits for them, and re-layouts  5.21 us
  transfers between devices with their start and end apart: 20, of which 10 were waited for; matrix products, arithmetic and copies ran while one was open for 9% of the time, Pallas kernels for 15%

profile of v7, /device:TPU:1, one launch (start us, length us, event | category | flops | bytes accessed | tf_op | source)
XLA Modules:
  0.0 155.7 jit_solution(6803341210274424061)
XLA Ops:
  0.6 4.5 %pack_relay.1 = bf16[8,392,256]{2,1,0:T(8,128)(2,1)} custom-call(s32[128]{0:T(128)} %bitcast.109, bf16[128,48,256]{2,1,0:T(8,128)(2,1)} %cache.3), custom_call_target="tpu_custom_call" | custom-call | tf_op jit(solution)/shard_map/pack_relay/pallas_call | solution.py:346
  5.2 9.3 %all-to-all-start.2 = ((bf16[8,392,256]{2,1,0:T(8,128)(2,1)}), bf16[8,392,256]{2,1,0:T(8,128)(2,1)}, u32[]{:S(2)}, u32[]{:S(2)}) async-start(bf16[8,392,256]{2,1,0:T(8,128)(2,1)} %pack_relay.1), calls=%async_computation.2 | async-start | bytes 3211264 | tf_op jit(solution)/shard_map/all_to_all | solution.py:316
  14.5 2.2 %fusion.39 = (bf16[128,48,128]{2,1,0:T(8,128)(2,1)}, bf16[128,48,128]{2,1,0:T(8,128)(2,1)}) fusion(bf16[128,48,256]{2,1,0:T(8,128)(2,1)S(1)} %copy-done.2), kind=kLoop, calls=%fused_computation.99 | loop fusion | bytes 6291456 | tf_op jit(solution)/shard_map/slice | solution.py:43
  16.7 2.1 %copy.61 = bf16[128,48,128]{0,2,1:T(8,128)(2,1)S(1)} copy(bf16[128,48,128]{2,1,0:T(8,128)(2,1)} %get-tuple-element.149) | data formatting | bytes 3145728
  18.9 0.1 fusion.12
  19.0 2.1 %copy.60 = bf16[128,48,128]{0,2,1:T(8,128)(2,1)S(1)} copy(bf16[128,48,128]{2,1,0:T(8,128)(2,1)} %get-tuple-element.148) | data formatting | bytes 3145728
  21.2 0.2 bitcast_convert_fusion
  21.5 0.2 convolution_convert_fusion.2
  21.7 0.6 multiply_reduce_fusion.1
  22.5 0.2 convolution_convert_fusion.1
  22.8 0.4 multiply_reduce_fusion
  23.2 0.9 fusion.9
  24.2 0.1 fusion.40
  24.4 0.9 fusion.26
  25.3 0.8 fusion.25
  26.1 0.2 fusion.41
  26.3 2.9 %collective-permute-start.1 = (f32[132,128]{1,0:T(8,128)S(1)}, f32[132,128]{1,0:T(8,128)S(1)}, u32[]{:S(2)}, u32[]{:S(2)}) collective-permute-start(f32[132,128]{1,0:T(8,128)S(1)} %pad_maximum_fusion.1), channel_id=1, source_target_pairs={{0,2},{1,3},{2,0},{3,1},{4,6},{5,7},{6,4},{7,5},{8,10},{9,11},{10,... | collective-permute-start | bytes 202760 | tf_op jit(solution)/shard_map/ppermute | solution.py:326
  29.2 0.8 collective-permute-start.2
  30.0 4.5 %pack_direct.3.rows = bf16[64,104,256]{2,1,0:T(8,128)(2,1)} custom-call(s32[128]{0:T(128)S(1)} %bitcast.110, bf16[128,48,256]{2,1,0:T(8,128)(2,1)} %cache.3), custom_call_target="tpu_custom_call" | custom-call | bytes 10485760 | tf_op jit(solution)/shard_map/pack_direct/pallas_call | solution.py:299
  34.5 0.1 convert_reduce_fusion
  34.6 3.1 %collective-permute-start.4 = (f32[132,128]{1,0:T(8,128)S(1)}, f32[132,128]{1,0:T(8,128)S(1)}, u32[]{:S(2)}, u32[]{:S(2)}) collective-permute-start(f32[132,128]{1,0:T(8,128)S(1)} %add_add_fusion.1), channel_id=1, source_target_pairs={{0,16},{4,20},{8,24},{12,28},{16,0},{20,4},{24,8},{28,12},{32,48},... | collective-permute-start | bytes 202760 | tf_op jit(solution)/shard_map/ppermute | solution.py:326
  37.7 0.8 collective-permute-start.5
  38.5 0.1 concatenate.21
  38.6 1.3 collective-permute-done.4
  39.8 2.7 %collective-permute-done.5 = f32[132,128]{1,0:T(8,128)S(1)} collective-permute-done((f32[132,128]{1,0:T(8,128)S(1)}, f32[132,128]{1,0:T(8,128)S(1)}, u32[]{:S(2)}, u32[]{:S(2)}) %collective-permute-start.5) | collective-permute-done | bytes 67616 | tf_op jit(solution)/shard_map/ppermute | solution.py:326
  42.5 0.1 collective-permute-done.3
  42.7 2.5 %collective-permute-start.6 = (f32[132,128]{1,0:T(8,128)S(1)}, f32[132,128]{1,0:T(8,128)S(1)}, u32[]{:S(2)}, u32[]{:S(2)}) collective-permute-start(f32[132,128]{1,0:T(8,128)S(1)} %add_add_fusion), channel_id=1, source_target_pairs={{0,4},{4,0},{8,12},{12,8},{16,20},{20,16},{24,28},{28,24},{32,36},... | collective-permute-start | bytes 202760 | tf_op jit(solution)/shard_map/ppermute | solution.py:326
  45.1 0.2 convolution_convert_fusion
  45.4 0.1 copy.41
  45.5 0.1 reshape.205
  45.6 0.1 copy.40
  45.8 0.1 pad.19.clone
  45.9 0.2 collective-permute-done.6
  46.2 0.1 reshape.206
  46.3 0.1 pad_maximum_fusion.4
  46.5 0.2 pad_maximum_fusion.tiles
  46.7 0.7 pack_tiles.1
  47.4 6.1 %all-to-all-done.2.got = bf16[8,392,256]{2,1,0:T(8,128)(2,1)} async-done(((bf16[8,392,256]{2,1,0:T(8,128)(2,1)}), bf16[8,392,256]{2,1,0:T(8,128)(2,1)}, u32[]{:S(2)}, u32[]{:S(2)}) %all-to-all-start.2) | async-done | bytes 1605664 | tf_op jit(solution)/shard_map/all_to_all | solution.py:316
  53.5 7.8 %all-to-all-start.1 = ((bf16[64,104,256]{2,1,0:T(8,128)(2,1)}), bf16[64,104,256]{2,1,0:T(8,128)(2,1)S(1)}, u32[]{:S(2)}, u32[]{:S(2)}) async-start(bf16[64,104,256]{2,1,0:T(8,128)(2,1)} %pack_tiles.1), calls=%async_computation.1 | async-start | bytes 6815744 | tf_op jit(solution)/shard_map/all_to_all | solution.py:316
  61.3 0.1 stack.75.side
  61.4 0.7 slice_convert_fusion
  62.1 9.1 %pack_plane.1 = (bf16[776,256]{1,0:T(8,128)(2,1)S(1)}, bf16[776,256]{1,0:T(8,128)(2,1)S(1)}, bf16[776,256]{1,0:T(8,128)(2,1)S(1)}, bf16[776,256]{1,0:T(8,128)(2,...) custom-call(s32[8,16]{1,0:T(8,128)S(1)} %bitcast.93, ...), custom_call_target="tpu_custom_call" | custom-call | bytes 5242880 | tf_op jit(solution)/shard_map/pack_plane/pallas_call | solution.py:409
  71.2 1.5 collective-permute-start.7
  72.7 1.3 collective-permute-start.8
  74.0 1.7 %collective-permute-start.9 = (bf16[776,256]{1,0:T(8,128)(2,1)S(1)}, bf16[776,256]{1,0:T(8,128)(2,1)S(1)}, u32[]{:S(2)}, u32[]{:S(2)}) collective-permute-start(bf16[776,256]{1,0:T(8,128)(2,1)S(1)} %get-tuple-element.102), channel_id=1, source_target_pairs={{0,16},{4,20},{8,24},{12,28},{16,0},{20,4},{24,8},{28,12},{32,48},... | collective-permute-start | bytes 1191944 | tf_op jit(solution)/shard_map/ppermute | solution.py:435
  75.7 2.5 %collective-permute-start.10 = (bf16[776,256]{1,0:T(8,128)(2,1)S(1)}, bf16[776,256]{1,0:T(8,128)(2,1)S(1)}, u32[]{:S(2)}, u32[]{:S(2)}) collective-permute-start(bf16[776,256]{1,0:T(8,128)(2,1)S(1)} %get-tuple-element.103), channel_id=1, source_target_pairs={{0,20},{4,16},{8,28},{12,24},{16,4},{20,0},{24,12},{28,8},{32,52},... | collective-permute-start | bytes 1191944 | tf_op jit(solution)/shard_map/ppermute | solution.py:435
  78.1 12.4 %collective-permute-done.7.refs_1_ = bf16[776,256]{1,0:T(8,128)(2,1)S(1)} collective-permute-done((bf16[776,256]{1,0:T(8,128)(2,1)S(1)}, bf16[776,256]{1,0:T(8,128)(2,1)S(1)}, u32[]{:S(2)}, u32[]{:S(2)}) %collective-permute-start.7) | collective-permute-done | bytes 397344 | tf_op jit(solution)/shard_map/ppermute | solution.py:435
  90.6 2.8 %collective-permute-start.12 = (bf16[776,256]{1,0:T(8,128)(2,1)S(1)}, bf16[776,256]{1,0:T(8,128)(2,1)S(1)}, u32[]{:S(2)}, u32[]{:S(2)}) collective-permute-start(bf16[776,256]{1,0:T(8,128)(2,1)S(1)} %get-tuple-element.105), channel_id=1, source_target_pairs={{0,28},{4,24},{8,4},{12,0},{16,12},{20,8},{24,20},{28,16},{32,60},... | collective-permute-start | bytes 1191944 | tf_op jit(solution)/shard_map/ppermute | solution.py:435
  93.4 4.8 %collective-permute-start.13 = (bf16[776,256]{1,0:T(8,128)(2,1)S(1)}, bf16[776,256]{1,0:T(8,128)(2,1)S(1)}, u32[]{:S(2)}, u32[]{:S(2)}) collective-permute-start(bf16[776,256]{1,0:T(8,128)(2,1)S(1)} %get-tuple-element.106), channel_id=1, source_target_pairs={{0,4},{4,0},{8,12},{12,8},{16,20},{20,16},{24,28},{28,24},{32,36},... | collective-permute-start | bytes 1191944 | tf_op jit(solution)/shard_map/ppermute | solution.py:435
  98.2 10.6 %collective-permute-done.9.refs_3_ = bf16[776,256]{1,0:T(8,128)(2,1)S(1)} collective-permute-done((bf16[776,256]{1,0:T(8,128)(2,1)S(1)}, bf16[776,256]{1,0:T(8,128)(2,1)S(1)}, u32[]{:S(2)}, u32[]{:S(2)}) %collective-permute-start.9) | collective-permute-done | bytes 397344 | tf_op jit(solution)/shard_map/ppermute | solution.py:435
  108.8 19.0 %collective-permute-done.10.refs_4_ = bf16[776,256]{1,0:T(8,128)(2,1)S(1)} collective-permute-done((bf16[776,256]{1,0:T(8,128)(2,1)S(1)}, bf16[776,256]{1,0:T(8,128)(2,1)S(1)}, u32[]{:S(2)}, u32[]{:S(2)}) %collective-permute-start.10) | collective-permute-done | bytes 397344 | tf_op jit(solution)/shard_map/ppermute | solution.py:435
  127.9 9.7 %collective-permute-done.11.refs_5_ = bf16[776,256]{1,0:T(8,128)(2,1)S(1)} collective-permute-done((bf16[776,256]{1,0:T(8,128)(2,1)S(1)}, bf16[776,256]{1,0:T(8,128)(2,1)S(1)}, u32[]{:S(2)}, u32[]{:S(2)}) %collective-permute-start.11) | collective-permute-done | bytes 397344 | tf_op jit(solution)/shard_map/ppermute | solution.py:435
  137.6 0.9 collective-permute-done.12.refs_6_
  138.6 0.7 copy-done.10
  139.3 0.1 copy-done.11
  139.4 0.6 flag.1
  140.1 0.8 plane_sum.1
  140.9 1.2 collective-permute-start.14
  142.1 0.1 stack.71.side
  143.0 2.4 %collective-permute-start.17 = (f32[32,128]{1,0:T(8,128)S(1)}, f32[32,128]{1,0:T(8,128)S(1)}, u32[]{:S(2)}, u32[]{:S(2)}) collective-permute-start(f32[32,128]{1,0:T(8,128)S(1)} %maximum_select_fusion), channel_id=1, source_target_pairs={{0,24},{4,28},{8,0},{12,4},{16,8},{20,12},{24,16},{28,20},{32,56},... | collective-permute-start | bytes 49160 | tf_op jit(solution)/shard_map/ppermute | solution.py:435
  145.4 0.7 collective-permute-start.16
  146.0 0.8 collective-permute-start.15
  146.8 8.1 %settle.1 = (bf16[49,256,256]{2,1,0:T(8,128)(2,1)}, f32[4,256]{1,0:T(4,128)}) custom-call(s32[8]{0:T(128)S(1)} %stack.71.side, bf16[64,104,256]{2,1,0:T(8,128)(2,1)S(1)} %all-to-all-done.1.tiles.direct, bf16[776,256]{1,0:T(8,128)(2,1)} %get-tuple-element.128.refs_0_, bf16[776,256]{1,0:T(8,128)(2,1)} %get-tuple-element.129.refs_1_, ...), custom_call_target="tpu_custom_call" | custom-call | flops 2147483648 | bytes 14680064 | tf_op jit(solution)/shard_map/settle/pallas_call | solution.py:275
  155.0 0.7 select_reduce_fusion
  (80 shorter events, 0.8 us)
Async XLA Ops:
  0.6 20.5 %copy-start = (bf16[128,128]{1,0:T(8,128)(2,1)S(1)}, bf16[128,128]{1,0:T(8,128)(2,1)}, u32[]{:S(2)}) copy-start(bf16[128,128]{1,0:T(8,128)(2,1)} %param.16) | copy-start | bytes 98308
  5.2 9.3 %copy-start.2 = (bf16[128,48,256]{2,1,0:T(8,128)(2,1)S(1)}, bf16[128,48,256]{2,1,0:T(8,128)(2,1)}, u32[]{:S(2)}) copy-start(bf16[128,48,256]{2,1,0:T(8,128)(2,1)} %cache.3) | copy-start | bytes 9437188
  5.2 48.3 %all-to-all-start.2 = ((bf16[8,392,256]{2,1,0:T(8,128)(2,1)}), bf16[8,392,256]{2,1,0:T(8,128)(2,1)}, u32[]{:S(2)}, u32[]{:S(2)}) async-start(bf16[8,392,256]{2,1,0:T(8,128)(2,1)} %pack_relay.1), calls=%async_computation.2 | async-start | bytes 3211264 | tf_op jit(solution)/shard_map/all_to_all | solution.py:316
  16.7 2.2 %copy-start.3 = (bf16[128,128]{1,0:T(8,128)(2,1)S(1)}, bf16[128,128]{1,0:T(8,128)(2,1)}, u32[]{:S(2)}) copy-start(bf16[128,128]{1,0:T(8,128)(2,1)} %param.13) | copy-start | bytes 98308
  16.7 4.4 %copy-start.14 = (f32[128]{0:T(128)S(1)}, f32[128]{0:T(128)}, u32[]{:S(2)}) copy-start(f32[128]{0:T(128)} %param.15) | copy-start | bytes 1540
  16.7 4.7 %copy-start.12 = (bf16[128,128]{1,0:T(8,128)(2,1)S(1)}, bf16[128,128]{1,0:T(8,128)(2,1)}, u32[]{:S(2)}) copy-start(bf16[128,128]{1,0:T(8,128)(2,1)} %param.17) | copy-start | bytes 98308
  18.9 3.6 %copy-start.13 = (bf16[128,128]{1,0:T(8,128)(2,1)S(1)}, bf16[128,128]{1,0:T(8,128)(2,1)}, u32[]{:S(2)}) copy-start(bf16[128,128]{1,0:T(8,128)(2,1)} %param.18) | copy-start | bytes 98308
  21.2 3.0 %copy-start.16 = (bf16[128,4]{0,1:T(4,128)(2,1)S(1)}, bf16[128,4]{0,1:T(4,128)(2,1)}, u32[]{:S(2)}) copy-start(bf16[128,4]{0,1:T(4,128)(2,1)} %param.20) | copy-start | bytes 3076
  21.2 8.8 %copy-start.15 = (s32[128,1]{0,1:T(1,128)S(1)}, s32[128,1]{0,1:T(1,128)}, u32[]{:S(2)}) copy-start(s32[128,1]{0,1:T(1,128)} %param.23) | copy-start | bytes 1540
  26.3 8.2 %collective-permute-start.1 = (f32[132,128]{1,0:T(8,128)S(1)}, f32[132,128]{1,0:T(8,128)S(1)}, u32[]{:S(2)}, u32[]{:S(2)}) collective-permute-start(f32[132,128]{1,0:T(8,128)S(1)} %pad_maximum_fusion.1), channel_id=1, source_target_pairs={{0,2},{1,3},{2,0},{3,1},{4,6},{5,7},{6,4},{7,5},{8,10},{9,11},{10,... | collective-permute-start | bytes 202760 | tf_op jit(solution)/shard_map/ppermute | solution.py:326
  29.2 5.4 %collective-permute-start.2 = (f32[132,128]{1,0:T(8,128)S(1)}, f32[132,128]{1,0:T(8,128)S(1)}, u32[]{:S(2)}, u32[]{:S(2)}) collective-permute-start(f32[132,128]{1,0:T(8,128)S(1)} %pad_maximum_fusion.1), channel_id=1, source_target_pairs={{0,3},{1,2},{2,1},{3,0},{4,7},{5,6},{6,5},{7,4},{8,11},{9,10},{10,... | collective-permute-start | bytes 202760 | tf_op jit(solution)/shard_map/ppermute | solution.py:326
  30.0 4.6 %collective-permute-start = (f32[132,128]{1,0:T(8,128)S(1)}, f32[132,128]{1,0:T(8,128)S(1)}, u32[]{:S(2)}, u32[]{:S(2)}) collective-permute-start(f32[132,128]{1,0:T(8,128)S(1)} %pad_maximum_fusion.1), channel_id=1, source_target_pairs={{0,1},{1,0},{2,3},{3,2},{4,5},{5,4},{6,7},{7,6},{8,9},{9,8},{10,11... | collective-permute-start | bytes 202760 | tf_op jit(solution)/shard_map/ppermute | solution.py:326
  34.6 5.2 %collective-permute-start.4 = (f32[132,128]{1,0:T(8,128)S(1)}, f32[132,128]{1,0:T(8,128)S(1)}, u32[]{:S(2)}, u32[]{:S(2)}) collective-permute-start(f32[132,128]{1,0:T(8,128)S(1)} %add_add_fusion.1), channel_id=1, source_target_pairs={{0,16},{4,20},{8,24},{12,28},{16,0},{20,4},{24,8},{28,12},{32,48},... | collective-permute-start | bytes 202760 | tf_op jit(solution)/shard_map/ppermute | solution.py:326
  37.7 4.8 %collective-permute-start.5 = (f32[132,128]{1,0:T(8,128)S(1)}, f32[132,128]{1,0:T(8,128)S(1)}, u32[]{:S(2)}, u32[]{:S(2)}) collective-permute-start(f32[132,128]{1,0:T(8,128)S(1)} %add_add_fusion.1), channel_id=1, source_target_pairs={{0,24},{4,28},{8,16},{12,20},{16,8},{20,12},{24,0},{28,4},{32,56},... | collective-permute-start | bytes 202760 | tf_op jit(solution)/shard_map/ppermute | solution.py:326
  38.5 4.2 %collective-permute-start.3 = (f32[132,128]{1,0:T(8,128)S(1)}, f32[132,128]{1,0:T(8,128)S(1)}, u32[]{:S(2)}, u32[]{:S(2)}) collective-permute-start(f32[132,128]{1,0:T(8,128)S(1)} %add_add_fusion.1), channel_id=1, source_target_pairs={{0,8},{4,12},{8,0},{12,4},{16,24},{20,28},{24,16},{28,20},{32,40},... | collective-permute-start | bytes 202760 | tf_op jit(solution)/shard_map/ppermute | solution.py:326
  42.7 3.4 %collective-permute-start.6 = (f32[132,128]{1,0:T(8,128)S(1)}, f32[132,128]{1,0:T(8,128)S(1)}, u32[]{:S(2)}, u32[]{:S(2)}) collective-permute-start(f32[132,128]{1,0:T(8,128)S(1)} %add_add_fusion), channel_id=1, source_target_pairs={{0,4},{4,0},{8,12},{12,8},{16,20},{20,16},{24,28},{28,24},{32,36},... | collective-permute-start | bytes 202760 | tf_op jit(solution)/shard_map/ppermute | solution.py:326
  53.5 86.6 %all-to-all-start.1 = ((bf16[64,104,256]{2,1,0:T(8,128)(2,1)}), bf16[64,104,256]{2,1,0:T(8,128)(2,1)S(1)}, u32[]{:S(2)}, u32[]{:S(2)}) async-start(bf16[64,104,256]{2,1,0:T(8,128)(2,1)} %pack_tiles.1), calls=%async_computation.1 | async-start | bytes 6815744 | tf_op jit(solution)/shard_map/all_to_all | solution.py:316
  71.2 67.3 %copy-start.4 = (bf16[776,256]{1,0:T(8,128)(2,1)}, bf16[776,256]{1,0:T(8,128)(2,1)S(1)}, u32[]{:S(2)}) copy-start(bf16[776,256]{1,0:T(8,128)(2,1)S(1)} %get-tuple-element.112.refs_0_) | copy-start | bytes 1191940
  71.2 19.4 %collective-permute-start.7 = (bf16[776,256]{1,0:T(8,128)(2,1)S(1)}, bf16[776,256]{1,0:T(8,128)(2,1)S(1)}, u32[]{:S(2)}, u32[]{:S(2)}) collective-permute-start(bf16[776,256]{1,0:T(8,128)(2,1)S(1)} %get-tuple-element.100), channel_id=1, source_target_pairs={{0,8},{4,12},{8,16},{12,20},{16,24},{20,28},{24,0},{28,4},{32,40},... | collective-permute-start | bytes 1191944 | tf_op jit(solution)/shard_map/ppermute | solution.py:435
  72.7 20.7 %collective-permute-start.8 = (bf16[776,256]{1,0:T(8,128)(2,1)S(1)}, bf16[776,256]{1,0:T(8,128)(2,1)S(1)}, u32[]{:S(2)}, u32[]{:S(2)}) collective-permute-start(bf16[776,256]{1,0:T(8,128)(2,1)S(1)} %get-tuple-element.101), channel_id=1, source_target_pairs={{0,24},{4,28},{8,0},{12,4},{16,8},{20,12},{24,16},{28,20},{32,56},... | collective-permute-start | bytes 1191944 | tf_op jit(solution)/shard_map/ppermute | solution.py:435
  74.0 34.8 %collective-permute-start.9 = (bf16[776,256]{1,0:T(8,128)(2,1)S(1)}, bf16[776,256]{1,0:T(8,128)(2,1)S(1)}, u32[]{:S(2)}, u32[]{:S(2)}) collective-permute-start(bf16[776,256]{1,0:T(8,128)(2,1)S(1)} %get-tuple-element.102), channel_id=1, source_target_pairs={{0,16},{4,20},{8,24},{12,28},{16,0},{20,4},{24,8},{28,12},{32,48},... | collective-permute-start | bytes 1191944 | tf_op jit(solution)/shard_map/ppermute | solution.py:435
  75.7 52.2 %collective-permute-start.10 = (bf16[776,256]{1,0:T(8,128)(2,1)S(1)}, bf16[776,256]{1,0:T(8,128)(2,1)S(1)}, u32[]{:S(2)}, u32[]{:S(2)}) collective-permute-start(bf16[776,256]{1,0:T(8,128)(2,1)S(1)} %get-tuple-element.103), channel_id=1, source_target_pairs={{0,20},{4,16},{8,28},{12,24},{16,4},{20,0},{24,12},{28,8},{32,52},... | collective-permute-start | bytes 1191944 | tf_op jit(solution)/shard_map/ppermute | solution.py:435
  78.1 59.5 %collective-permute-start.11 = (bf16[776,256]{1,0:T(8,128)(2,1)S(1)}, bf16[776,256]{1,0:T(8,128)(2,1)S(1)}, u32[]{:S(2)}, u32[]{:S(2)}) collective-permute-start(bf16[776,256]{1,0:T(8,128)(2,1)S(1)} %get-tuple-element.104), channel_id=1, source_target_pairs={{0,12},{4,8},{8,20},{12,16},{16,28},{20,24},{24,4},{28,0},{32,44},... | collective-permute-start | bytes 1191944 | tf_op jit(solution)/shard_map/ppermute | solution.py:435
  90.6 47.9 %copy-start.5 = (bf16[776,256]{1,0:T(8,128)(2,1)}, bf16[776,256]{1,0:T(8,128)(2,1)S(1)}, u32[]{:S(2)}) copy-start(bf16[776,256]{1,0:T(8,128)(2,1)S(1)} %collective-permute-done.7.refs_1_) | copy-start | bytes 1191940
  90.6 47.9 %collective-permute-start.12 = (bf16[776,256]{1,0:T(8,128)(2,1)S(1)}, bf16[776,256]{1,0:T(8,128)(2,1)S(1)}, u32[]{:S(2)}, u32[]{:S(2)}) collective-permute-start(bf16[776,256]{1,0:T(8,128)(2,1)S(1)} %get-tuple-element.105), channel_id=1, source_target_pairs={{0,28},{4,24},{8,4},{12,0},{16,12},{20,8},{24,20},{28,16},{32,60},... | collective-permute-start | bytes 1191944 | tf_op jit(solution)/shard_map/ppermute | solution.py:435
  93.4 45.1 %copy-start.6 = (bf16[776,256]{1,0:T(8,128)(2,1)}, bf16[776,256]{1,0:T(8,128)(2,1)S(1)}, u32[]{:S(2)}) copy-start(bf16[776,256]{1,0:T(8,128)(2,1)S(1)} %collective-permute-done.8.refs_2_) | copy-start | bytes 1191940
  93.4 45.1 %collective-permute-start.13 = (bf16[776,256]{1,0:T(8,128)(2,1)S(1)}, bf16[776,256]{1,0:T(8,128)(2,1)S(1)}, u32[]{:S(2)}, u32[]{:S(2)}) collective-permute-start(bf16[776,256]{1,0:T(8,128)(2,1)S(1)} %get-tuple-element.106), channel_id=1, source_target_pairs={{0,4},{4,0},{8,12},{12,8},{16,20},{20,16},{24,28},{28,24},{32,36},... | collective-permute-start | bytes 1191944 | tf_op jit(solution)/shard_map/ppermute | solution.py:435
  108.8 29.7 %copy-start.7 = (bf16[776,256]{1,0:T(8,128)(2,1)}, bf16[776,256]{1,0:T(8,128)(2,1)S(1)}, u32[]{:S(2)}) copy-start(bf16[776,256]{1,0:T(8,128)(2,1)S(1)} %collective-permute-done.9.refs_3_) | copy-start | bytes 1191940
  127.9 10.7 %copy-start.8 = (bf16[776,256]{1,0:T(8,128)(2,1)}, bf16[776,256]{1,0:T(8,128)(2,1)S(1)}, u32[]{:S(2)}) copy-start(bf16[776,256]{1,0:T(8,128)(2,1)S(1)} %collective-permute-done.10.refs_4_) | copy-start | bytes 1191940
  137.6 0.9 copy-start.9
  138.5 0.8 copy-start.10
  138.5 0.9 copy-start.11
  140.9 2.1 %collective-permute-start.14 = (f32[16,128]{1,0:T(8,128)S(1)}, f32[16,128]{1,0:T(8,128)S(1)}, u32[]{:S(2)}, u32[]{:S(2)}) collective-permute-start(f32[16,128]{1,0:T(8,128)S(1)} %get-tuple-element.108), channel_id=1, source_target_pairs={{0,4},{4,0},{8,12},{12,8},{16,20},{20,16},{24,28},{28,24},{32,36},... | collective-permute-start | bytes 24584 | tf_op jit(solution)/shard_map/ppermute | solution.py:475
  143.0 12.0 %collective-permute-start.17 = (f32[32,128]{1,0:T(8,128)S(1)}, f32[32,128]{1,0:T(8,128)S(1)}, u32[]{:S(2)}, u32[]{:S(2)}) collective-permute-start(f32[32,128]{1,0:T(8,128)S(1)} %maximum_select_fusion), channel_id=1, source_target_pairs={{0,24},{4,28},{8,0},{12,4},{16,8},{20,12},{24,16},{28,20},{32,56},... | collective-permute-start | bytes 49160 | tf_op jit(solution)/shard_map/ppermute | solution.py:435
  145.4 9.6 %collective-permute-start.16 = (f32[32,128]{1,0:T(8,128)S(1)}, f32[32,128]{1,0:T(8,128)S(1)}, u32[]{:S(2)}, u32[]{:S(2)}) collective-permute-start(f32[32,128]{1,0:T(8,128)S(1)} %maximum_select_fusion), channel_id=1, source_target_pairs={{0,16},{4,20},{8,24},{12,28},{16,0},{20,4},{24,8},{28,12},{32,48},... | collective-permute-start | bytes 49160 | tf_op jit(solution)/shard_map/ppermute | solution.py:435
  146.0 8.9 %collective-permute-start.15 = (f32[32,128]{1,0:T(8,128)S(1)}, f32[32,128]{1,0:T(8,128)S(1)}, u32[]{:S(2)}, u32[]{:S(2)}) collective-permute-start(f32[32,128]{1,0:T(8,128)S(1)} %maximum_select_fusion), channel_id=1, source_target_pairs={{0,8},{4,12},{8,16},{12,20},{16,24},{20,28},{24,0},{28,4},{32,40},... | collective-permute-start | bytes 49160 | tf_op jit(solution)/shard_map/ppermute | solution.py:435

commit v8 on v7

--- a/solution.py
+++ b/solution.py
@@ -446,16 +446,6 @@
         name="flag",
     )(*lasts)
 
-    def by_relay(lasts):
-        return lasts
-
-    def by_pairs(lasts):
-        high = exchanged(pack_direct(2, target, cache))
-        high = high[:, : 2 * LEVELS].reshape(PLANES, SIDE, 2 * LEVELS, WIDTH)
-        high = jnp.swapaxes(high, 0, 1).reshape(SIDE, 2 * PLANES * LEVELS, WIDTH)
-        high = jnp.pad(high, ((0, 0), (0, LAST - 2 * PLANES * LEVELS), (0, 0)))
-        return [lax.dynamic_index_in_dim(high, came[k], 0, keepdims=False) for k in range(SIDE)]
-
     direct, over = lax.optimization_barrier((direct, over))
     piece, head = pl.pallas_call(
         plane_sum_kernel,
@@ -477,13 +467,24 @@
         core == 0, jnp.concatenate([piece, other], 0), jnp.concatenate([other, piece], 0)
     )
     direct, lasts, piece = lax.optimization_barrier((direct, lasts, piece))
-    lasts = lax.cond(over[0] > 0, by_pairs, by_relay, lasts)
-    piece, lasts = lax.optimization_barrier((piece, lasts))
     shares = jnp.stack([piece] + [in_plane(piece, shifts.index((dy, 0))) for dy in (1, 2, 3)])
     rows_y = jnp.arange(4, dtype=jnp.int32)
     ours = (lax.rem(y - rows_y + 4, 4)[:, None] == rows_y[None, :])[..., None, None]
     grad_out = jnp.sum(jnp.where(ours, shares[None], 0.0), 1).reshape(ROWS, ROWS)
     new_cache, log_probs = settle(came, direct, lasts)
+
+    def by_relay(new_cache):
+        return new_cache
+
+    def by_pairs(new_cache):
+        high = exchanged(pack_direct(2, target, cache))
+        high = high[:, : 2 * LEVELS].reshape(PLANES, SIDE, 2 * LEVELS, WIDTH)
+        high = jnp.swapaxes(high, 0, 1).reshape(SIDE, 2 * PLANES * LEVELS, WIDTH)
+        high = jnp.pad(high, ((0, 0), (0, LAST - 2 * PLANES * LEVELS), (0, 0)))
+        lasts = [lax.dynamic_index_in_dim(high, came[k], 0, keepdims=False) for k in range(SIDE)]
+        return settle(came, direct, lasts)[0]
+
+    new_cache = lax.cond(over[0] > 0, by_pairs, by_relay, new_cache)
     return (jnp.swapaxes(new_cache, 0, 1), log_probs.T, grad_out, head.T)
 
 

time: 157 us -> 157 us (level)
  starting transfers between devices: 46.6 us -> 41.9 us
  waiting for transfers between devices: 63.1 us -> 67.2 us
  matrix products: 3.95 us -> 1.84 us
  local copies, waits for them, and re-layouts: 8.37 us -> 10.1 us
    ppermute x10, waiting for transfers between devices: 52.7 us -> 58.3 us  [in_plane(): return lax.ppermute(x, 'sample', pairs)]
    ppermute x10, starting transfers between devices: 18.4 us -> 13 us  [in_plane(): return lax.ppermute(x, 'sample', pairs)]
    slice x1, local copies, waits for them, and re-layouts: 2.23 us -> 4.08 us  [decode_rows(): key_rows = cache[:, :, :width].reshape(count, levels, HEADS, size)]
    unnamed x35 -> x23, local copies, waits for them, and re-layouts: 5.21 us -> 5.1 us
  transfers between devices with their start and end apart: 20 -> 20, of which waited for: 10 -> 10; matrix products, arithmetic and copies ran while one was open for 9% -> 10% of each run, Pallas kernels for 15% -> 15%
where the time goes in v8:
time: 157 us; the launch traced here: 156 us
  waiting for transfers between devices  67.2 us (43%)
  starting transfers between devices  41.9 us (27%)
  Pallas kernels  29.3 us (19%)
  local copies, waits for them, and re-layouts  10.1 us (6%)
  other arithmetic  4.06 us (3%)
  matrix products  1.84 us (1%)
  between operations  1.84 us (1%)
    ppermute x10, waiting for transfers between devices, in_plane(): return lax.ppermute(x, 'sample', pairs)  58.3 us
    all_to_all x2, starting transfers between devices, exchanged(): lax.all_to_all(x, 'sample', split_axis=0, concat_axis=0, tiled=True, axis...  16.9 us
    ppermute x10, starting transfers between devices, in_plane(): return lax.ppermute(x, 'sample', pairs)  13 us
    ppermute x7, starting transfers between devices, tree_sum(): terms = [x] + [lax.ppermute(x, axis, xor_pairs(size, bit)) for bit in bits]  10.1 us
    pallas_call x1, Pallas kernels, on_device(): pl.pallas_call(forward_kernel, out_shape=[jax.ShapeDtypeStruct((LAST, WID...  8.84 us
    pallas_call x1, Pallas kernels, settle(): pl.pallas_call(settle_kernel, grid=(PLANES,), out_shape=(jax.ShapeDtypeSt...  8.35 us
    unnamed x23, local copies, waits for them, and re-layouts  5.1 us
    all_to_all x2, waiting for transfers between devices, exchanged(): lax.all_to_all(x, 'sample', split_axis=0, concat_axis=0, tiled=True, axis...  4.83 us
  transfers between devices with their start and end apart: 20, of which 10 were waited for; matrix products, arithmetic and copies ran while one was open for 10% of the time, Pallas kernels for 15%

profile of v8, /device:TPU:1, one launch (start us, length us, event | category | flops | bytes accessed | tf_op | source)
XLA Modules:
  0.0 156.2 jit_solution(3339923128037755412)
XLA Ops:
  0.6 4.6 %pack_relay.1 = bf16[8,392,256]{2,1,0:T(8,128)(2,1)} custom-call(s32[128]{0:T(128)} %bitcast.109, bf16[128,48,256]{2,1,0:T(8,128)(2,1)} %cache.3), custom_call_target="tpu_custom_call" | custom-call | tf_op jit(solution)/shard_map/pack_relay/pallas_call | solution.py:346
  5.2 9.0 %all-to-all-start.2 = ((bf16[8,392,256]{2,1,0:T(8,128)(2,1)}), bf16[8,392,256]{2,1,0:T(8,128)(2,1)S(1)}, u32[]{:S(2)}, u32[]{:S(2)}) async-start(bf16[8,392,256]{2,1,0:T(8,128)(2,1)} %pack_relay.1), calls=%async_computation.2 | async-start | bytes 3211264 | tf_op jit(solution)/shard_map/all_to_all | solution.py:316
  14.2 4.1 %fusion.39 = (bf16[128,48,128]{2,1,0:T(8,128)(2,1)}, bf16[128,48,128]{2,1,0:T(8,128)(2,1)}) fusion(bf16[128,48,256]{2,1,0:T(8,128)(2,1)} %cache.3), kind=kLoop, calls=%fused_computation.99 | loop fusion | bytes 6291456 | tf_op jit(solution)/shard_map/slice | solution.py:43
  18.3 2.1 %copy.62 = bf16[128,48,128]{0,2,1:T(8,128)(2,1)S(1)} copy(bf16[128,48,128]{2,1,0:T(8,128)(2,1)} %get-tuple-element.110) | data formatting | bytes 3145728
  20.5 0.1 fusion.12
  20.6 2.8 %copy.61 = bf16[128,48,128]{0,2,1:T(8,128)(2,1)} copy(bf16[128,48,128]{2,1,0:T(8,128)(2,1)} %get-tuple-element.109) | data formatting | bytes 3145728
  23.5 0.2 bitcast_convert_fusion
  23.8 0.2 convolution_convert_fusion.2
  24.0 2.0 %multiply_reduce_fusion.1 = f32[128,4,48]{0,1,2:T(4,128)S(1)} fusion(f32[128,4,32]{0,2,1:T(8,128)S(1)} %get-tuple-element.122, bf16[128,48,128]{0,2,1:T(8,128)(2,1)} %copy.61), kind=kLoop, calls=%fused_computation.17 | loop fusion | flops 2334720 | bytes 1736704
  26.1 0.1 reduce_max.19
  26.3 0.2 convolution_convert_fusion.1
  26.5 0.4 multiply_reduce_fusion
  27.0 0.2 fusion.9
  27.2 0.1 fusion.40
  27.4 0.3 fusion.26
  27.7 0.1 fusion.25
  27.8 0.2 fusion.41
  28.0 2.8 %collective-permute-start.1 = (f32[132,128]{1,0:T(8,128)S(1)}, f32[132,128]{1,0:T(8,128)S(1)}, u32[]{:S(2)}, u32[]{:S(2)}) collective-permute-start(f32[132,128]{1,0:T(8,128)S(1)} %pad_maximum_fusion.1), channel_id=1, source_target_pairs={{0,2},{1,3},{2,0},{3,1},{4,6},{5,7},{6,4},{7,5},{8,10},{9,11},{10,... | collective-permute-start | bytes 202760 | tf_op jit(solution)/shard_map/ppermute | solution.py:326
  30.8 0.9 collective-permute-start.2
  31.7 4.4 %pack_direct.3.rows = bf16[64,104,256]{2,1,0:T(8,128)(2,1)} custom-call(s32[128]{0:T(128)S(1)} %bitcast.110, bf16[128,48,256]{2,1,0:T(8,128)(2,1)} %cache.3), custom_call_target="tpu_custom_call" | custom-call | bytes 10485760 | tf_op jit(solution)/shard_map/pack_direct/pallas_call | solution.py:299
  36.2 0.1 convert_reduce_fusion
  36.3 3.0 %collective-permute-start.4 = (f32[132,128]{1,0:T(8,128)S(1)}, f32[132,128]{1,0:T(8,128)S(1)}, u32[]{:S(2)}, u32[]{:S(2)}) collective-permute-start(f32[132,128]{1,0:T(8,128)S(1)} %add_add_fusion.1), channel_id=1, source_target_pairs={{0,16},{4,20},{8,24},{12,28},{16,0},{20,4},{24,8},{28,12},{32,48},... | collective-permute-start | bytes 202760 | tf_op jit(solution)/shard_map/ppermute | solution.py:326
  39.3 0.8 collective-permute-start.5
  40.1 0.1 concatenate.21
  40.1 1.1 collective-permute-done.4
  41.2 2.9 %collective-permute-done.5 = f32[132,128]{1,0:T(8,128)S(1)} collective-permute-done((f32[132,128]{1,0:T(8,128)S(1)}, f32[132,128]{1,0:T(8,128)S(1)}, u32[]{:S(2)}, u32[]{:S(2)}) %collective-permute-start.5) | collective-permute-done | bytes 67616 | tf_op jit(solution)/shard_map/ppermute | solution.py:326
  44.1 2.6 %collective-permute-start.6 = (f32[132,128]{1,0:T(8,128)S(1)}, f32[132,128]{1,0:T(8,128)S(1)}, u32[]{:S(2)}, u32[]{:S(2)}) collective-permute-start(f32[132,128]{1,0:T(8,128)S(1)} %add_add_fusion), channel_id=1, source_target_pairs={{0,4},{4,0},{8,12},{12,8},{16,20},{20,16},{24,28},{28,24},{32,36},... | collective-permute-start | bytes 202760 | tf_op jit(solution)/shard_map/ppermute | solution.py:326
  46.7 0.2 convolution_convert_fusion
  47.0 0.1 copy.42
  47.1 0.1 reshape.205
  47.2 0.1 copy.41
  47.4 0.1 pad.19.clone
  47.5 0.2 collective-permute-done.6
  47.8 0.1 reshape.206
  47.9 0.1 pad_maximum_fusion.4
  47.9 0.1 copy.46
  48.1 0.2 pad_maximum_fusion.tiles
  48.3 0.7 pack_tiles.1
  49.0 4.1 %all-to-all-done.2.got = bf16[8,392,256]{2,1,0:T(8,128)(2,1)S(1)} async-done(((bf16[8,392,256]{2,1,0:T(8,128)(2,1)}), bf16[8,392,256]{2,1,0:T(8,128)(2,1)S(1)}, u32[]{:S(2)}, u32[]{:S(2)}) %all-to-all-start.2) | async-done | bytes 1605664 | tf_op jit(solution)/shard_map/all_to_all | solution.py:316
  53.1 7.9 %all-to-all-start.1 = ((bf16[64,104,256]{2,1,0:T(8,128)(2,1)}), bf16[64,104,256]{2,1,0:T(8,128)(2,1)}, u32[]{:S(2)}, u32[]{:S(2)}) async-start(bf16[64,104,256]{2,1,0:T(8,128)(2,1)} %pack_tiles.1), calls=%async_computation.1 | async-start | bytes 6815744 | tf_op jit(solution)/shard_map/all_to_all | solution.py:316
  61.1 0.1 stack.72.side
  61.2 8.8 %pack_plane.1 = (bf16[776,256]{1,0:T(8,128)(2,1)S(1)}, bf16[776,256]{1,0:T(8,128)(2,1)S(1)}, bf16[776,256]{1,0:T(8,128)(2,1)S(1)}, bf16[776,256]{1,0:T(8,128)(2,...) custom-call(s32[8,16]{1,0:T(8,128)S(1)} %bitcast.93, ...), custom_call_target="tpu_custom_call" | custom-call | bytes 5242880 | tf_op jit(solution)/shard_map/pack_plane/pallas_call | solution.py:409
  70.0 1.5 collective-permute-start.7
  71.5 1.3 collective-permute-start.8
  72.8 1.7 %collective-permute-start.9 = (bf16[776,256]{1,0:T(8,128)(2,1)S(1)}, bf16[776,256]{1,0:T(8,128)(2,1)S(1)}, u32[]{:S(2)}, u32[]{:S(2)}) collective-permute-start(bf16[776,256]{1,0:T(8,128)(2,1)S(1)} %get-tuple-element.80), channel_id=1, source_target_pairs={{0,16},{4,20},{8,24},{12,28},{16,0},{20,4},{24,8},{28,12},{32,48},... | collective-permute-start | bytes 1191944 | tf_op jit(solution)/shard_map/ppermute | solution.py:435
  74.5 2.6 %collective-permute-start.10 = (bf16[776,256]{1,0:T(8,128)(2,1)S(1)}, bf16[776,256]{1,0:T(8,128)(2,1)S(1)}, u32[]{:S(2)}, u32[]{:S(2)}) collective-permute-start(bf16[776,256]{1,0:T(8,128)(2,1)S(1)} %get-tuple-element.81), channel_id=1, source_target_pairs={{0,20},{4,16},{8,28},{12,24},{16,4},{20,0},{24,12},{28,8},{32,52},... | collective-permute-start | bytes 1191944 | tf_op jit(solution)/shard_map/ppermute | solution.py:435
  77.0 12.9 %collective-permute-done.7.refs_1_ = bf16[776,256]{1,0:T(8,128)(2,1)S(1)} collective-permute-done((bf16[776,256]{1,0:T(8,128)(2,1)S(1)}, bf16[776,256]{1,0:T(8,128)(2,1)S(1)}, u32[]{:S(2)}, u32[]{:S(2)}) %collective-permute-start.7) | collective-permute-done | bytes 397344 | tf_op jit(solution)/shard_map/ppermute | solution.py:435
  89.9 2.5 %collective-permute-start.12 = (bf16[776,256]{1,0:T(8,128)(2,1)S(1)}, bf16[776,256]{1,0:T(8,128)(2,1)S(1)}, u32[]{:S(2)}, u32[]{:S(2)}) collective-permute-start(bf16[776,256]{1,0:T(8,128)(2,1)S(1)} %get-tuple-element.83), channel_id=1, source_target_pairs={{0,28},{4,24},{8,4},{12,0},{16,12},{20,8},{24,20},{28,16},{32,60},... | collective-permute-start | bytes 1191944 | tf_op jit(solution)/shard_map/ppermute | solution.py:435
  92.4 14.6 %collective-permute-done.9.refs_3_ = bf16[776,256]{1,0:T(8,128)(2,1)S(1)} collective-permute-done((bf16[776,256]{1,0:T(8,128)(2,1)S(1)}, bf16[776,256]{1,0:T(8,128)(2,1)S(1)}, u32[]{:S(2)}, u32[]{:S(2)}) %collective-permute-start.9) | collective-permute-done | bytes 397344 | tf_op jit(solution)/shard_map/ppermute | solution.py:435
  107.0 19.9 %collective-permute-done.10.refs_4_ = bf16[776,256]{1,0:T(8,128)(2,1)S(1)} collective-permute-done((bf16[776,256]{1,0:T(8,128)(2,1)S(1)}, bf16[776,256]{1,0:T(8,128)(2,1)S(1)}, u32[]{:S(2)}, u32[]{:S(2)}) %collective-permute-start.10) | collective-permute-done | bytes 397344 | tf_op jit(solution)/shard_map/ppermute | solution.py:435
  126.9 9.6 %collective-permute-done.11.refs_5_ = bf16[776,256]{1,0:T(8,128)(2,1)S(1)} collective-permute-done((bf16[776,256]{1,0:T(8,128)(2,1)S(1)}, bf16[776,256]{1,0:T(8,128)(2,1)S(1)}, u32[]{:S(2)}, u32[]{:S(2)}) %collective-permute-start.11) | collective-permute-done | bytes 397344 | tf_op jit(solution)/shard_map/ppermute | solution.py:435
  136.5 1.3 collective-permute-done.12.refs_6_
  137.8 0.6 flag.1
  138.4 0.7 all-to-all-done.1.tiles.direct
  139.2 1.7 %plane_sum.1 = (f32[16,128]{1,0:T(8,128)S(1)}, f32[4,128]{1,0:T(4,128)}) custom-call(bf16[64,104,256]{2,1,0:T(8,128)(2,1)} %all-to-all-done.1.tiles.direct), custom_call_target="tpu_custom_call" | custom-call | tf_op jit(solution)/shard_map/plane_sum/pallas_call | solution.py:450
  140.9 1.8 %collective-permute-start.14 = (f32[16,128]{1,0:T(8,128)S(1)}, f32[16,128]{1,0:T(8,128)S(1)}, u32[]{:S(2)}, u32[]{:S(2)}) collective-permute-start(f32[16,128]{1,0:T(8,128)S(1)} %get-tuple-element.87), channel_id=1, source_target_pairs={{0,4},{4,0},{8,12},{12,8},{16,20},{20,16},{24,28},{28,24},{32,36},... | collective-permute-start | bytes 24584 | tf_op jit(solution)/shard_map/ppermute | solution.py:465
  142.7 0.1 iota_compare_fusion.3
  142.8 0.1 stack.75.side
  143.5 0.0 collective-permute-done.14
  143.6 2.4 %collective-permute-start.17 = (f32[32,128]{1,0:T(8,128)S(1)}, f32[32,128]{1,0:T(8,128)S(1)}, u32[]{:S(2)}, u32[]{:S(2)}) collective-permute-start(f32[32,128]{1,0:T(8,128)S(1)} %maximum_select_fusion), channel_id=1, source_target_pairs={{0,24},{4,28},{8,0},{12,4},{16,8},{20,12},{24,16},{28,20},{32,56},... | collective-permute-start | bytes 49160 | tf_op jit(solution)/shard_map/ppermute | solution.py:435
  146.0 0.5 collective-permute-start.16
  146.5 0.6 collective-permute-start.15
  147.1 8.3 %settle.3 = (bf16[49,256,256]{2,1,0:T(8,128)(2,1)}, f32[4,256]{1,0:T(4,128)}) custom-call(s32[8]{0:T(128)S(1)} %stack.75.side, bf16[64,104,256]{2,1,0:T(8,128)(2,1)} %all-to-all-done.1.tiles.direct, bf16[776,256]{1,0:T(8,128)(2,1)S(1)} %get-tuple-element.89.refs_0_, bf16[776,256]{1,0:T(8,128)(2,1)S(1)} %collective-permute-done.7.refs_1_, ...), custom_call_target="tpu_custom_call" | custom-call | flops 2147483648 | bytes 14680064 | tf_op jit(solution)/shard_map/settle/pallas_call | solution.py:275
  155.5 0.7 select_reduce_fusion
  (68 shorter events, 0.6 us)
Async XLA Ops:
  0.6 22.9 %copy-start = (bf16[128,128]{1,0:T(8,128)(2,1)S(1)}, bf16[128,128]{1,0:T(8,128)(2,1)}, u32[]{:S(2)}) copy-start(bf16[128,128]{1,0:T(8,128)(2,1)} %param.16) | copy-start | bytes 98308
  5.2 47.9 %all-to-all-start.2 = ((bf16[8,392,256]{2,1,0:T(8,128)(2,1)}), bf16[8,392,256]{2,1,0:T(8,128)(2,1)S(1)}, u32[]{:S(2)}, u32[]{:S(2)}) async-start(bf16[8,392,256]{2,1,0:T(8,128)(2,1)} %pack_relay.1), calls=%async_computation.2 | async-start | bytes 3211264 | tf_op jit(solution)/shard_map/all_to_all | solution.py:316
  18.3 2.2 %copy-start.1 = (bf16[128,128]{1,0:T(8,128)(2,1)S(1)}, bf16[128,128]{1,0:T(8,128)(2,1)}, u32[]{:S(2)}) copy-start(bf16[128,128]{1,0:T(8,128)(2,1)} %param.13) | copy-start | bytes 98308
  18.3 5.2 %copy-start.5 = (f32[128]{0:T(128)S(1)}, f32[128]{0:T(128)}, u32[]{:S(2)}) copy-start(f32[128]{0:T(128)} %param.15) | copy-start | bytes 1540
  18.3 5.5 %copy-start.2 = (bf16[128,128]{1,0:T(8,128)(2,1)S(1)}, bf16[128,128]{1,0:T(8,128)(2,1)}, u32[]{:S(2)}) copy-start(bf16[128,128]{1,0:T(8,128)(2,1)} %param.17) | copy-start | bytes 98308
  20.5 5.8 %copy-start.3 = (bf16[128,128]{1,0:T(8,128)(2,1)S(1)}, bf16[128,128]{1,0:T(8,128)(2,1)}, u32[]{:S(2)}) copy-start(bf16[128,128]{1,0:T(8,128)(2,1)} %param.18) | copy-start | bytes 98308
  20.6 6.3 %copy-start.4 = (bf16[128,128]{1,0:T(8,128)(2,1)S(1)}, bf16[128,128]{1,0:T(8,128)(2,1)}, u32[]{:S(2)}) copy-start(bf16[128,128]{1,0:T(8,128)(2,1)} %param.19) | copy-start | bytes 98308
  23.5 3.7 %copy-start.7 = (bf16[128,4]{0,1:T(4,128)(2,1)S(1)}, bf16[128,4]{0,1:T(4,128)(2,1)}, u32[]{:S(2)}) copy-start(bf16[128,4]{0,1:T(4,128)(2,1)} %param.20) | copy-start | bytes 3076
  23.5 3.9 %copy-start.8 = (s32[128]{0:T(128)S(1)}, s32[128]{0:T(128)}, u32[]{:S(2)}) copy-start(s32[128]{0:T(128)} %param.22) | copy-start | bytes 1540
  23.5 3.9 %copy-start.9 = (f32[128]{0:T(128)S(1)}, f32[128]{0:T(128)}, u32[]{:S(2)}) copy-start(f32[128]{0:T(128)} %param.21) | copy-start | bytes 1540
  23.5 8.2 %copy-start.6 = (s32[128,1]{0,1:T(1,128)S(1)}, s32[128,1]{0,1:T(1,128)}, u32[]{:S(2)}) copy-start(s32[128,1]{0,1:T(1,128)} %param.23) | copy-start | bytes 1540
  28.0 8.2 %collective-permute-start.1 = (f32[132,128]{1,0:T(8,128)S(1)}, f32[132,128]{1,0:T(8,128)S(1)}, u32[]{:S(2)}, u32[]{:S(2)}) collective-permute-start(f32[132,128]{1,0:T(8,128)S(1)} %pad_maximum_fusion.1), channel_id=1, source_target_pairs={{0,2},{1,3},{2,0},{3,1},{4,6},{5,7},{6,4},{7,5},{8,10},{9,11},{10,... | collective-permute-start | bytes 202760 | tf_op jit(solution)/shard_map/ppermute | solution.py:326
  30.8 5.5 %collective-permute-start.2 = (f32[132,128]{1,0:T(8,128)S(1)}, f32[132,128]{1,0:T(8,128)S(1)}, u32[]{:S(2)}, u32[]{:S(2)}) collective-permute-start(f32[132,128]{1,0:T(8,128)S(1)} %pad_maximum_fusion.1), channel_id=1, source_target_pairs={{0,3},{1,2},{2,1},{3,0},{4,7},{5,6},{6,5},{7,4},{8,11},{9,10},{10,... | collective-permute-start | bytes 202760 | tf_op jit(solution)/shard_map/ppermute | solution.py:326
  31.7 4.6 %collective-permute-start = (f32[132,128]{1,0:T(8,128)S(1)}, f32[132,128]{1,0:T(8,128)S(1)}, u32[]{:S(2)}, u32[]{:S(2)}) collective-permute-start(f32[132,128]{1,0:T(8,128)S(1)} %pad_maximum_fusion.1), channel_id=1, source_target_pairs={{0,1},{1,0},{2,3},{3,2},{4,5},{5,4},{6,7},{7,6},{8,9},{9,8},{10,11... | collective-permute-start | bytes 202760 | tf_op jit(solution)/shard_map/ppermute | solution.py:326
  36.3 4.9 %collective-permute-start.4 = (f32[132,128]{1,0:T(8,128)S(1)}, f32[132,128]{1,0:T(8,128)S(1)}, u32[]{:S(2)}, u32[]{:S(2)}) collective-permute-start(f32[132,128]{1,0:T(8,128)S(1)} %add_add_fusion.1), channel_id=1, source_target_pairs={{0,16},{4,20},{8,24},{12,28},{16,0},{20,4},{24,8},{28,12},{32,48},... | collective-permute-start | bytes 202760 | tf_op jit(solution)/shard_map/ppermute | solution.py:326
  39.3 4.8 %collective-permute-start.5 = (f32[132,128]{1,0:T(8,128)S(1)}, f32[132,128]{1,0:T(8,128)S(1)}, u32[]{:S(2)}, u32[]{:S(2)}) collective-permute-start(f32[132,128]{1,0:T(8,128)S(1)} %add_add_fusion.1), channel_id=1, source_target_pairs={{0,24},{4,28},{8,16},{12,20},{16,8},{20,12},{24,0},{28,4},{32,56},... | collective-permute-start | bytes 202760 | tf_op jit(solution)/shard_map/ppermute | solution.py:326
  40.1 4.0 %collective-permute-start.3 = (f32[132,128]{1,0:T(8,128)S(1)}, f32[132,128]{1,0:T(8,128)S(1)}, u32[]{:S(2)}, u32[]{:S(2)}) collective-permute-start(f32[132,128]{1,0:T(8,128)S(1)} %add_add_fusion.1), channel_id=1, source_target_pairs={{0,8},{4,12},{8,0},{12,4},{16,24},{20,28},{24,16},{28,20},{32,40},... | collective-permute-start | bytes 202760 | tf_op jit(solution)/shard_map/ppermute | solution.py:326
  44.1 3.5 %collective-permute-start.6 = (f32[132,128]{1,0:T(8,128)S(1)}, f32[132,128]{1,0:T(8,128)S(1)}, u32[]{:S(2)}, u32[]{:S(2)}) collective-permute-start(f32[132,128]{1,0:T(8,128)S(1)} %add_add_fusion), channel_id=1, source_target_pairs={{0,4},{4,0},{8,12},{12,8},{16,20},{20,16},{24,28},{28,24},{32,36},... | collective-permute-start | bytes 202760 | tf_op jit(solution)/shard_map/ppermute | solution.py:326
  53.1 86.0 %all-to-all-start.1 = ((bf16[64,104,256]{2,1,0:T(8,128)(2,1)}), bf16[64,104,256]{2,1,0:T(8,128)(2,1)}, u32[]{:S(2)}, u32[]{:S(2)}) async-start(bf16[64,104,256]{2,1,0:T(8,128)(2,1)} %pack_tiles.1), calls=%async_computation.1 | async-start | bytes 6815744 | tf_op jit(solution)/shard_map/all_to_all | solution.py:316
  70.0 19.9 %collective-permute-start.7 = (bf16[776,256]{1,0:T(8,128)(2,1)S(1)}, bf16[776,256]{1,0:T(8,128)(2,1)S(1)}, u32[]{:S(2)}, u32[]{:S(2)}) collective-permute-start(bf16[776,256]{1,0:T(8,128)(2,1)S(1)} %get-tuple-element.78), channel_id=1, source_target_pairs={{0,8},{4,12},{8,16},{12,20},{16,24},{20,28},{24,0},{28,4},{32,40},... | collective-permute-start | bytes 1191944 | tf_op jit(solution)/shard_map/ppermute | solution.py:435
  71.5 20.9 %collective-permute-start.8 = (bf16[776,256]{1,0:T(8,128)(2,1)S(1)}, bf16[776,256]{1,0:T(8,128)(2,1)S(1)}, u32[]{:S(2)}, u32[]{:S(2)}) collective-permute-start(bf16[776,256]{1,0:T(8,128)(2,1)S(1)} %get-tuple-element.79), channel_id=1, source_target_pairs={{0,24},{4,28},{8,0},{12,4},{16,8},{20,12},{24,16},{28,20},{32,56},... | collective-permute-start | bytes 1191944 | tf_op jit(solution)/shard_map/ppermute | solution.py:435
  72.8 34.2 %collective-permute-start.9 = (bf16[776,256]{1,0:T(8,128)(2,1)S(1)}, bf16[776,256]{1,0:T(8,128)(2,1)S(1)}, u32[]{:S(2)}, u32[]{:S(2)}) collective-permute-start(bf16[776,256]{1,0:T(8,128)(2,1)S(1)} %get-tuple-element.80), channel_id=1, source_target_pairs={{0,16},{4,20},{8,24},{12,28},{16,0},{20,4},{24,8},{28,12},{32,48},... | collective-permute-start | bytes 1191944 | tf_op jit(solution)/shard_map/ppermute | solution.py:435
  74.5 52.4 %collective-permute-start.10 = (bf16[776,256]{1,0:T(8,128)(2,1)S(1)}, bf16[776,256]{1,0:T(8,128)(2,1)S(1)}, u32[]{:S(2)}, u32[]{:S(2)}) collective-permute-start(bf16[776,256]{1,0:T(8,128)(2,1)S(1)} %get-tuple-element.81), channel_id=1, source_target_pairs={{0,20},{4,16},{8,28},{12,24},{16,4},{20,0},{24,12},{28,8},{32,52},... | collective-permute-start | bytes 1191944 | tf_op jit(solution)/shard_map/ppermute | solution.py:435
  77.0 59.5 %collective-permute-start.11 = (bf16[776,256]{1,0:T(8,128)(2,1)S(1)}, bf16[776,256]{1,0:T(8,128)(2,1)S(1)}, u32[]{:S(2)}, u32[]{:S(2)}) collective-permute-start(bf16[776,256]{1,0:T(8,128)(2,1)S(1)} %get-tuple-element.82), channel_id=1, source_target_pairs={{0,12},{4,8},{8,20},{12,16},{16,28},{20,24},{24,4},{28,0},{32,44},... | collective-permute-start | bytes 1191944 | tf_op jit(solution)/shard_map/ppermute | solution.py:435
  89.9 47.9 %collective-permute-start.12 = (bf16[776,256]{1,0:T(8,128)(2,1)S(1)}, bf16[776,256]{1,0:T(8,128)(2,1)S(1)}, u32[]{:S(2)}, u32[]{:S(2)}) collective-permute-start(bf16[776,256]{1,0:T(8,128)(2,1)S(1)} %get-tuple-element.83), channel_id=1, source_target_pairs={{0,28},{4,24},{8,4},{12,0},{16,12},{20,8},{24,20},{28,16},{32,60},... | collective-permute-start | bytes 1191944 | tf_op jit(solution)/shard_map/ppermute | solution.py:435
  92.4 45.4 %collective-permute-start.13 = (bf16[776,256]{1,0:T(8,128)(2,1)S(1)}, bf16[776,256]{1,0:T(8,128)(2,1)S(1)}, u32[]{:S(2)}, u32[]{:S(2)}) collective-permute-start(bf16[776,256]{1,0:T(8,128)(2,1)S(1)} %get-tuple-element.84), channel_id=1, source_target_pairs={{0,4},{4,0},{8,12},{12,8},{16,20},{20,16},{24,28},{28,24},{32,36},... | collective-permute-start | bytes 1191944 | tf_op jit(solution)/shard_map/ppermute | solution.py:435
  140.9 2.6 %collective-permute-start.14 = (f32[16,128]{1,0:T(8,128)S(1)}, f32[16,128]{1,0:T(8,128)S(1)}, u32[]{:S(2)}, u32[]{:S(2)}) collective-permute-start(f32[16,128]{1,0:T(8,128)S(1)} %get-tuple-element.87), channel_id=1, source_target_pairs={{0,4},{4,0},{8,12},{12,8},{16,20},{20,16},{24,28},{28,24},{32,36},... | collective-permute-start | bytes 24584 | tf_op jit(solution)/shard_map/ppermute | solution.py:465
  143.6 11.9 %collective-permute-start.17 = (f32[32,128]{1,0:T(8,128)S(1)}, f32[32,128]{1,0:T(8,128)S(1)}, u32[]{:S(2)}, u32[]{:S(2)}) collective-permute-start(f32[32,128]{1,0:T(8,128)S(1)} %maximum_select_fusion), channel_id=1, source_target_pairs={{0,24},{4,28},{8,0},{12,4},{16,8},{20,12},{24,16},{28,20},{32,56},... | collective-permute-start | bytes 49160 | tf_op jit(solution)/shard_map/ppermute | solution.py:435
  146.0 9.5 %collective-permute-start.16 = (f32[32,128]{1,0:T(8,128)S(1)}, f32[32,128]{1,0:T(8,128)S(1)}, u32[]{:S(2)}, u32[]{:S(2)}) collective-permute-start(f32[32,128]{1,0:T(8,128)S(1)} %maximum_select_fusion), channel_id=1, source_target_pairs={{0,16},{4,20},{8,24},{12,28},{16,0},{20,4},{24,8},{28,12},{32,48},... | collective-permute-start | bytes 49160 | tf_op jit(solution)/shard_map/ppermute | solution.py:435
  146.5 9.0 %collective-permute-start.15 = (f32[32,128]{1,0:T(8,128)S(1)}, f32[32,128]{1,0:T(8,128)S(1)}, u32[]{:S(2)}, u32[]{:S(2)}) collective-permute-start(f32[32,128]{1,0:T(8,128)S(1)} %maximum_select_fusion), channel_id=1, source_target_pairs={{0,8},{4,12},{8,16},{12,20},{16,24},{20,28},{24,0},{28,4},{32,40},... | collective-permute-start | bytes 49160 | tf_op jit(solution)/shard_map/ppermute | solution.py:435

commit v9 on v8

--- a/solution.py
+++ b/solution.py
@@ -289,10 +289,41 @@
             pltpu.VMEM((SIDE, 2 * LEVELS, WIDTH), jnp.bfloat16),
             pltpu.VMEM((4 * PEERS, WIDTH), jnp.bfloat16),
         ],
-        compiler_params=pltpu.CompilerParams(vmem_limit_bytes=12 << 20),
+        compiler_params=pltpu.CompilerParams(vmem_limit_bytes=54 << 20),
         cost_estimate=pl.CostEstimate(flops=2 << 30, bytes_accessed=14 << 20, transcendentals=0),
         name="settle",
     )(side, direct, *lasts)
+
+
+def patch_kernel(high, old, out):
+    turn = chosen_rows(WIDTH, WIDTH, lambda i: lax.rem(i, 16) * 16 + lax.div(i, 16))
+    slot = lax.broadcasted_iota(jnp.int32, (16, 16, WIDTH), 1)
+    for group in range(2):
+        for low in range(0, LEVELS, 16):
+            parts = []
+            for j in range(4 * group, 4 * group + 4):
+                parts.append(jnp.zeros((32, WIDTH), jnp.bfloat16))
+                for r in range(2):
+                    start = r * LEVELS + low
+                    parts.append(high[j, start : start + 16, :])
+            turned = jnp.dot(turn, jnp.concatenate(parts, 0), preferred_element_type=jnp.float32)
+            kept = old[low : low + 16, 16 * group : 16 * group + 16, :].astype(jnp.float32)
+            both = jnp.where(lax.rem(slot, 4) >= 2, turned.reshape(16, 16, WIDTH), kept)
+            out[low : low + 16, 16 * group : 16 * group + 16, :] = both.astype(jnp.bfloat16)
+    out[LEVELS] = old[LEVELS]
+
+
+def patch(high, new_cache):
+    block = pl.BlockSpec((LEVELS + 1, 4 * SIDE, WIDTH), lambda t: (0, t, 0))
+    return pl.pallas_call(
+        patch_kernel,
+        grid=(PLANES,),
+        out_shape=jax.ShapeDtypeStruct(new_cache.shape, new_cache.dtype),
+        in_specs=[pl.BlockSpec((SIDE, DIRECT, WIDTH), lambda t: (t, 0, 0)), block],
+        out_specs=block,
+        compiler_params=pltpu.CompilerParams(vmem_limit_bytes=16 << 20),
+        name="patch",
+    )(high, new_cache)
 
 
 def pack_direct(low, dest, cache):
@@ -466,7 +497,7 @@
     piece = jnp.where(
         core == 0, jnp.concatenate([piece, other], 0), jnp.concatenate([other, piece], 0)
     )
-    direct, lasts, piece = lax.optimization_barrier((direct, lasts, piece))
+    direct, piece = lax.optimization_barrier((direct, piece))
     shares = jnp.stack([piece] + [in_plane(piece, shifts.index((dy, 0))) for dy in (1, 2, 3)])
     rows_y = jnp.arange(4, dtype=jnp.int32)
     ours = (lax.rem(y - rows_y + 4, 4)[:, None] == rows_y[None, :])[..., None, None]
@@ -478,11 +509,7 @@
 
     def by_pairs(new_cache):
         high = exchanged(pack_direct(2, target, cache))
-        high = high[:, : 2 * LEVELS].reshape(PLANES, SIDE, 2 * LEVELS, WIDTH)
-        high = jnp.swapaxes(high, 0, 1).reshape(SIDE, 2 * PLANES * LEVELS, WIDTH)
-        high = jnp.pad(high, ((0, 0), (0, LAST - 2 * PLANES * LEVELS), (0, 0)))
-        lasts = [lax.dynamic_index_in_dim(high, came[k], 0, keepdims=False) for k in range(SIDE)]
-        return settle(came, direct, lasts)[0]
+        return patch(high, new_cache)
 
     new_cache = lax.cond(over[0] > 0, by_pairs, by_relay, new_cache)
     return (jnp.swapaxes(new_cache, 0, 1), log_probs.T, grad_out, head.T)

time: 157 us -> 164 us (1.045)
  waiting for transfers between devices: 67.2 us -> 38.1 us
  starting transfers between devices: 41.9 us -> 70.5 us
  local copies, waits for them, and re-layouts: 10.1 us -> 18.5 us
    ppermute x10, starting transfers between devices: 13 us -> 43.6 us  [in_plane(): return lax.ppermute(x, 'sample', pairs)]
    ppermute x10, waiting for transfers between devices: 58.3 us -> 27.7 us  [in_plane(): return lax.ppermute(x, 'sample', pairs)]
    unnamed x23 -> x45, local copies, waits for them, and re-layouts: 5.1 us -> 13 us
    ppermute x1, starting transfers between devices: 1.82 us -> 0.01 us  [on_device(): other = lax.ppermute(piece, 'sample', xor_pairs(PEERS, 1))]
  transfers between devices with their start and end apart: 20 -> 20, of which waited for: 10 -> 8; matrix products, arithmetic and copies ran while one was open for 10% -> 9% of each run, Pallas kernels for 15% -> 14%
where the time goes in v9:
time: 164 us; the launch traced here: 163 us
  starting transfers between devices  70.5 us (43%)
  waiting for transfers between devices  38.1 us (23%)
  Pallas kernels  28.9 us (18%)
  local copies, waits for them, and re-layouts  18.5 us (11%)
  other arithmetic  3.37 us (2%)
  between operations  1.94 us (1%)
  matrix products  1.83 us (1%)
    ppermute x10, starting transfers between devices, in_plane(): return lax.ppermute(x, 'sample', pairs)  43.6 us
    ppermute x10, waiting for transfers between devices, in_plane(): return lax.ppermute(x, 'sample', pairs)  27.7 us
    all_to_all x2, starting transfers between devices, exchanged(): lax.all_to_all(x, 'sample', split_axis=0, concat_axis=0, tiled=True, axis...  16.8 us
    unnamed x45, local copies, waits for them, and re-layouts  13 us
    ppermute x7, starting transfers between devices, tree_sum(): terms = [x] + [lax.ppermute(x, axis, xor_pairs(size, bit)) for bit in bits]  10.1 us
    pallas_call x1, Pallas kernels, on_device(): pl.pallas_call(forward_kernel, out_shape=[jax.ShapeDtypeStruct((LAST, WID...  8.84 us
    pallas_call x1, Pallas kernels, settle(): pl.pallas_call(settle_kernel, grid=(PLANES,), out_shape=(jax.ShapeDtypeSt...  8.69 us
    all_to_all x2, waiting for transfers between devices, exchanged(): lax.all_to_all(x, 'sample', split_axis=0, concat_axis=0, tiled=True, axis...  6.1 us
  transfers between devices with their start and end apart: 20, of which 8 were waited for; matrix products, arithmetic and copies ran while one was open for 9% of the time, Pallas kernels for 14%

profile of v9, /device:TPU:1, one launch (start us, length us, event | category | flops | bytes accessed | tf_op | source)
XLA Modules:
  0.0 163.1 jit_solution(4704290644111589305)
XLA Ops:
  0.6 4.6 %pack_relay.1 = bf16[8,392,256]{2,1,0:T(8,128)(2,1)} custom-call(s32[128]{0:T(128)} %bitcast.88, bf16[128,48,256]{2,1,0:T(8,128)(2,1)} %cache.3), custom_call_target="tpu_custom_call" | custom-call | tf_op jit(solution)/shard_map/pack_relay/pallas_call | solution.py:377
  5.2 8.9 %all-to-all-start.2 = ((bf16[8,392,256]{2,1,0:T(8,128)(2,1)}), bf16[8,392,256]{2,1,0:T(8,128)(2,1)S(1)}, u32[]{:S(2)}, u32[]{:S(2)}) async-start(bf16[8,392,256]{2,1,0:T(8,128)(2,1)} %pack_relay.1), calls=%async_computation.2 | async-start | bytes 3211264 | tf_op jit(solution)/shard_map/all_to_all | solution.py:347
  14.2 4.1 %fusion.31 = (bf16[128,48,128]{2,1,0:T(8,128)(2,1)}, bf16[128,48,128]{2,1,0:T(8,128)(2,1)}) fusion(bf16[128,48,256]{2,1,0:T(8,128)(2,1)} %cache.3), kind=kLoop, calls=%fused_computation.83 | loop fusion | bytes 6291456 | tf_op jit(solution)/shard_map/slice | solution.py:43
  18.3 0.1 fusion.4
  18.5 0.2 convolution_convert_fusion.1
  18.7 0.2 convolution_convert_fusion.2
  19.0 0.2 bitcast_convert_fusion
  19.2 2.1 %copy.57 = bf16[128,48,128]{0,2,1:T(8,128)(2,1)S(1)} copy(bf16[128,48,128]{2,1,0:T(8,128)(2,1)} %get-tuple-element.57) | data formatting | bytes 3145728
  21.4 0.6 multiply_reduce_fusion.1
  22.2 2.1 %copy.58 = bf16[128,48,128]{0,2,1:T(8,128)(2,1)S(1)} copy(bf16[128,48,128]{2,1,0:T(8,128)(2,1)} %get-tuple-element.58) | data formatting | bytes 3145728
  24.4 0.4 multiply_reduce_fusion
  24.8 0.2 fusion.1
  25.0 0.1 fusion.32
  25.2 0.3 fusion.18
  25.5 0.1 fusion.17
  25.6 0.2 fusion.33
  25.8 2.7 %collective-permute-start.2 = (f32[132,128]{1,0:T(8,128)S(1)}, f32[132,128]{1,0:T(8,128)S(1)}, u32[]{:S(2)}, u32[]{:S(2)}) collective-permute-start(f32[132,128]{1,0:T(8,128)S(1)} %pad_maximum_fusion.1), channel_id=1, source_target_pairs={{0,3},{1,2},{2,1},{3,0},{4,7},{5,6},{6,5},{7,4},{8,11},{9,10},{10,... | collective-permute-start | bytes 202760 | tf_op jit(solution)/shard_map/ppermute | solution.py:357
  28.5 0.5 collective-permute-start.1
  29.0 0.2 collective-permute-start
  29.2 4.4 %pack_direct.3.rows = bf16[64,104,256]{2,1,0:T(8,128)(2,1)} custom-call(s32[128]{0:T(128)S(1)} %bitcast.89, bf16[128,48,256]{2,1,0:T(8,128)(2,1)} %cache.3), custom_call_target="tpu_custom_call" | custom-call | bytes 10485760 | tf_op jit(solution)/shard_map/pack_direct/pallas_call | solution.py:330
  33.8 2.9 %collective-permute-start.5 = (f32[132,128]{1,0:T(8,128)S(1)}, f32[132,128]{1,0:T(8,128)S(1)}, u32[]{:S(2)}, u32[]{:S(2)}) collective-permute-start(f32[132,128]{1,0:T(8,128)S(1)} %add_add_fusion.1), channel_id=1, source_target_pairs={{0,24},{4,28},{8,16},{12,20},{16,8},{20,12},{24,0},{28,4},{32,56},... | collective-permute-start | bytes 202760 | tf_op jit(solution)/shard_map/ppermute | solution.py:357
  36.7 0.4 collective-permute-start.4
  37.0 0.3 collective-permute-start.3
  37.4 1.2 collective-permute-done.5
  38.7 2.8 %collective-permute-done.4 = f32[132,128]{1,0:T(8,128)S(1)} collective-permute-done((f32[132,128]{1,0:T(8,128)S(1)}, f32[132,128]{1,0:T(8,128)S(1)}, u32[]{:S(2)}, u32[]{:S(2)}) %collective-permute-start.4) | collective-permute-done | bytes 67616 | tf_op jit(solution)/shard_map/ppermute | solution.py:357
  41.5 3.2 %collective-permute-start.6 = (f32[132,128]{1,0:T(8,128)S(1)}, f32[132,128]{1,0:T(8,128)S(1)}, u32[]{:S(2)}, u32[]{:S(2)}) collective-permute-start(f32[132,128]{1,0:T(8,128)S(1)} %add_add_fusion), channel_id=1, source_target_pairs={{0,4},{4,0},{8,12},{12,8},{16,20},{20,16},{24,28},{28,24},{32,36},... | collective-permute-start | bytes 202760 | tf_op jit(solution)/shard_map/ppermute | solution.py:357
  44.7 0.2 convolution_convert_fusion
  45.1 0.1 copy.38
  45.2 0.1 reshape.199
  45.4 0.2 collective-permute-done.6
  46.0 0.2 pad_maximum_fusion.tiles
  46.2 0.7 pack_tiles.1
  46.9 6.1 %all-to-all-done.2.got = bf16[8,392,256]{2,1,0:T(8,128)(2,1)S(1)} async-done(((bf16[8,392,256]{2,1,0:T(8,128)(2,1)}), bf16[8,392,256]{2,1,0:T(8,128)(2,1)S(1)}, u32[]{:S(2)}, u32[]{:S(2)}) %all-to-all-start.2) | async-done | bytes 1605664 | tf_op jit(solution)/shard_map/all_to_all | solution.py:347
  53.0 1.2 copy-done.2
  54.2 7.9 %all-to-all-start.1 = ((bf16[64,104,256]{2,1,0:T(8,128)(2,1)}), bf16[64,104,256]{2,1,0:T(8,128)(2,1)S(1)}, u32[]{:S(2)}, u32[]{:S(2)}) async-start(bf16[64,104,256]{2,1,0:T(8,128)(2,1)} %pack_tiles.1), calls=%async_computation.1 | async-start | bytes 6815744 | tf_op jit(solution)/shard_map/all_to_all | solution.py:347
  62.2 0.7 slice_convert_fusion
  63.0 1.4 copy-done.3
  64.4 8.8 %pack_plane.1 = (bf16[776,256]{1,0:T(8,128)(2,1)S(1)}, bf16[776,256]{1,0:T(8,128)(2,1)S(1)}, bf16[776,256]{1,0:T(8,128)(2,1)S(1)}, bf16[776,256]{1,0:T(8,128)(2,...) custom-call(s32[8,16]{1,0:T(8,128)S(1)} %bitcast.73, ...), custom_call_target="tpu_custom_call" | custom-call | bytes 5242880 | tf_op jit(solution)/shard_map/pack_plane/pallas_call | solution.py:440
  73.2 1.5 collective-permute-start.7
  74.7 1.3 collective-permute-start.8
  76.0 1.7 %collective-permute-start.9 = (bf16[776,256]{1,0:T(8,128)(2,1)S(1)}, bf16[776,256]{1,0:T(8,128)(2,1)S(1)}, u32[]{:S(2)}, u32[]{:S(2)}) collective-permute-start(bf16[776,256]{1,0:T(8,128)(2,1)S(1)} %get-tuple-element.44), channel_id=1, source_target_pairs={{0,16},{4,20},{8,24},{12,28},{16,0},{20,4},{24,8},{28,12},{32,48},... | collective-permute-start | bytes 1191944 | tf_op jit(solution)/shard_map/ppermute | solution.py:466
  77.6 2.5 %collective-permute-start.10 = (bf16[776,256]{1,0:T(8,128)(2,1)S(1)}, bf16[776,256]{1,0:T(8,128)(2,1)S(1)}, u32[]{:S(2)}, u32[]{:S(2)}) collective-permute-start(bf16[776,256]{1,0:T(8,128)(2,1)S(1)} %get-tuple-element.45), channel_id=1, source_target_pairs={{0,20},{4,16},{8,28},{12,24},{16,4},{20,0},{24,12},{28,8},{32,52},... | collective-permute-start | bytes 1191944 | tf_op jit(solution)/shard_map/ppermute | solution.py:466
  80.1 11.9 %collective-permute-done.7.refs_1_ = bf16[776,256]{1,0:T(8,128)(2,1)S(1)} collective-permute-done((bf16[776,256]{1,0:T(8,128)(2,1)S(1)}, bf16[776,256]{1,0:T(8,128)(2,1)S(1)}, u32[]{:S(2)}, u32[]{:S(2)}) %collective-permute-start.7) | collective-permute-done | bytes 397344 | tf_op jit(solution)/shard_map/ppermute | solution.py:466
  92.0 4.6 %collective-permute-start.12 = (bf16[776,256]{1,0:T(8,128)(2,1)S(1)}, bf16[776,256]{1,0:T(8,128)(2,1)S(1)}, u32[]{:S(2)}, u32[]{:S(2)}) collective-permute-start(bf16[776,256]{1,0:T(8,128)(2,1)S(1)} %get-tuple-element.47), channel_id=1, source_target_pairs={{0,28},{4,24},{8,4},{12,0},{16,12},{20,8},{24,20},{28,16},{32,60},... | collective-permute-start | bytes 1191944 | tf_op jit(solution)/shard_map/ppermute | solution.py:466
  96.6 27.3 %collective-permute-start.13 = (bf16[776,256]{1,0:T(8,128)(2,1)S(1)}, bf16[776,256]{1,0:T(8,128)(2,1)S(1)}, u32[]{:S(2)}, u32[]{:S(2)}) collective-permute-start(bf16[776,256]{1,0:T(8,128)(2,1)S(1)} %get-tuple-element.48), channel_id=1, source_target_pairs={{0,4},{4,0},{8,12},{12,8},{16,20},{20,16},{24,28},{28,24},{32,36},... | collective-permute-start | bytes 1191944 | tf_op jit(solution)/shard_map/ppermute | solution.py:466
  124.0 6.7 %collective-permute-done.10.refs_4_ = bf16[776,256]{1,0:T(8,128)(2,1)S(1)} collective-permute-done((bf16[776,256]{1,0:T(8,128)(2,1)S(1)}, bf16[776,256]{1,0:T(8,128)(2,1)S(1)}, u32[]{:S(2)}, u32[]{:S(2)}) %collective-permute-start.10) | collective-permute-done | bytes 397344 | tf_op jit(solution)/shard_map/ppermute | solution.py:466
  130.7 8.6 %collective-permute-done.11.refs_5_ = bf16[776,256]{1,0:T(8,128)(2,1)S(1)} collective-permute-done((bf16[776,256]{1,0:T(8,128)(2,1)S(1)}, bf16[776,256]{1,0:T(8,128)(2,1)S(1)}, u32[]{:S(2)}, u32[]{:S(2)}) %collective-permute-start.11) | collective-permute-done | bytes 397344 | tf_op jit(solution)/shard_map/ppermute | solution.py:466
  139.3 0.5 collective-permute-done.12.refs_6_
  139.8 0.6 flag.1
  140.5 0.7 copy-done.4
  141.2 0.7 copy-done.5
  142.0 0.8 copy-done.6
  142.7 0.7 copy-done.7
  143.5 0.8 copy-done.8
  144.2 0.8 copy-done.9
  145.0 0.8 copy-done.10
  145.7 0.8 copy-done.11
  146.5 1.0 plane_sum.1
  147.6 0.6 stack.75.side
  148.9 3.4 %collective-permute-start.17 = (f32[32,128]{1,0:T(8,128)S(1)}, f32[32,128]{1,0:T(8,128)S(1)}, u32[]{:S(2)}, u32[]{:S(2)}) collective-permute-start(f32[32,128]{1,0:T(8,128)S(1)} %maximum_select_fusion), channel_id=1, source_target_pairs={{0,24},{4,28},{8,0},{12,4},{16,8},{20,12},{24,16},{28,20},{32,56},... | collective-permute-start | bytes 49160 | tf_op jit(solution)/shard_map/ppermute | solution.py:466
  152.3 0.6 collective-permute-start.16
  152.9 0.8 collective-permute-start.15
  153.7 8.7 %settle.1 = (bf16[49,256,256]{2,1,0:T(8,128)(2,1)}, f32[4,256]{1,0:T(4,128)}) custom-call(s32[8]{0:T(128)} %stack.75.side, bf16[64,104,256]{2,1,0:T(8,128)(2,1)} %copy-done.1, bf16[776,256]{1,0:T(8,128)(2,1)} %copy-done.4, bf16[776,256]{1,0:T(8,128)(2,1)} %copy-done.5, bf16[776,256]{1,0:T(8,128)(2,1)} %copy-done.6, bf16[776,256]{1,0:T(8,128)(2,1)} %copy-done.7, ...), custom_call_target="tpu_custom_call" | custom-call | flops 2147483648 | bytes 14680064 | tf_op jit(solution)/shard_map/settle/pallas_call | solution.py:275
  162.4 0.7 select_reduce_fusion
  (90 shorter events, 1.4 us)
Async XLA Ops:
  0.6 18.3 %copy-start = (bf16[128,128]{1,0:T(8,128)(2,1)S(1)}, bf16[128,128]{1,0:T(8,128)(2,1)}, u32[]{:S(2)}) copy-start(bf16[128,128]{1,0:T(8,128)(2,1)} %param.16) | copy-start | bytes 98308
  5.2 47.8 %all-to-all-start.2 = ((bf16[8,392,256]{2,1,0:T(8,128)(2,1)}), bf16[8,392,256]{2,1,0:T(8,128)(2,1)S(1)}, u32[]{:S(2)}, u32[]{:S(2)}) async-start(bf16[8,392,256]{2,1,0:T(8,128)(2,1)} %pack_relay.1), calls=%async_computation.2 | async-start | bytes 3211264 | tf_op jit(solution)/shard_map/all_to_all | solution.py:347
  14.2 4.1 %copy-start.13 = (bf16[128,128]{1,0:T(8,128)(2,1)S(1)}, bf16[128,128]{1,0:T(8,128)(2,1)}, u32[]{:S(2)}) copy-start(bf16[128,128]{1,0:T(8,128)(2,1)} %param.13) | copy-start | bytes 98308
  14.2 4.3 %copy-start.14 = (bf16[128,128]{1,0:T(8,128)(2,1)S(1)}, bf16[128,128]{1,0:T(8,128)(2,1)}, u32[]{:S(2)}) copy-start(bf16[128,128]{1,0:T(8,128)(2,1)} %param.18) | copy-start | bytes 98308
  14.2 4.3 %copy-start.17 = (f32[128]{0:T(128)S(1)}, f32[128]{0:T(128)}, u32[]{:S(2)}) copy-start(f32[128]{0:T(128)} %param.15) | copy-start | bytes 1540
  14.2 4.5 %copy-start.15 = (bf16[128,128]{1,0:T(8,128)(2,1)S(1)}, bf16[128,128]{1,0:T(8,128)(2,1)}, u32[]{:S(2)}) copy-start(bf16[128,128]{1,0:T(8,128)(2,1)} %param.17) | copy-start | bytes 98308
  22.0 2.8 %copy-start.16 = (bf16[128,128]{1,0:T(8,128)(2,1)S(1)}, bf16[128,128]{1,0:T(8,128)(2,1)}, u32[]{:S(2)}) copy-start(bf16[128,128]{1,0:T(8,128)(2,1)} %param.19) | copy-start | bytes 98308
  22.0 3.0 %copy-start.19 = (bf16[128,4]{0,1:T(4,128)(2,1)S(1)}, bf16[128,4]{0,1:T(4,128)(2,1)}, u32[]{:S(2)}) copy-start(bf16[128,4]{0,1:T(4,128)(2,1)} %param.20) | copy-start | bytes 3076
  22.0 3.2 %copy-start.20 = (s32[128]{0:T(128)S(1)}, s32[128]{0:T(128)}, u32[]{:S(2)}) copy-start(s32[128]{0:T(128)} %param.22) | copy-start | bytes 1540
  22.0 3.2 %copy-start.21 = (f32[128]{0:T(128)S(1)}, f32[128]{0:T(128)}, u32[]{:S(2)}) copy-start(f32[128]{0:T(128)} %param.21) | copy-start | bytes 1540
  22.0 7.2 %copy-start.18 = (s32[128,1]{0,1:T(1,128)S(1)}, s32[128,1]{0,1:T(1,128)}, u32[]{:S(2)}) copy-start(s32[128,1]{0,1:T(1,128)} %param.23) | copy-start | bytes 1540
  25.8 7.9 %collective-permute-start.2 = (f32[132,128]{1,0:T(8,128)S(1)}, f32[132,128]{1,0:T(8,128)S(1)}, u32[]{:S(2)}, u32[]{:S(2)}) collective-permute-start(f32[132,128]{1,0:T(8,128)S(1)} %pad_maximum_fusion.1), channel_id=1, source_target_pairs={{0,3},{1,2},{2,1},{3,0},{4,7},{5,6},{6,5},{7,4},{8,11},{9,10},{10,... | collective-permute-start | bytes 202760 | tf_op jit(solution)/shard_map/ppermute | solution.py:357
  28.5 5.3 %collective-permute-start.1 = (f32[132,128]{1,0:T(8,128)S(1)}, f32[132,128]{1,0:T(8,128)S(1)}, u32[]{:S(2)}, u32[]{:S(2)}) collective-permute-start(f32[132,128]{1,0:T(8,128)S(1)} %pad_maximum_fusion.1), channel_id=1, source_target_pairs={{0,2},{1,3},{2,0},{3,1},{4,6},{5,7},{6,4},{7,5},{8,10},{9,11},{10,... | collective-permute-start | bytes 202760 | tf_op jit(solution)/shard_map/ppermute | solution.py:357
  29.0 4.8 %collective-permute-start = (f32[132,128]{1,0:T(8,128)S(1)}, f32[132,128]{1,0:T(8,128)S(1)}, u32[]{:S(2)}, u32[]{:S(2)}) collective-permute-start(f32[132,128]{1,0:T(8,128)S(1)} %pad_maximum_fusion.1), channel_id=1, source_target_pairs={{0,1},{1,0},{2,3},{3,2},{4,5},{5,4},{6,7},{7,6},{8,9},{9,8},{10,11... | collective-permute-start | bytes 202760 | tf_op jit(solution)/shard_map/ppermute | solution.py:357
  33.8 4.9 %collective-permute-start.5 = (f32[132,128]{1,0:T(8,128)S(1)}, f32[132,128]{1,0:T(8,128)S(1)}, u32[]{:S(2)}, u32[]{:S(2)}) collective-permute-start(f32[132,128]{1,0:T(8,128)S(1)} %add_add_fusion.1), channel_id=1, source_target_pairs={{0,24},{4,28},{8,16},{12,20},{16,8},{20,12},{24,0},{28,4},{32,56},... | collective-permute-start | bytes 202760 | tf_op jit(solution)/shard_map/ppermute | solution.py:357
  36.7 4.8 %collective-permute-start.4 = (f32[132,128]{1,0:T(8,128)S(1)}, f32[132,128]{1,0:T(8,128)S(1)}, u32[]{:S(2)}, u32[]{:S(2)}) collective-permute-start(f32[132,128]{1,0:T(8,128)S(1)} %add_add_fusion.1), channel_id=1, source_target_pairs={{0,16},{4,20},{8,24},{12,28},{16,0},{20,4},{24,8},{28,12},{32,48},... | collective-permute-start | bytes 202760 | tf_op jit(solution)/shard_map/ppermute | solution.py:357
  37.0 4.4 %collective-permute-start.3 = (f32[132,128]{1,0:T(8,128)S(1)}, f32[132,128]{1,0:T(8,128)S(1)}, u32[]{:S(2)}, u32[]{:S(2)}) collective-permute-start(f32[132,128]{1,0:T(8,128)S(1)} %add_add_fusion.1), channel_id=1, source_target_pairs={{0,8},{4,12},{8,0},{12,4},{16,24},{20,28},{24,16},{28,20},{32,40},... | collective-permute-start | bytes 202760 | tf_op jit(solution)/shard_map/ppermute | solution.py:357
  41.5 4.1 %collective-permute-start.6 = (f32[132,128]{1,0:T(8,128)S(1)}, f32[132,128]{1,0:T(8,128)S(1)}, u32[]{:S(2)}, u32[]{:S(2)}) collective-permute-start(f32[132,128]{1,0:T(8,128)S(1)} %add_add_fusion), channel_id=1, source_target_pairs={{0,4},{4,0},{8,12},{12,8},{16,20},{20,16},{24,28},{28,24},{32,36},... | collective-permute-start | bytes 202760 | tf_op jit(solution)/shard_map/ppermute | solution.py:357
  53.0 1.2 copy-start.2
  54.2 92.3 %all-to-all-start.1 = ((bf16[64,104,256]{2,1,0:T(8,128)(2,1)}), bf16[64,104,256]{2,1,0:T(8,128)(2,1)S(1)}, u32[]{:S(2)}, u32[]{:S(2)}) async-start(bf16[64,104,256]{2,1,0:T(8,128)(2,1)} %pack_tiles.1), calls=%async_computation.1 | async-start | bytes 6815744 | tf_op jit(solution)/shard_map/all_to_all | solution.py:347
  63.0 1.4 copy-start.3
  73.2 18.8 %collective-permute-start.7 = (bf16[776,256]{1,0:T(8,128)(2,1)S(1)}, bf16[776,256]{1,0:T(8,128)(2,1)S(1)}, u32[]{:S(2)}, u32[]{:S(2)}) collective-permute-start(bf16[776,256]{1,0:T(8,128)(2,1)S(1)} %get-tuple-element.42), channel_id=1, source_target_pairs={{0,8},{4,12},{8,16},{12,20},{16,24},{20,28},{24,0},{28,4},{32,40},... | collective-permute-start | bytes 1191944 | tf_op jit(solution)/shard_map/ppermute | solution.py:466
  74.7 22.0 %collective-permute-start.8 = (bf16[776,256]{1,0:T(8,128)(2,1)S(1)}, bf16[776,256]{1,0:T(8,128)(2,1)S(1)}, u32[]{:S(2)}, u32[]{:S(2)}) collective-permute-start(bf16[776,256]{1,0:T(8,128)(2,1)S(1)} %get-tuple-element.43), channel_id=1, source_target_pairs={{0,24},{4,28},{8,0},{12,4},{16,8},{20,12},{24,16},{28,20},{32,56},... | collective-permute-start | bytes 1191944 | tf_op jit(solution)/shard_map/ppermute | solution.py:466
  76.0 48.0 %collective-permute-start.9 = (bf16[776,256]{1,0:T(8,128)(2,1)S(1)}, bf16[776,256]{1,0:T(8,128)(2,1)S(1)}, u32[]{:S(2)}, u32[]{:S(2)}) collective-permute-start(bf16[776,256]{1,0:T(8,128)(2,1)S(1)} %get-tuple-element.44), channel_id=1, source_target_pairs={{0,16},{4,20},{8,24},{12,28},{16,0},{20,4},{24,8},{28,12},{32,48},... | collective-permute-start | bytes 1191944 | tf_op jit(solution)/shard_map/ppermute | solution.py:466
  77.6 53.1 %collective-permute-start.10 = (bf16[776,256]{1,0:T(8,128)(2,1)S(1)}, bf16[776,256]{1,0:T(8,128)(2,1)S(1)}, u32[]{:S(2)}, u32[]{:S(2)}) collective-permute-start(bf16[776,256]{1,0:T(8,128)(2,1)S(1)} %get-tuple-element.45), channel_id=1, source_target_pairs={{0,20},{4,16},{8,28},{12,24},{16,4},{20,0},{24,12},{28,8},{32,52},... | collective-permute-start | bytes 1191944 | tf_op jit(solution)/shard_map/ppermute | solution.py:466
  80.1 59.2 %collective-permute-start.11 = (bf16[776,256]{1,0:T(8,128)(2,1)S(1)}, bf16[776,256]{1,0:T(8,128)(2,1)S(1)}, u32[]{:S(2)}, u32[]{:S(2)}) collective-permute-start(bf16[776,256]{1,0:T(8,128)(2,1)S(1)} %get-tuple-element.46), channel_id=1, source_target_pairs={{0,12},{4,8},{8,20},{12,16},{16,28},{20,24},{24,4},{28,0},{32,44},... | collective-permute-start | bytes 1191944 | tf_op jit(solution)/shard_map/ppermute | solution.py:466
  92.0 47.8 %collective-permute-start.12 = (bf16[776,256]{1,0:T(8,128)(2,1)S(1)}, bf16[776,256]{1,0:T(8,128)(2,1)S(1)}, u32[]{:S(2)}, u32[]{:S(2)}) collective-permute-start(bf16[776,256]{1,0:T(8,128)(2,1)S(1)} %get-tuple-element.47), channel_id=1, source_target_pairs={{0,28},{4,24},{8,4},{12,0},{16,12},{20,8},{24,20},{28,16},{32,60},... | collective-permute-start | bytes 1191944 | tf_op jit(solution)/shard_map/ppermute | solution.py:466
  96.6 43.2 %collective-permute-start.13 = (bf16[776,256]{1,0:T(8,128)(2,1)S(1)}, bf16[776,256]{1,0:T(8,128)(2,1)S(1)}, u32[]{:S(2)}, u32[]{:S(2)}) collective-permute-start(bf16[776,256]{1,0:T(8,128)(2,1)S(1)} %get-tuple-element.48), channel_id=1, source_target_pairs={{0,4},{4,0},{8,12},{12,8},{16,20},{20,16},{24,28},{28,24},{32,36},... | collective-permute-start | bytes 1191944 | tf_op jit(solution)/shard_map/ppermute | solution.py:466
  140.4 0.8 copy-start.4
  141.2 0.7 copy-start.5
  142.0 0.8 copy-start.6
  142.7 0.7 copy-start.7
  143.5 0.8 copy-start.8
  144.2 0.8 copy-start.9
  145.0 0.8 copy-start.10
  145.7 0.8 copy-start.11
  146.5 7.1 %copy-start.1 = (bf16[64,104,256]{2,1,0:T(8,128)(2,1)}, bf16[64,104,256]{2,1,0:T(8,128)(2,1)S(1)}, u32[]{:S(2)}) copy-start(bf16[64,104,256]{2,1,0:T(8,128)(2,1)S(1)} %all-to-all-done.1.tiles.direct) | copy-start | bytes 10223620
  147.5 1.3 collective-permute-start.14
  148.9 13.5 %collective-permute-start.17 = (f32[32,128]{1,0:T(8,128)S(1)}, f32[32,128]{1,0:T(8,128)S(1)}, u32[]{:S(2)}, u32[]{:S(2)}) collective-permute-start(f32[32,128]{1,0:T(8,128)S(1)} %maximum_select_fusion), channel_id=1, source_target_pairs={{0,24},{4,28},{8,0},{12,4},{16,8},{20,12},{24,16},{28,20},{32,56},... | collective-permute-start | bytes 49160 | tf_op jit(solution)/shard_map/ppermute | solution.py:466
  152.3 10.0 %collective-permute-start.16 = (f32[32,128]{1,0:T(8,128)S(1)}, f32[32,128]{1,0:T(8,128)S(1)}, u32[]{:S(2)}, u32[]{:S(2)}) collective-permute-start(f32[32,128]{1,0:T(8,128)S(1)} %maximum_select_fusion), channel_id=1, source_target_pairs={{0,16},{4,20},{8,24},{12,28},{16,0},{20,4},{24,8},{28,12},{32,48},... | collective-permute-start | bytes 49160 | tf_op jit(solution)/shard_map/ppermute | solution.py:466
  152.9 9.5 %collective-permute-start.15 = (f32[32,128]{1,0:T(8,128)S(1)}, f32[32,128]{1,0:T(8,128)S(1)}, u32[]{:S(2)}, u32[]{:S(2)}) collective-permute-start(f32[32,128]{1,0:T(8,128)S(1)} %maximum_select_fusion), channel_id=1, source_target_pairs={{0,8},{4,12},{8,16},{12,20},{16,24},{20,28},{24,0},{28,4},{32,40},... | collective-permute-start | bytes 49160 | tf_op jit(solution)/shard_map/ppermute | solution.py:466
